TPU v7x, 32 devices: a whole 2x2x4 slice. The times are simulated.
32 devices in a mesh: gx: 2 (over core), gy: 4 (over y, x), gz: 4 (over z).
Axes of the slice: x: 2, y: 2, z: 4, core: 2. Of those that a mesh axis runs over, the one named last changes fastest.
Arguments:
- offsets: float32 [3, 8, 16, 512], P(None, 'gx', 'gy', 'gz'), may hold values from 0 to 1, as said below
- charges: float32 [8, 16, 512], P('gx', 'gy', 'gz'), may hold values from -0.3 to 0.3
- up_inverse: float32 [64, 64], replicated, may hold values from -0.75 to 0.75
- translations: bfloat16 [316, 4096], replicated, may hold values from -0.0546875 to 0.0546875
- down_inverse: float32 [64, 64], replicated, may hold values from -0.75 to 0.75
Outputs:
- potential: float32 [8, 16, 512], P('gx', 'gy', 'gz')
Inputs may be any that keep to these rules, and one draw needn't show every extreme that they name: `offsets`: each leaf box is cut into a regular lattice of 32 equal cells; the box's 32 bodies lie in distinct cells, each at least 0.15 of a cell's side away from its cell's faces.
All inputs are finite; a program needn't handle non-finite values.
Results may differ from a plain program's by a relative error of at most 0.0028.
Values may be sent and summed in bfloat16 or wider, within the bound.
No kernel may reach another device: no remote copies, remote signals or barrier semaphores. Data moves between devices by JAX's collectives and lax.ppermute only.
A program may use at most 128 MiB of HBM per device.

v0:
```python
import math

import jax
import jax.numpy as jnp
import numpy as np
from jax import lax
from jax.sharding import PartitionSpec as P

BODIES = 32


RADIUS = 0.9


def with_halo(cells, sides, width):
    for axis, dim in sides:
        count = lax.axis_size(axis)
        ends = count - 1
        head = lax.slice_in_dim(cells, 0, width, axis=dim)
        tail = lax.slice_in_dim(cells, cells.shape[dim] - width, cells.shape[dim], axis=dim)
        cells = jnp.concatenate(
            [
                lax.ppermute(tail, axis, [(i, (i + 1) % count) for i in range(ends)]),
                cells,
                lax.ppermute(head, axis, [((i + 1) % count, i) for i in range(ends)]),
            ],
            axis=dim,
        )
    return cells


def sphere_points(num_points):
    number = jnp.arange(num_points).astype(jnp.float32)
    height = 1.0 - (2.0 * number + 1.0) / num_points
    across = jnp.sqrt(1.0 - height * height)
    turned = number * (math.pi * (3.0 - math.sqrt(5.0)))
    return (across * jnp.cos(turned), across * jnp.sin(turned), height)


def green(delta_x, delta_y, delta_z):
    square = delta_x * delta_x + delta_y * delta_y + delta_z * delta_z
    inside = square > 0.0
    return jnp.where(inside, lax.rsqrt(jnp.where(inside, square, 1.0)), 0.0)


def table_rows(zero_row):
    listing = []
    counter = 0
    for along_x in range(-3, 4):
        for along_y in range(-3, 4):
            for along_z in range(-3, 4):
                if max(abs(along_x), abs(along_y), abs(along_z)) >= 2:
                    listing.append(counter)
                    counter += 1
                else:
                    listing.append(zero_row)
    return np.array(listing, dtype=np.int32)


def full_table(translations, points):
    padded = jnp.concatenate(
        [translations, jnp.zeros((1, translations.shape[1]), translations.dtype)], axis=0
    )
    picked = jnp.take(padded, jnp.asarray(table_rows(translations.shape[0])), axis=0)
    return picked.reshape(7, 7, 7, points, points)


def unfold(source_array, along_axis, parents):
    middle = lax.slice_in_dim(source_array, 1, 1 + 2 * (parents + 2), axis=along_axis)
    old_shape = middle.shape
    paired = middle.reshape(old_shape[:along_axis] + (parents + 2, 2) + old_shape[along_axis + 1 :])
    windows = [
        lax.slice_in_dim(paired, offset, offset + parents, axis=along_axis) for offset in range(3)
    ]
    stacked = jnp.stack(windows, axis=along_axis + 1)
    return stacked.reshape(old_shape[:along_axis] + (parents, 6) + old_shape[along_axis + 1 :])


def translate(extended, operators, parents_x, parents_y, parents_z, points):
    unfolded = unfold(unfold(unfold(extended, 0, parents_x), 2, parents_y), 4, parents_z)
    flat_rows = unfolded.transpose(0, 2, 4, 1, 3, 5, 6).reshape(
        parents_x * parents_y * parents_z, 216 * points
    )
    results = []
    for class_x in range(2):
        for class_y in range(2):
            for class_z in range(2):
                slab_table = operators[
                    1 - class_x : 7 - class_x, 1 - class_y : 7 - class_y, 1 - class_z : 7 - class_z
                ]
                slab_table = slab_table.reshape(216 * points, points)
                results.append(jnp.dot(flat_rows, slab_table, preferred_element_type=jnp.float32))
    joined = jnp.stack(results).reshape(2, 2, 2, parents_x, parents_y, parents_z, points)
    return joined.transpose(3, 0, 4, 1, 5, 2, 6).reshape(
        2 * parents_x, 2 * parents_y, 2 * parents_z, points
    )


def place_bodies(offsets, start_x, start_y, start_z):
    leaves_x, leaves_y = (offsets.shape[1], offsets.shape[2])
    leaves_z = offsets.shape[3] // BODIES
    scaled = offsets.reshape(3, leaves_x, leaves_y, leaves_z, BODIES)
    box_shape = (leaves_x, leaves_y, leaves_z)
    corner_x = (lax.broadcasted_iota(jnp.int32, box_shape, 0) + start_x).astype(jnp.float32)
    corner_y = (lax.broadcasted_iota(jnp.int32, box_shape, 1) + start_y).astype(jnp.float32)
    corner_z = (lax.broadcasted_iota(jnp.int32, box_shape, 2) + start_z).astype(jnp.float32)
    body_x = corner_x[..., None] + scaled[0]
    body_y = corner_y[..., None] + scaled[1]
    body_z = corner_z[..., None] + scaled[2]
    return (body_x, body_y, body_z, corner_x + 0.5, corner_y + 0.5, corner_z + 0.5)


def upward_check(body_x, body_y, body_z, weights, centre_x, centre_y, centre_z, sphere):
    point_x = centre_x[..., None] + RADIUS * sphere[0]
    point_y = centre_y[..., None] + RADIUS * sphere[1]
    point_z = centre_z[..., None] + RADIUS * sphere[2]
    kernel = green(
        point_x[..., :, None] - body_x[..., None, :],
        point_y[..., :, None] - body_y[..., None, :],
        point_z[..., :, None] - body_z[..., None, :],
    )
    return jnp.sum(kernel * weights[..., None, :], axis=-1)


def evaluate_far(body_x, body_y, body_z, density, centre_x, centre_y, centre_z, sphere):
    point_x = centre_x[..., None] + RADIUS * sphere[0]
    point_y = centre_y[..., None] + RADIUS * sphere[1]
    point_z = centre_z[..., None] + RADIUS * sphere[2]
    kernel = green(
        body_x[..., :, None] - point_x[..., None, :],
        body_y[..., :, None] - point_y[..., None, :],
        body_z[..., :, None] - point_z[..., None, :],
    )
    return jnp.sum(kernel * density[..., None, :], axis=-1)


def pair_sum(target_x, target_y, target_z, source_x, source_y, source_z, source_q):
    kernel = green(
        target_x[..., :, None] - source_x[..., None, :],
        target_y[..., :, None] - source_y[..., None, :],
        target_z[..., :, None] - source_z[..., None, :],
    )
    return jnp.sum(kernel * source_q[..., None, :], axis=-1)


def per_device(offsets, charges, up_inverse, translations, down_inverse):
    points = up_inverse.shape[0]
    leaves_x, leaves_y = (offsets.shape[1], offsets.shape[2])
    leaves_z = offsets.shape[3] // BODIES
    body_x, body_y, body_z, centre_x, centre_y, centre_z = place_bodies(
        offsets,
        lax.axis_index("gx") * leaves_x,
        lax.axis_index("gy") * leaves_y,
        lax.axis_index("gz") * leaves_z,
    )
    weights = charges.reshape(leaves_x, leaves_y, leaves_z, BODIES)
    sphere = sphere_points(points)
    packet = jnp.concatenate([body_x, body_y, body_z, weights], axis=3)
    edge_data = with_halo(packet, (("gx", 0), ("gy", 1), ("gz", 2)), 1)
    up_check = upward_check(body_x, body_y, body_z, weights, centre_x, centre_y, centre_z, sphere)
    up_density = jnp.dot(
        up_check.reshape(leaves_x * leaves_y * leaves_z, points),
        up_inverse,
        precision=lax.Precision.HIGHEST,
        preferred_element_type=jnp.float32,
    ).astype(jnp.bfloat16)
    cubed = up_density.reshape(leaves_x, leaves_y, leaves_z, points)
    extended = with_halo(cubed, (("gx", 0), ("gy", 1), ("gz", 2)), 3)
    near_part = jnp.zeros((leaves_x, leaves_y, leaves_z, BODIES), jnp.float32)
    for shift_x in range(3):
        for shift_y in range(3):
            for shift_z in range(3):
                window = edge_data[
                    shift_x : shift_x + leaves_x,
                    shift_y : shift_y + leaves_y,
                    shift_z : shift_z + leaves_z,
                ]
                near_part = near_part + pair_sum(
                    body_x,
                    body_y,
                    body_z,
                    window[..., 0:BODIES],
                    window[..., BODIES : 2 * BODIES],
                    window[..., 2 * BODIES : 3 * BODIES],
                    window[..., 3 * BODIES : 4 * BODIES],
                )
    operators = full_table(translations, points)
    down_check = translate(extended, operators, leaves_x // 2, leaves_y // 2, leaves_z // 2, points)
    down_density = jnp.dot(
        down_check.reshape(leaves_x * leaves_y * leaves_z, points),
        down_inverse,
        precision=lax.Precision.HIGHEST,
        preferred_element_type=jnp.float32,
    )
    down_density = down_density.reshape(leaves_x, leaves_y, leaves_z, points)
    far_part = evaluate_far(
        body_x, body_y, body_z, down_density, centre_x, centre_y, centre_z, sphere
    )
    return (near_part + far_part).reshape(leaves_x, leaves_y, leaves_z * BODIES)


def solution(mesh):
    in_specs = (P(None, "gx", "gy", "gz"), P("gx", "gy", "gz"), P(), P(), P())
    out_specs = P("gx", "gy", "gz")
    return jax.shard_map(
        per_device, mesh=mesh, in_specs=in_specs, out_specs=out_specs, check_vma=False
    )
```

profile of v0, /device:TPU:12, one launch (start us, length us, event | category | flops | bytes accessed | tf_op | source)
XLA Modules:
  0.0 119.5 jit_solution(5666378314141607330)
XLA Ops:
  0.2 0.8 reshape.286
  1.0 0.7 fusion.111
  2.3 1.3 %fusion.94 = f32[4,4,4,64]{3,2,1,0:T(4,128)S(1)} fusion(f32[4,4,4,32]{3,2,1,0:T(4,128)S(1)} %reshape.286, f32[4,4,4,32]{3,2,1,0:T(4,128)S(1)} %get-tuple-element.173, f32[4,4,4,64]{3,2,1,0:T(4,128)S(1)} %get-tuple-element.175, f32[4,4,4,32]{3,2,1,0:T(4,128)S(1)} %get-tuple-element.174, f32[4,4,4,64]{3,2,1,0:T(4,128)S(1)} %get-tuple-element.176, ...), kind=kLoop, calls=%fused_computation.162 | loop fusion | flops 1699840 | bytes 98304 | tf_op jit(solution)/shard_map/reduce_sum | solution.py:122
  3.8 1.3 %collective-permute-start.7 = (bf16[3,4,4,64]{3,0,2,1:T(4,128)(2,1)S(1)}, bf16[3,4,4,64]{3,0,2,1:T(4,128)(2,1)S(1)}, u32[]{:S(2)}, u32[]{:S(2)}) collective-permute-start(bf16[3,4,4,64]{3,0,2,1:T(4,128)(2,1)S(1)} %copy.29), channel_id=1, source_target_pairs={{16,0},{17,1},{18,2},{19,3},{20,4},{21,5},{22,6},{23,7},{24,8},{25... | collective-permute-start | bytes 18440 | tf_op jit(solution)/shard_map/ppermute | solution.py:25
  5.1 3.0 %collective-permute-start.6 = (bf16[3,4,4,64]{3,0,2,1:T(4,128)(2,1)S(1)}, bf16[3,4,4,64]{3,0,2,1:T(4,128)(2,1)S(1)}, u32[]{:S(2)}, u32[]{:S(2)}) collective-permute-start(bf16[3,4,4,64]{3,0,2,1:T(4,128)(2,1)S(1)} %copy.28), channel_id=1, source_target_pairs={{0,16},{1,17},{2,18},{3,19},{4,20},{5,21},{6,22},{7,23},{8,24},{9,... | collective-permute-start | bytes 18440 | tf_op jit(solution)/shard_map/ppermute | solution.py:23
  8.2 1.3 %collective-permute-start.1 = (f32[1,4,4,128]{3,2,1,0:T(4,128)S(1)}, f32[1,4,4,128]{3,2,1,0:T(4,128)S(1)}, u32[]{:S(2)}, u32[]{:S(2)}) collective-permute-start(f32[1,4,4,128]{3,2,1,0:T(4,128)S(1)} %get-tuple-element.131), channel_id=1, source_target_pairs={{16,0},{17,1},{18,2},{19,3},{20,4},{21,5},{22,6},{23,7},{24,8},{25... | collective-permute-start | bytes 24584 | tf_op jit(solution)/shard_map/ppermute | solution.py:25
  9.5 3.0 %collective-permute-start = (f32[1,4,4,128]{3,2,1,0:T(4,128)S(1)}, f32[1,4,4,128]{3,2,1,0:T(4,128)S(1)}, u32[]{:S(2)}, u32[]{:S(2)}) collective-permute-start(f32[1,4,4,128]{3,2,1,0:T(4,128)S(1)} %get-tuple-element.130), channel_id=1, source_target_pairs={{0,16},{1,17},{2,18},{3,19},{4,20},{5,21},{6,22},{7,23},{8,24},{9,... | collective-permute-start | bytes 24584 | tf_op jit(solution)/shard_map/ppermute | solution.py:23
  12.6 0.7 pad_clamp_fusion
  13.3 1.9 %concatenate.72 = bf16[317,4096]{1,0:T(8,128)(2,1)S(1)} pad(bf16[316,4096]{1,0:T(8,128)(2,1)} %param.9, bf16[]{:T(256)} %constant.52.clone.1), padding=0_1x0_0 | pad | bytes 5185538 | tf_op jit(solution)/shard_map/concatenate | solution.py:61
  15.2 4.0 %gather_fusion = bf16[343,4096]{1,0:T(8,128)(2,1)} fusion(bf16[317,4096]{1,0:T(8,128)(2,1)S(1)} %concatenate.72, s32[1024]{0:T(1024)S(1)} %pad_clamp_fusion), kind=kCustom, calls=%fused_computation | custom fusion | bytes 5621084 | tf_op jit(solution)/shard_map/jit(_take)/gather | solution.py:64
  19.1 8.9 %gather.7 = bf16[7,7,7,64,64]{4,3,2,1,0:T(8,128)(2,1)} reshape(bf16[343,4096]{1,0:T(8,128)(2,1)} %gather_fusion) | data formatting | bytes 5619712 | tf_op jit(solution)/shard_map/jit(_take)/gather | solution.py:64
  28.1 21.4 %fusion.97 = (bf16[6,6,6,64,64]{4,3,2,1,0:T(8,128)(2,1)}, bf16[6,6,6,64,64]{4,3,2,1,0:T(8,128)(2,1)}, bf16[6,6,6,64,64]{4,3,2,1,0:T(8,128)(2,1)}, bf16[6,6,6,64,...) fusion(bf16[7,7,7,64,64]{4,3,2,1,0:T(8,128)(2,1)} %gather.7), kind=kLoop, calls=%fused_computation.222 | loop fusion | bytes 28311552 | tf_op jit(solution)/shard_map/slice | solution.py:88
  49.6 3.3 %collective-permute-start.9 = (bf16[10,3,4,64]{3,0,2,1:T(8,128)(2,1)S(1)}, bf16[10,3,4,64]{3,0,2,1:T(8,128)(2,1)S(1)}, u32[]{:S(2)}, u32[]{:S(2)}) collective-permute-start(bf16[10,3,4,64]{3,0,2,1:T(8,128)(2,1)S(1)} %get-tuple-element.135), channel_id=1, source_target_pairs={{4,0},{8,4},{12,8},{5,1},{9,5},{13,9},{6,2},{10,6},{14,10},{7,3},{... | collective-permute-start | bytes 46088 | tf_op jit(solution)/shard_map/ppermute | solution.py:25
  52.9 2.5 %collective-permute-start.8 = (bf16[10,3,4,64]{3,0,2,1:T(8,128)(2,1)S(1)}, bf16[10,3,4,64]{3,0,2,1:T(8,128)(2,1)S(1)}, u32[]{:S(2)}, u32[]{:S(2)}) collective-permute-start(bf16[10,3,4,64]{3,0,2,1:T(8,128)(2,1)S(1)} %get-tuple-element.134), channel_id=1, source_target_pairs={{0,4},{4,8},{8,12},{1,5},{5,9},{9,13},{2,6},{6,10},{10,14},{3,7},{... | collective-permute-start | bytes 46088 | tf_op jit(solution)/shard_map/ppermute | solution.py:23
  55.5 4.2 %collective-permute-start.3 = (f32[6,1,4,128]{3,2,1,0:T(4,128)S(1)}, f32[6,1,4,128]{3,2,1,0:T(4,128)S(1)}, u32[]{:S(2)}, u32[]{:S(2)}) collective-permute-start(f32[6,1,4,128]{3,2,1,0:T(4,128)S(1)} %get-tuple-element.127), channel_id=1, source_target_pairs={{4,0},{8,4},{12,8},{5,1},{9,5},{13,9},{6,2},{10,6},{14,10},{7,3},{... | collective-permute-start | bytes 36872 | tf_op jit(solution)/shard_map/ppermute | solution.py:25
  59.8 1.9 %collective-permute-start.2 = (f32[6,1,4,128]{3,2,1,0:T(4,128)S(1)}, f32[6,1,4,128]{3,2,1,0:T(4,128)S(1)}, u32[]{:S(2)}, u32[]{:S(2)}) collective-permute-start(f32[6,1,4,128]{3,2,1,0:T(4,128)S(1)} %get-tuple-element.126), channel_id=1, source_target_pairs={{0,4},{4,8},{8,12},{1,5},{5,9},{9,13},{2,6},{6,10},{10,14},{3,7},{... | collective-permute-start | bytes 36872 | tf_op jit(solution)/shard_map/ppermute | solution.py:23
  62.1 4.1 %collective-permute-done.2 = f32[6,1,4,128]{3,2,1,0:T(4,128)S(1)} collective-permute-done((f32[6,1,4,128]{3,2,1,0:T(4,128)S(1)}, f32[6,1,4,128]{3,2,1,0:T(4,128)S(1)}, u32[]{:S(2)}, u32[]{:S(2)}) %collective-permute-start.2) | collective-permute-done | bytes 12320 | tf_op jit(solution)/shard_map/ppermute | solution.py:23
  66.4 2.4 %collective-permute-start.5 = (f32[6,6,1,128]{3,2,1,0:T(1,128)S(1)}, f32[6,6,1,128]{3,2,1,0:T(1,128)S(1)}, u32[]{:S(2)}, u32[]{:S(2)}) collective-permute-start(f32[6,6,1,128]{3,2,1,0:T(1,128)S(1)} %get-tuple-element.132), channel_id=1, source_target_pairs={{1,0},{2,1},{3,2},{5,4},{6,5},{7,6},{9,8},{10,9},{11,10},{13,12},{... | collective-permute-start | bytes 55304 | tf_op jit(solution)/shard_map/ppermute | solution.py:25
  68.8 3.5 %collective-permute-start.4 = (f32[6,6,1,128]{3,2,1,0:T(1,128)S(1)}, f32[6,6,1,128]{3,2,1,0:T(1,128)S(1)}, u32[]{:S(2)}, u32[]{:S(2)}) collective-permute-start(f32[6,6,1,128]{3,2,1,0:T(1,128)S(1)} %get-tuple-element.133), channel_id=1, source_target_pairs={{0,1},{1,2},{2,3},{4,5},{5,6},{6,7},{8,9},{9,10},{10,11},{12,13},{... | collective-permute-start | bytes 55304 | tf_op jit(solution)/shard_map/ppermute | solution.py:23
  73.0 2.4 %collective-permute-start.11 = (bf16[10,10,3,64]{3,0,2,1:T(8,128)(2,1)S(1)}, bf16[10,10,3,64]{3,0,2,1:T(8,128)(2,1)S(1)}, u32[]{:S(2)}, u32[]{:S(2)}) collective-permute-start(bf16[10,10,3,64]{3,0,2,1:T(8,128)(2,1)S(1)} %get-tuple-element.51), channel_id=1, source_target_pairs={{1,0},{2,1},{3,2},{5,4},{6,5},{7,6},{9,8},{10,9},{11,10},{13,12},{... | collective-permute-start | bytes 115208 | tf_op jit(solution)/shard_map/ppermute | solution.py:25
  75.4 3.7 %collective-permute-start.10 = (bf16[10,10,3,64]{3,0,2,1:T(8,128)(2,1)S(1)}, bf16[10,10,3,64]{3,0,2,1:T(8,128)(2,1)S(1)}, u32[]{:S(2)}, u32[]{:S(2)}) collective-permute-start(bf16[10,10,3,64]{3,0,2,1:T(8,128)(2,1)S(1)} %get-tuple-element.50), channel_id=1, source_target_pairs={{0,1},{1,2},{2,3},{4,5},{5,6},{6,7},{8,9},{9,10},{10,11},{12,13},{... | collective-permute-start | bytes 115208 | tf_op jit(solution)/shard_map/ppermute | solution.py:23
  80.5 2.4 %fusion.82 = (f32[4,4,4,32]{3,2,1,0:T(4,128)S(1)}, f32[4,4,4,32]{3,2,1,0:T(4,128)S(1)}, f32[4,4,4,32]{3,2,1,0:T(4,128)S(1)}) fusion(f32[4,4,4,32]{3,2,1,0:T(4,128)S(1)} %get-tuple-element.53, f32[4,4,4,32]{3,2,1,0:T(4,128)S(1)} %get-tuple-element.54, f32[4,4,4,32]{3,2,1,0:T(4,128)S(1)} %get-tuple-element.55, f32[4,4,4,32]{3,2,1,0:T(4,128)S(1)} %get-tuple-element.56, ...), kind=kLoop, calls=%fused_computation.150 | loop fusion | flops 2549760 | bytes 147456 | tf_op jit(solution)/shard_map/reduce_sum | solution.py:143
  82.9 3.0 %fusion.49 = (f32[4,4,4,32]{3,2,1,0:T(4,128)S(1)}, f32[4,4,4,32]{3,2,1,0:T(4,128)S(1)}, f32[4,4,4,32]{3,2,1,0:T(4,128)S(1)}, f32[4,4,4,32]{3,2,1,0:T(4,128)S(1)}) fusion(f32[4,4,4,32]{3,2,1,0:T(4,128)S(1)} %reshape.286, f32[4,4,4,32]{3,2,1,0:T(4,128)S(1)} %get-tuple-element.173, f32[4,4,4,32]{3,2,1,0:T(4,128)S(1)} %get-tuple-element.174, ...), kind=kLoop, calls=%fused_computation.117 | loop fusion | flops 3399680 | bytes 163840 | tf_op jit(solution)/shard_map/reduce_sum | solution.py:143
  85.9 3.0 %fusion.70 = (f32[4,4,4,32]{3,2,1,0:T(4,128)S(1)}, f32[4,4,4,32]{3,2,1,0:T(4,128)S(1)}, f32[4,4,4,32]{3,2,1,0:T(4,128)S(1)}, f32[4,4,4,32]{3,2,1,0:T(4,128)S(1)}) fusion(f32[4,4,4,32]{3,2,1,0:T(4,128)S(1)} %get-tuple-element.97, f32[4,4,4,32]{3,2,1,0:T(4,128)S(1)} %get-tuple-element.98, f32[4,4,4,32]{3,2,1,0:T(4,128)S(1)} %get-tuple-element.99, ...), kind=kLoop, calls=%fused_computation.138 | loop fusion | flops 3399680 | bytes 188416 | tf_op jit(solution)/shard_map/reduce_sum | solution.py:143
  88.9 3.0 %fusion.43 = (f32[4,4,4,32]{3,2,1,0:T(4,128)S(1)}, f32[4,4,4,32]{3,2,1,0:T(4,128)S(1)}, f32[4,4,4,32]{3,2,1,0:T(4,128)S(1)}, f32[4,4,4,32]{3,2,1,0:T(4,128)S(1)}) fusion(f32[4,4,4,32]{3,2,1,0:T(4,128)S(1)} %get-tuple-element.110, f32[4,4,4,32]{3,2,1,0:T(4,128)S(1)} %get-tuple-element.111, f32[4,4,4,32]{3,2,1,0:T(4,128)S(1)} %get-tuple-element.112, ...), kind=kLoop, calls=%fused_computation.111 | loop fusion | flops 3399680 | bytes 188416 | tf_op jit(solution)/shard_map/reduce_sum | solution.py:143
  91.8 3.0 %fusion.31 = (f32[4,4,4,32]{3,2,1,0:T(4,128)S(1)}, f32[4,4,4,32]{3,2,1,0:T(4,128)S(1)}, f32[4,4,4,32]{3,2,1,0:T(4,128)S(1)}, f32[4,4,4,32]{3,2,1,0:T(4,128)S(1)}) fusion(f32[4,4,4,32]{3,2,1,0:T(4,128)S(1)} %get-tuple-element.157, f32[4,4,4,32]{3,2,1,0:T(4,128)S(1)} %get-tuple-element.158, f32[4,4,4,32]{3,2,1,0:T(4,128)S(1)} %get-tuple-element.159, ...), kind=kLoop, calls=%fused_computation.99 | loop fusion | flops 3399680 | bytes 188416 | tf_op jit(solution)/shard_map/reduce_sum | solution.py:143
  94.8 3.0 %fusion.10 = (f32[4,4,4,32]{3,2,1,0:T(4,128)S(1)}, f32[4,4,4,32]{3,2,1,0:T(4,128)S(1)}, f32[4,4,4,32]{3,2,1,0:T(4,128)S(1)}, f32[4,4,4,32]{3,2,1,0:T(4,128)S(1)}) fusion(f32[4,4,4,32]{3,2,1,0:T(4,128)S(1)} %get-tuple-element.84, f32[4,4,4,32]{3,2,1,0:T(4,128)S(1)} %get-tuple-element.85, f32[4,4,4,32]{3,2,1,0:T(4,128)S(1)} %get-tuple-element.173, ...), kind=kLoop, calls=%fused_computation.78 | loop fusion | flops 3399680 | bytes 188416 | tf_op jit(solution)/shard_map/reduce_sum | solution.py:143
  97.8 3.2 %fusion.61 = (f32[4,4,4,32]{3,2,1,0:T(4,128)S(1)}, f32[4,4,4,32]{3,2,1,0:T(4,128)S(1)}, f32[4,4,4,32]{3,2,1,0:T(4,128)S(1)}, f32[4,4,4,32]{3,2,1,0:T(4,128)S(1)}) fusion(f32[4,4,4,32]{3,2,1,0:T(4,128)S(1)} %get-tuple-element.101, f32[4,4,4,32]{3,2,1,0:T(4,128)S(1)} %get-tuple-element.102, f32[4,4,4,32]{3,2,1,0:T(4,128)S(1)} %get-tuple-element.103, ...), kind=kLoop, calls=%fused_computation.129 | loop fusion | flops 3399680 | bytes 188416 | tf_op jit(solution)/shard_map/reduce_sum | solution.py:143
  102.4 0.6 pad_maximum_fusion.2
  103.9 0.6 pad_maximum_fusion.1
  105.4 0.7 pad_maximum_fusion
  106.2 0.5 reshape.294
  106.7 2.7 %fusion.7 = f32[8,8,64]{2,1,0:T(8,128)S(1)} fusion(bf16[8,13824]{1,0:T(8,128)(2,1)S(1)} %reshape.294, bf16[13824,64]{1,0:T(8,128)(2,1)} %bitcast.138), kind=kOutput, calls=%fused_computation.75 | convolution fusion | flops 14155775 | bytes 1994752 | tf_op jit(solution)/shard_map/dot_general | solution.py:92
  109.8 0.6 fusion.6
  110.3 0.5 copy-done.6
  110.8 0.6 fusion.5
  111.4 0.7 copy-done.5
  112.1 0.6 fusion.4
  112.6 0.4 copy-done.4
  113.0 0.6 fusion.3
  113.6 0.7 copy-done.3
  114.3 0.6 fusion.2
  114.9 0.4 copy-done.2
  115.3 0.6 fusion.1
  115.8 0.7 copy-done.1
  116.5 0.6 fusion
  117.3 1.5 %fusion.91 = f32[4,4,4,32]{3,2,1,0:T(4,128)S(1)} fusion(f32[4,4,4,64]{3,2,1,0:T(4,128)S(1)} %fusion.95, f32[4,4,4,64]{3,2,1,0:T(4,128)S(1)} %get-tuple-element.175, f32[4,4,4,32]{3,2,1,0:T(4,128)S(1)} %get-tuple-element.173, f32[4,4,4,64]{3,2,1,0:T(4,128)S(1)} %get-tuple-element.176, f32[4,4,4,32]{3,2,1,0:T(4,128)S(1)} %get-tuple-element.174, ...), kind=kLoop, calls=%fused_computation.159 | loop fusion | flops 1701888 | bytes 98304 | tf_op jit(solution)/shard_map/reduce_sum | solution.py:134
  118.9 0.6 add_add_fusion.1
  (92 shorter events, 7.6 us)
Async XLA Ops:
  0.0 3.6 %copy-start = (f32[64,64]{1,0:T(8,128)S(1)}, f32[64,64]{1,0:T(8,128)}, u32[]{:S(2)}) copy-start(f32[64,64]{1,0:T(8,128)} %param.8) | copy-start | bytes 49156
  3.8 45.7 %collective-permute-start.7 = (bf16[3,4,4,64]{3,0,2,1:T(4,128)(2,1)S(1)}, bf16[3,4,4,64]{3,0,2,1:T(4,128)(2,1)S(1)}, u32[]{:S(2)}, u32[]{:S(2)}) collective-permute-start(bf16[3,4,4,64]{3,0,2,1:T(4,128)(2,1)S(1)} %copy.29), channel_id=1, source_target_pairs={{16,0},{17,1},{18,2},{19,3},{20,4},{21,5},{22,6},{23,7},{24,8},{25... | collective-permute-start | bytes 18440 | tf_op jit(solution)/shard_map/ppermute | solution.py:25
  5.1 44.4 %collective-permute-start.6 = (bf16[3,4,4,64]{3,0,2,1:T(4,128)(2,1)S(1)}, bf16[3,4,4,64]{3,0,2,1:T(4,128)(2,1)S(1)}, u32[]{:S(2)}, u32[]{:S(2)}) collective-permute-start(bf16[3,4,4,64]{3,0,2,1:T(4,128)(2,1)S(1)} %copy.28), channel_id=1, source_target_pairs={{0,16},{1,17},{2,18},{3,19},{4,20},{5,21},{6,22},{7,23},{8,24},{9,... | collective-permute-start | bytes 18440 | tf_op jit(solution)/shard_map/ppermute | solution.py:23
  8.2 47.2 %collective-permute-start.1 = (f32[1,4,4,128]{3,2,1,0:T(4,128)S(1)}, f32[1,4,4,128]{3,2,1,0:T(4,128)S(1)}, u32[]{:S(2)}, u32[]{:S(2)}) collective-permute-start(f32[1,4,4,128]{3,2,1,0:T(4,128)S(1)} %get-tuple-element.131), channel_id=1, source_target_pairs={{16,0},{17,1},{18,2},{19,3},{20,4},{21,5},{22,6},{23,7},{24,8},{25... | collective-permute-start | bytes 24584 | tf_op jit(solution)/shard_map/ppermute | solution.py:25
  9.5 45.9 %collective-permute-start = (f32[1,4,4,128]{3,2,1,0:T(4,128)S(1)}, f32[1,4,4,128]{3,2,1,0:T(4,128)S(1)}, u32[]{:S(2)}, u32[]{:S(2)}) collective-permute-start(f32[1,4,4,128]{3,2,1,0:T(4,128)S(1)} %get-tuple-element.130), channel_id=1, source_target_pairs={{0,16},{1,17},{2,18},{3,19},{4,20},{5,21},{6,22},{7,23},{8,24},{9,... | collective-permute-start | bytes 24584 | tf_op jit(solution)/shard_map/ppermute | solution.py:23
  49.6 23.4 %collective-permute-start.9 = (bf16[10,3,4,64]{3,0,2,1:T(8,128)(2,1)S(1)}, bf16[10,3,4,64]{3,0,2,1:T(8,128)(2,1)S(1)}, u32[]{:S(2)}, u32[]{:S(2)}) collective-permute-start(bf16[10,3,4,64]{3,0,2,1:T(8,128)(2,1)S(1)} %get-tuple-element.135), channel_id=1, source_target_pairs={{4,0},{8,4},{12,8},{5,1},{9,5},{13,9},{6,2},{10,6},{14,10},{7,3},{... | collective-permute-start | bytes 46088 | tf_op jit(solution)/shard_map/ppermute | solution.py:25
  52.9 20.0 %collective-permute-start.8 = (bf16[10,3,4,64]{3,0,2,1:T(8,128)(2,1)S(1)}, bf16[10,3,4,64]{3,0,2,1:T(8,128)(2,1)S(1)}, u32[]{:S(2)}, u32[]{:S(2)}) collective-permute-start(bf16[10,3,4,64]{3,0,2,1:T(8,128)(2,1)S(1)} %get-tuple-element.134), channel_id=1, source_target_pairs={{0,4},{4,8},{8,12},{1,5},{5,9},{9,13},{2,6},{6,10},{10,14},{3,7},{... | collective-permute-start | bytes 46088 | tf_op jit(solution)/shard_map/ppermute | solution.py:23
  55.5 6.6 %collective-permute-start.3 = (f32[6,1,4,128]{3,2,1,0:T(4,128)S(1)}, f32[6,1,4,128]{3,2,1,0:T(4,128)S(1)}, u32[]{:S(2)}, u32[]{:S(2)}) collective-permute-start(f32[6,1,4,128]{3,2,1,0:T(4,128)S(1)} %get-tuple-element.127), channel_id=1, source_target_pairs={{4,0},{8,4},{12,8},{5,1},{9,5},{13,9},{6,2},{10,6},{14,10},{7,3},{... | collective-permute-start | bytes 36872 | tf_op jit(solution)/shard_map/ppermute | solution.py:25
  59.8 6.5 %collective-permute-start.2 = (f32[6,1,4,128]{3,2,1,0:T(4,128)S(1)}, f32[6,1,4,128]{3,2,1,0:T(4,128)S(1)}, u32[]{:S(2)}, u32[]{:S(2)}) collective-permute-start(f32[6,1,4,128]{3,2,1,0:T(4,128)S(1)} %get-tuple-element.126), channel_id=1, source_target_pairs={{0,4},{4,8},{8,12},{1,5},{5,9},{9,13},{2,6},{6,10},{10,14},{3,7},{... | collective-permute-start | bytes 36872 | tf_op jit(solution)/shard_map/ppermute | solution.py:23
  66.4 12.7 %collective-permute-start.5 = (f32[6,6,1,128]{3,2,1,0:T(1,128)S(1)}, f32[6,6,1,128]{3,2,1,0:T(1,128)S(1)}, u32[]{:S(2)}, u32[]{:S(2)}) collective-permute-start(f32[6,6,1,128]{3,2,1,0:T(1,128)S(1)} %get-tuple-element.132), channel_id=1, source_target_pairs={{1,0},{2,1},{3,2},{5,4},{6,5},{7,6},{9,8},{10,9},{11,10},{13,12},{... | collective-permute-start | bytes 55304 | tf_op jit(solution)/shard_map/ppermute | solution.py:25
  68.8 10.3 %collective-permute-start.4 = (f32[6,6,1,128]{3,2,1,0:T(1,128)S(1)}, f32[6,6,1,128]{3,2,1,0:T(1,128)S(1)}, u32[]{:S(2)}, u32[]{:S(2)}) collective-permute-start(f32[6,6,1,128]{3,2,1,0:T(1,128)S(1)} %get-tuple-element.133), channel_id=1, source_target_pairs={{0,1},{1,2},{2,3},{4,5},{5,6},{6,7},{8,9},{9,10},{10,11},{12,13},{... | collective-permute-start | bytes 55304 | tf_op jit(solution)/shard_map/ppermute | solution.py:23
  73.0 29.0 %collective-permute-start.11 = (bf16[10,10,3,64]{3,0,2,1:T(8,128)(2,1)S(1)}, bf16[10,10,3,64]{3,0,2,1:T(8,128)(2,1)S(1)}, u32[]{:S(2)}, u32[]{:S(2)}) collective-permute-start(bf16[10,10,3,64]{3,0,2,1:T(8,128)(2,1)S(1)} %get-tuple-element.51), channel_id=1, source_target_pairs={{1,0},{2,1},{3,2},{5,4},{6,5},{7,6},{9,8},{10,9},{11,10},{13,12},{... | collective-permute-start | bytes 115208 | tf_op jit(solution)/shard_map/ppermute | solution.py:25
  75.4 26.6 %collective-permute-start.10 = (bf16[10,10,3,64]{3,0,2,1:T(8,128)(2,1)S(1)}, bf16[10,10,3,64]{3,0,2,1:T(8,128)(2,1)S(1)}, u32[]{:S(2)}, u32[]{:S(2)}) collective-permute-start(bf16[10,10,3,64]{3,0,2,1:T(8,128)(2,1)S(1)} %get-tuple-element.50), channel_id=1, source_target_pairs={{0,1},{1,2},{2,3},{4,5},{5,6},{6,7},{8,9},{9,10},{10,11},{12,13},{... | collective-permute-start | bytes 115208 | tf_op jit(solution)/shard_map/ppermute | solution.py:23
  106.7 3.1 %copy-start.7 = (bf16[6,6,6,64,64]{4,3,2,1,0:T(8,128)(2,1)S(1)}, bf16[6,6,6,64,64]{4,3,2,1,0:T(8,128)(2,1)}, u32[]{:S(2)}) copy-start(bf16[6,6,6,64,64]{4,3,2,1,0:T(8,128)(2,1)} %get-tuple-element.38) | copy-start | bytes 5308420
  106.7 4.1 %copy-start.6 = (bf16[6,6,6,64,64]{4,3,2,1,0:T(8,128)(2,1)S(1)}, bf16[6,6,6,64,64]{4,3,2,1,0:T(8,128)(2,1)}, u32[]{:S(2)}) copy-start(bf16[6,6,6,64,64]{4,3,2,1,0:T(8,128)(2,1)} %get-tuple-element.37) | copy-start | bytes 5308420
  109.8 2.3 %copy-start.5 = (bf16[6,6,6,64,64]{4,3,2,1,0:T(8,128)(2,1)S(1)}, bf16[6,6,6,64,64]{4,3,2,1,0:T(8,128)(2,1)}, u32[]{:S(2)}) copy-start(bf16[6,6,6,64,64]{4,3,2,1,0:T(8,128)(2,1)} %get-tuple-element.36) | copy-start | bytes 5308420
  110.8 2.2 %copy-start.4 = (bf16[6,6,6,64,64]{4,3,2,1,0:T(8,128)(2,1)S(1)}, bf16[6,6,6,64,64]{4,3,2,1,0:T(8,128)(2,1)}, u32[]{:S(2)}) copy-start(bf16[6,6,6,64,64]{4,3,2,1,0:T(8,128)(2,1)} %get-tuple-element.35) | copy-start | bytes 5308420
  112.1 2.2 %copy-start.3 = (bf16[6,6,6,64,64]{4,3,2,1,0:T(8,128)(2,1)S(1)}, bf16[6,6,6,64,64]{4,3,2,1,0:T(8,128)(2,1)}, u32[]{:S(2)}) copy-start(bf16[6,6,6,64,64]{4,3,2,1,0:T(8,128)(2,1)} %get-tuple-element.34) | copy-start | bytes 5308420
  113.0 2.2 %copy-start.2 = (bf16[6,6,6,64,64]{4,3,2,1,0:T(8,128)(2,1)S(1)}, bf16[6,6,6,64,64]{4,3,2,1,0:T(8,128)(2,1)}, u32[]{:S(2)}) copy-start(bf16[6,6,6,64,64]{4,3,2,1,0:T(8,128)(2,1)} %get-tuple-element.33) | copy-start | bytes 5308420
  114.3 2.2 %copy-start.1 = (bf16[6,6,6,64,64]{4,3,2,1,0:T(8,128)(2,1)S(1)}, bf16[6,6,6,64,64]{4,3,2,1,0:T(8,128)(2,1)}, u32[]{:S(2)}) copy-start(bf16[6,6,6,64,64]{4,3,2,1,0:T(8,128)(2,1)} %get-tuple-element.32) | copy-start | bytes 5308420
  115.3 1.9 %copy-start.8 = (f32[64,64]{1,0:T(8,128)S(1)}, f32[64,64]{1,0:T(8,128)}, u32[]{:S(2)}) copy-start(f32[64,64]{1,0:T(8,128)} %param.10) | copy-start | bytes 49156
where the time goes:
time: 120 us
  local copies, waits for them, and re-layouts  47 us (39%)
  starting transfers between devices  32.5 us (27%)
  other arithmetic  28.2 us (24%)
  matrix products  6.98 us (6%)
  waiting for transfers between devices  4.17 us (3%)
    slice x1, local copies, waits for them, and re-layouts, translate(): operators[1 - class_x:7 - class_x, 1 - class_y:7 - class_y, 1 - class_z:7...  21.4 us
    reduce_sum x7, other arithmetic, pair_sum(): return jnp.sum(kernel * source_q[..., None, :], axis=-1)  20.5 us
    ppermute x6, starting transfers between devices, with_halo(): lax.ppermute(tail, axis, [(i, (i + 1) % count) for i in range(ends)])  17.6 us
    ppermute x6, starting transfers between devices, with_halo(): lax.ppermute(head, axis, [((i + 1) % count, i) for i in range(ends)])  14.9 us
    gather x2, local copies, waits for them, and re-layouts, full_table(): jnp.take(padded, jnp.asarray(table_rows(translations.shape[0])), axis=0)  12.9 us
    dot_general x8, matrix products, translate(): jnp.dot(flat_rows, slab_table, preferred_element_type=jnp.float32)  6.63 us
    unnamed x24, local copies, waits for them, and re-layouts  4.4 us
    ppermute x6, waiting for transfers between devices, with_halo(): lax.ppermute(tail, axis, [(i, (i + 1) % count) for i in range(ends)])  4.15 us
  transfers between devices with their start and end apart: 12, of which 1 were waited for; matrix products, arithmetic and copies ran while one was open for 51% of the time, Pallas kernels for 0%

commit v1 on v0

v1 whole, which is shorter than its diff:
```python
import functools
import math

import jax
import jax.numpy as jnp
import numpy as np
from jax import lax
from jax.experimental import pallas as pl
from jax.experimental.pallas import tpu as pltpu
from jax.sharding import PartitionSpec as P

BODIES = 32
RADIUS = 0.9
REACH = 3
SPAN = 2 * REACH + 1
F32 = jnp.float32
BF16 = jnp.bfloat16
NT = (((1,), (1,)), ((), ()))


def surface(points):
    number = np.arange(points).astype(np.float32)
    height = np.float32(1.0) - (np.float32(2.0) * number + np.float32(1.0)) / np.float32(points)
    across = np.sqrt(np.float32(1.0) - height * height)
    turned = number * np.float32(math.pi * (3.0 - math.sqrt(5.0)))
    columns = np.zeros((points, 128), np.float32)
    columns[:, 0] = RADIUS * across * np.cos(turned)
    columns[:, 1] = RADIUS * across * np.sin(turned)
    columns[:, 2] = RADIUS * height
    return columns


def numbering():
    table, count = {}, 0
    for ox in range(-REACH, REACH + 1):
        for oy in range(-REACH, REACH + 1):
            for oz in range(-REACH, REACH + 1):
                if max(abs(ox), abs(oy), abs(oz)) >= 2:
                    table[ox, oy, oz] = count
                    count += 1
    return table


def split(value):
    high = value.astype(BF16)
    return high, (value - high.astype(F32)).astype(BF16)


def surface_green(sphere, offs_ref, x, y):
    rows = [offs_ref[c, x, pl.ds(y, 1), :] - 0.5 for c in range(3)]
    square = None
    for c in range(3):
        delta = sphere[:, c : c + 1] - rows[c]
        square = delta * delta if square is None else square + delta * delta
    return lax.rsqrt(square)


def upward_kernel(offs_ref, q_ref, sphere_ref, uinv_ref, shuffle_ref, u_ref, check_ref, wide_ref):
    _, lx, ly, lanes = offs_ref.shape
    lz = lanes // BODIES
    points = uinv_ref.shape[0]
    sphere = sphere_ref[...]
    segment = (
        lax.broadcasted_iota(jnp.int32, (8, lanes), 1) // BODIES
        == lax.broadcasted_iota(jnp.int32, (8, lanes), 0)
    ).astype(BF16)
    wide_ref[...] = jnp.zeros_like(wide_ref)
    wide_ref[:points, :points] = uinv_ref[...]
    wide_ref[points:, points:] = uinv_ref[...]
    for x in range(lx):
        for pair in range(ly // 2):
            parts = [
                surface_green(sphere, offs_ref, x, 2 * pair + par) * q_ref[x, pl.ds(2 * pair + par, 1), :]
                for par in range(2)
            ]
            high, low = split(jnp.concatenate(parts, axis=0))
            sums = lax.dot_general(segment, high, NT, preferred_element_type=F32)
            sums = sums + lax.dot_general(segment, low, NT, preferred_element_type=F32)
            check_ref[pl.ds((x * (ly // 2) + pair) * lz, lz), :] = sums[:lz]
    density = jnp.dot(
        check_ref[...], wide_ref[...], precision=lax.Precision.HIGHEST, preferred_element_type=F32
    ).astype(BF16)
    u_ref[...] = jnp.dot(density, shuffle_ref[...], preferred_element_type=F32)


def table_kernel(t_ref, w_ref, rows_ref):
    count, width = t_ref.shape
    groups = width // 128
    stride = rows_ref.shape[0] // groups
    points = math.isqrt(width)
    half = points // 2
    order = numbering()
    for a in range(groups):
        rows_ref[pl.ds(a * stride, count), :] = t_ref[:, a * 128 : (a + 1) * 128].astype(F32)
    left = lax.broadcasted_iota(jnp.int32, (groups, 128), 1) < points
    zero = jnp.zeros((groups, 128), F32)
    for ox in range(SPAN):
        for oy in range(SPAN):
            for k in range((SPAN + 1) // 2):
                loaded = []
                for oz in (2 * k, 2 * k + 1):
                    at = order.get((ox - REACH, oy - REACH, oz - REACH))
                    loaded.append(zero if at is None else rows_ref[pl.ds(at, groups, stride=stride), :])
                one, two = loaded
                even = jnp.where(left, one, pltpu.roll(two, points, 1))
                odd = jnp.where(left, pltpu.roll(one, points, 1), two)
                at = slice(k * 128, (k + 1) * 128)
                w_ref[ox, pl.ds(oy * points, half), at] = even.astype(BF16)
                w_ref[ox, pl.ds(oy * points + half, half), at] = odd.astype(BF16)


def final_kernel(
    offs_ref, u_ref, w_ref, dinv_ref, sphere_ref, body_ref, out_ref, left_ref, acc_ref, dense_ref, win_ref, sum_ref
):
    _, lx, ly, lanes = offs_ref.shape
    lz = lanes // BODIES
    points = dinv_ref.shape[0]
    ext_x, pairs, ext_z, _ = u_ref.shape
    half = ly // 2
    block = half * ext_z
    width = (SPAN - 1) * points
    for x in range(ext_x):
        for j in range(SPAN // 2):
            left_ref[pl.ds(x * block, block), j * 128 : (j + 1) * 128] = (
                u_ref[x, j : j + half].reshape(block, 128).astype(BF16)
            )
    wide = jnp.concatenate([dinv_ref[...]] * 2, axis=0)
    expand = (
        lax.broadcasted_iota(jnp.int32, (lx * half * lz, lx * half * lanes), 1) // BODIES
        == lax.broadcasted_iota(jnp.int32, (lx * half * lz, lx * half * lanes), 0)
    ).astype(BF16)
    lane = lax.broadcasted_iota(jnp.int32, (lz, 128), 1)
    level = lax.broadcasted_iota(jnp.int32, (lz, 128), 0)
    for cy in range(2):
        total = [None] * lx
        for ox in range(-REACH, REACH + 1):
            chosen = [b for b in range(lx) if not (ox == -REACH and b % 2 == 0) and not (ox == REACH and b % 2 == 1)]
            parts = [left_ref[pl.ds((b + ox + 2) * block, block), :] for b in chosen]
            lhs = jnp.concatenate(parts, axis=0)
            rhs = w_ref[ox + REACH, pl.ds((1 - cy) * points, width), :]
            got = jnp.dot(lhs, rhs, preferred_element_type=F32)
            for n, b in enumerate(chosen):
                piece = got[n * block : (n + 1) * block]
                total[b] = piece if total[b] is None else total[b] + piece
        for b in range(lx):
            for p in range(half):
                acc_ref[b * half + p, pl.ds(8, ext_z), :] = total[b][p * ext_z : (p + 1) * ext_z]
        for g in range(lx * half):
            folded = None
            for k in range((SPAN + 1) // 2):
                shown = []
                for oz in (2 * k - REACH, 2 * k + 1 - REACH):
                    if oz > REACH:
                        shown.append(jnp.zeros((lz, 128), F32))
                        continue
                    got = acc_ref[g, pl.ds(8 + oz + 2, lz), k * 128 : (k + 1) * 128]
                    if oz == -REACH:
                        got = jnp.where(level % 2 == 1, got, 0.0)
                    if oz == REACH:
                        got = jnp.where(level % 2 == 0, got, 0.0)
                    shown.append(got)
                both = jnp.where(lane < points, shown[0], shown[1])
                folded = both if folded is None else folded + both
            sum_ref[pl.ds(g * lz, lz), :] = folded
        dense = jnp.dot(sum_ref[...], wide, precision=lax.Precision.HIGHEST, preferred_element_type=F32)
        high, low = split(dense.T)
        spread = jnp.dot(high, expand, preferred_element_type=F32)
        spread = spread + jnp.dot(low, expand, preferred_element_type=F32)
        for g in range(lx * half):
            dense_ref[g, cy] = spread[:, g * lanes : (g + 1) * lanes]

    rows = (lx + 2) * (ly + 2)
    place = lax.broadcasted_iota(jnp.int32, (rows, 128), 0)
    spot = lax.broadcasted_iota(jnp.int32, (rows, 128), 1) // BODIES
    base = [place // (ly + 2) - 1, place % (ly + 2) - 1, None]
    for w in range(2):
        for c in range(3):
            at = base[c] if c < 2 else spot - 1 + 2 * w
            win_ref[w * 3 + c] = body_ref[w, c] + at.astype(F32)
        for s in range(2):
            fit = (spot >= s) & (spot < s + 3)
            win_ref[6 + w * 2 + s] = jnp.where(fit, body_ref[w, 3], 0.0)

    sphere = sphere_ref[...]
    ones = jnp.ones((8, 128), BF16)

    def plane(x, carry):
        lead = lax.broadcasted_iota(jnp.int32, (ly, lanes), 0)
        spots = lax.broadcasted_iota(jnp.int32, (ly, lanes), 1) // BODIES
        places = [offs_ref[0, x] + x.astype(F32), offs_ref[1, x] + lead.astype(F32), offs_ref[2, x] + spots.astype(F32)]
        turned = jnp.concatenate(places + [places[0]] * (4 - 3), axis=0).T
        for y in range(ly):
            gathered = []
            for z in range(lz):
                w, s = z // 2, z % 2
                target = [turned[z * BODIES : (z + 1) * BODIES, c * ly + y : c * ly + y + 1] for c in range(3)]
                total = None
                for dx in range(3):
                    for dy in range(3):
                        r = (x + dx) * (ly + 2) + y + dy
                        square = None
                        for c in range(3):
                            delta = target[c] - win_ref[w * 3 + c, pl.ds(r, 1), :]
                            square = delta * delta if square is None else square + delta * delta
                        inverse = lax.rsqrt(square)
                        if dx == 1 and dy == 1:
                            inverse = jnp.where(square > 0.0, inverse, 0.0)
                        term = inverse * win_ref[6 + w * 2 + s, pl.ds(r, 1), :]
                        total = term if total is None else total + term
                gathered.append(total)
            high, low = split(jnp.concatenate(gathered, axis=0))
            near = lax.dot_general(ones, high, NT, preferred_element_type=F32)
            near = near + lax.dot_general(ones, low, NT, preferred_element_type=F32)
            kernel = surface_green(sphere, offs_ref, x, y)
            far = jnp.sum(kernel * dense_ref[x * half + y // 2, y % 2], axis=0, keepdims=True)
            out_ref[x, pl.ds(y, 1), :] = near[:1] + far
        return carry

    lax.fori_loop(0, lx, plane, 0)


def swap(low, high, axis):
    count = lax.axis_size(axis)
    even = lax.axis_index(axis) % 2 == 0
    first = [(i, i + 1) for i in range(0, count - 1, 2)]
    second = [(i, i + 1) for i in range(1, count - 1, 2)]

    def both(pairs):
        return [pair for i, j in pairs for pair in ((i, j), (j, i))]

    one = lax.ppermute(jnp.where(even, high, low), axis, both(first))
    if not second:
        two = jnp.zeros_like(one)
    else:
        two = lax.ppermute(jnp.where(even, low, high), axis, both(second))
    return jnp.where(even, two, one), jnp.where(even, one, two)


def vmem():
    return pl.BlockSpec(memory_space=pltpu.VMEM)


def per_device(offsets, charges, up_inverse, translations, down_inverse):
    points = up_inverse.shape[0]
    _, lx, ly, lanes = offsets.shape
    lz = lanes // BODIES
    half = ly // 2
    sphere = jnp.asarray(surface(points))
    source = np.concatenate([np.arange(0, points, 2), np.arange(1, points, 2)])
    shuffle = np.zeros((2 * points, 2 * points), np.float32)
    for par in range(2):
        shuffle[par * points + source, par * points + np.arange(points)] = 1.0
    density = pl.pallas_call(
        upward_kernel,
        out_shape=jax.ShapeDtypeStruct((lx * half * lz, 2 * points), F32),
        in_specs=[vmem()] * 5,
        out_specs=vmem(),
        scratch_shapes=[pltpu.VMEM((lx * half * lz, 2 * points), F32), pltpu.VMEM((2 * points, 2 * points), F32)],
        name="upward",
    )(offsets, charges, sphere, up_inverse, jnp.asarray(shuffle, BF16))
    count, width = translations.shape
    stride = (count + 7) // 8 * 8
    weights = pl.pallas_call(
        table_kernel,
        out_shape=jax.ShapeDtypeStruct((SPAN, SPAN * points, (SPAN + 1) * points), BF16),
        in_specs=[vmem()],
        out_specs=vmem(),
        scratch_shapes=[pltpu.VMEM((width // 128 * stride, 128), F32)],
        compiler_params=pltpu.CompilerParams(vmem_limit_bytes=20 << 20),
        name="table",
    )(translations)

    dense = density.reshape(lx, half, lz, 2 * points)
    body = jnp.concatenate([offsets, charges[None]], axis=0)

    def pack(one, two):
        return jnp.concatenate([one.reshape(-1, 128), two.reshape(-1, 128)], axis=0)

    def unpack(packet, one, two):
        cut = math.prod(one) // 128
        return packet[:cut].reshape(one), packet[cut:].reshape(two)

    size = (lx, 1, lz, 2 * points), (4, lx, 1, lanes)
    below, above = swap(pack(dense[:, :1], body[:, :, :1]), pack(dense[:, -1:], body[:, :, -1:]), "gy")
    below, above = unpack(below, *size), unpack(above, *size)
    dense = jnp.concatenate([below[0], dense, above[0]], axis=1)
    body = jnp.concatenate([below[1], body, above[1]], axis=2)
    size = (lx, half + 2, 2, 2 * points), (4, lx, ly + 2, BODIES)
    below, above = swap(
        pack(dense[:, :, :2], body[..., :BODIES]), pack(dense[:, :, -2:], body[..., -BODIES:]), "gz"
    )
    below, above = unpack(below, *size), unpack(above, *size)
    dense = jnp.concatenate([below[0], dense, above[0]], axis=2)
    body = jnp.concatenate([below[1], body, above[1]], axis=3)
    size = (2, half + 2, lz + 4, 2 * points), (4, 1, ly + 2, lanes + 2 * BODIES)
    below, above = swap(pack(dense[:2], body[:, :1]), pack(dense[-2:], body[:, -1:]), "gx")
    below, above = unpack(below, *size), unpack(above, *size)
    dense = jnp.concatenate([below[0], dense, above[0]], axis=0)
    body = jnp.concatenate([below[1], body, above[1]], axis=1)
    rows = (lx + 2) * (ly + 2)
    body = jnp.stack([body[..., :lanes], body[..., 2 * BODIES :]]).reshape(2, 4, rows, lanes)

    ext = (lx + 4) * half * (lz + 4)
    return pl.pallas_call(
        final_kernel,
        out_shape=jax.ShapeDtypeStruct((lx, ly, lanes), F32),
        in_specs=[vmem()] * 6,
        out_specs=vmem(),
        scratch_shapes=[
            pltpu.VMEM((ext, 6 * points), BF16),
            pltpu.VMEM((lx * half, 8 + lz + 4 + 8, (SPAN + 1) * points), F32),
            pltpu.VMEM((lx * half, 2, points, lanes), F32),
            pltpu.VMEM((10, rows, lanes), F32),
            pltpu.VMEM((lx * half * lz, 2 * points), F32),
        ],
        compiler_params=pltpu.CompilerParams(vmem_limit_bytes=30 << 20),
        name="final",
    )(offsets, dense, weights, down_inverse, sphere, body)


def solution(mesh):
    in_specs = (P(None, "gx", "gy", "gz"), P("gx", "gy", "gz"), P(), P(), P())
    out_specs = P("gx", "gy", "gz")
    return jax.shard_map(
        per_device, mesh=mesh, in_specs=in_specs, out_specs=out_specs, check_vma=False
    )
```

time: 120 us -> 43.9 us (0.37)
  the two profiles are of different devices: /device:TPU:12 before, /device:TPU:11 now
where the time goes in v1:
time: 43.9 us; the launch traced here: 43.1 us
  Pallas kernels  13.9 us (32%)
  starting transfers between devices  10.1 us (23%)
  local copies, waits for them, and re-layouts  7.84 us (18%)
  other arithmetic  5.79 us (13%)
  waiting for transfers between devices  5.26 us (12%)
    pallas_call x1, Pallas kernels, per_device(): pl.pallas_call(final_kernel, out_shape=jax.ShapeDtypeStruct((lx, ly, lane...  7.64 us
    ppermute x2, starting transfers between devices, swap(): two = lax.ppermute(jnp.where(even, low, high), axis, both(second))  6.32 us
    pallas_call x1, Pallas kernels, per_device(): pl.pallas_call(table_kernel, out_shape=jax.ShapeDtypeStruct((SPAN, SPAN *...  4.04 us
    ppermute x3, starting transfers between devices, swap(): one = lax.ppermute(jnp.where(even, high, low), axis, both(first))  3.74 us
    ppermute x2, waiting for transfers between devices, swap(): two = lax.ppermute(jnp.where(even, low, high), axis, both(second))  3.47 us
    slice x9, local copies, waits for them, and re-layouts, unpack(): return (packet[:cut].reshape(one), packet[cut:].reshape(two))  2.43 us
    reshape x4, local copies, waits for them, and re-layouts, unpack(): return (packet[:cut].reshape(one), packet[cut:].reshape(two))  2.35 us
    pallas_call x1, Pallas kernels, per_device(): pl.pallas_call(upward_kernel, out_shape=jax.ShapeDtypeStruct((lx * half *...  2.26 us
  transfers between devices with their start and end apart: 5, of which 4 were waited for; matrix products, arithmetic and copies ran while one was open for 0% of the time, Pallas kernels for 9%

profile of v1, /device:TPU:11, one launch (start us, length us, event | category | flops | bytes accessed | tf_op | source)
XLA Modules:
  0.0 43.1 jit_solution(2548928587492914609)
XLA Ops:
  0.0 2.3 %upward.1 = f32[32,128]{1,0:T(8,128)} custom-call(f32[3,4,4,128]{3,2,1,0:T(4,128)} %offs_ref.3, f32[4,4,128]{2,1,0:T(4,128)} %q_ref.1, f32[64,128]{1,0:T(8,128)} %constant.41.clone.sphere_ref, f32[64,64]{1,0:T(8,128)} %uinv_ref.1, bf16[128,128]{1,0:T(8,128)(2,1)} %constant.42.clone.shuffle_ref), custom_call_target="tpu_custom_call" | custom-call | tf_op jit(solution)/shard_map/upward/pallas_call | solution.py:253
  2.3 0.7 %fusion.10 = (f32[4,1,4,128]{3,2,1,0:T(4,128)S(1)}, f32[4,1,4,128]{3,2,1,0:T(4,128)S(1)}) fusion(f32[4,2,4,128]{3,2,1,0:T(4,128)} %bitcast.22), kind=kLoop, calls=%fused_computation.35 | loop fusion | bytes 32768 | tf_op jit(solution)/shard_map/slice | solution.py:284
  3.0 0.8 %pad_maximum_fusion.17 = (f32[4,4,1,128]{3,2,1,0:T(1,128)S(1)}, f32[4,4,1,128]{3,2,1,0:T(1,128)S(1)}) fusion(f32[1,4,4,128]{3,2,1,0:T(4,128)} %bitcast.28, f32[3,4,4,128]{3,2,1,0:T(4,128)} %offs_ref.3), kind=kLoop, calls=%fused_computation.26 | loop fusion | flops 4096 | bytes 49152 | tf_op jit(solution)/shard_map/slice | solution.py:284
  3.8 3.1 %collective-permute-start = (f32[32,128]{1,0:T(8,128)S(1)}, f32[32,128]{1,0:T(8,128)S(1)}, u32[]{:S(2)}, u32[]{:S(2)}) collective-permute-start(f32[32,128]{1,0:T(8,128)S(1)} %get-tuple-element.23), channel_id=1, source_target_pairs={{4,8},{8,4},{5,9},{9,5},{6,10},{10,6},{7,11},{11,7},{20,24},{24,20... | collective-permute-start | bytes 49160 | tf_op jit(solution)/shard_map/ppermute | solution.py:235
  7.0 0.1 collective-permute-start.1
  7.0 2.2 %collective-permute-done = f32[32,128]{1,0:T(8,128)S(1)} collective-permute-done((f32[32,128]{1,0:T(8,128)S(1)}, f32[32,128]{1,0:T(8,128)S(1)}, u32[]{:S(2)}, u32[]{:S(2)}) %collective-permute-start) | collective-permute-done | bytes 16416 | tf_op jit(solution)/shard_map/ppermute | solution.py:235
  9.2 0.4 collective-permute-done.1
  9.6 0.7 %pad_maximum_fusion.11 = f32[4,4,4,128]{3,2,1,0:T(4,128)S(1)} fusion(f32[4,1,4,128]{3,2,1,0:T(4,128)S(1)} %bitcast.49, f32[4,2,4,128]{3,2,1,0:T(4,128)} %bitcast.23, f32[4,1,4,128]{3,2,1,0:T(4,128)S(1)} %bitcast.46), kind=kLoop, calls=%fused_computation.12 | loop fusion | flops 16384 | bytes 65536 | tf_op jit(solution)/shard_map/concatenate | solution.py:286
  10.4 0.8 %pad_maximum_fusion.3 = f32[4,4,6,128]{3,2,1,0:T(8,128)S(1)} fusion(f32[4,4,1,128]{3,2,1,0:T(1,128)S(1)} %bitcast.39, f32[1,4,4,128]{3,2,1,0:T(4,128)} %bitcast.29, f32[3,4,4,128]{3,2,1,0:T(4,128)} %offs_ref.3, f32[4,4,1,128]{3,2,1,0:T(1,128)S(1)} %bitcast.36), kind=kLoop, calls=%fused_computation.3 | loop fusion | flops 36864 | bytes 98304 | tf_op jit(solution)/shard_map/concatenate | solution.py:287
  11.2 0.1 fusion.6
  11.2 0.1 reshape.90
  11.3 0.1 reshape.92
  11.4 3.2 %collective-permute-start.2 = (f32[56,128]{1,0:T(8,128)S(1)}, f32[56,128]{1,0:T(8,128)S(1)}, u32[]{:S(2)}, u32[]{:S(2)}) collective-permute-start(f32[56,128]{1,0:T(8,128)S(1)} %get-tuple-element.15), channel_id=1, source_target_pairs={{1,2},{2,1},{5,6},{6,5},{9,10},{10,9},{13,14},{14,13},{17,18},{18,... | collective-permute-start | bytes 86024 | tf_op jit(solution)/shard_map/ppermute | solution.py:235
  14.6 0.1 collective-permute-start.3
  14.7 1.3 %collective-permute-done.2 = f32[56,128]{1,0:T(8,128)S(1)} collective-permute-done((f32[56,128]{1,0:T(8,128)S(1)}, f32[56,128]{1,0:T(8,128)S(1)}, u32[]{:S(2)}, u32[]{:S(2)}) %collective-permute-start.2) | collective-permute-done | bytes 28704 | tf_op jit(solution)/shard_map/ppermute | solution.py:235
  16.0 1.4 %collective-permute-done.3 = f32[56,128]{1,0:T(8,128)S(1)} collective-permute-done((f32[56,128]{1,0:T(8,128)S(1)}, f32[56,128]{1,0:T(8,128)S(1)}, u32[]{:S(2)}, u32[]{:S(2)}) %collective-permute-start.3) | collective-permute-done | bytes 28704 | tf_op jit(solution)/shard_map/ppermute | solution.py:231
  17.5 0.1 reshape.97
  17.5 0.1 reshape.96
  17.6 0.7 %pad_maximum_fusion.4 = f32[4,4,8,128]{3,2,1,0:T(8,128)S(1)} fusion(f32[4,4,2,128]{3,2,1,0:T(2,128)S(1)} %bitcast.34, f32[4,1,4,128]{3,2,1,0:T(4,128)S(1)} %bitcast.50, f32[4,2,4,128]{3,2,1,0:T(4,128)} %bitcast.24, f32[4,1,4,128]{3,2,1,0:T(4,128)S(1)} %bitcast.47, f32[4,4,2,128]{3,2,1,0:T(2,128)S(1)} %bitcast.32), kind=kLoop, calls=%fused_computation.4 | loop fusion | flops 65536 | bytes 131072 | tf_op jit(solution)/shard_map/concatenate | solution.py:293
  18.4 0.9 %pad_maximum_fusion.5 = (f32[4,1,6,192]{3,2,1,0:T(8,128)S(1)}, f32[4,1,6,192]{3,2,1,0:T(8,128)S(1)}) fusion(f32[4,4,6,32]{3,2,1,0:T(8,128)S(1)} %reshape.97, f32[4,4,6,32]{3,2,1,0:T(8,128)S(1)} %reshape.96, f32[4,4,1,128]{3,2,1,0:T(1,128)S(1)} %bitcast.40, f32[4,4,1,128]{3,2,1,0:T(1,128)S(1)} %bitcast.37, f32[1,4,4,128]{3,2,1,0:T(4,128)} %bitcast.30, ...), kind=kLoop, calls=%fused_computation.6 | loop fusion | flops 46080 | bytes 110592 | tf_op jit(solution)/shard_map/concatenate | solution.py:294
  19.3 0.1 reshape.100
  19.4 0.1 reshape.98
  19.4 0.0 copy-start.1
  19.4 0.0 copy-start.5
  19.4 3.6 %collective-permute-start.4 = (f32[100,128]{1,0:T(8,128)S(1)}, f32[100,128]{1,0:T(8,128)S(1)}, u32[]{:S(2)}, u32[]{:S(2)}) collective-permute-start(f32[100,128]{1,0:T(8,128)S(1)} %maximum_select_fusion), channel_id=1, source_target_pairs={{0,16},{16,0},{1,17},{17,1},{2,18},{18,2},{3,19},{19,3},{4,20},{20... | collective-permute-start | bytes 153608 | tf_op jit(solution)/shard_map/ppermute | solution.py:231
  23.0 0.0 copy-start
  23.1 1.7 %copy-done = bf16[316,4096]{1,0:T(8,128)(2,1)S(1)} copy-done((bf16[316,4096]{1,0:T(8,128)(2,1)S(1)}, bf16[316,4096]{1,0:T(8,128)(2,1)}, u32[]{:S(2)}) %copy-start) | copy-done | bytes 2588696
  24.8 0.0 copy-start.4
  24.8 0.0 copy-start.2
  24.8 0.0 copy-start.3
  24.8 4.0 %table.1.w_ref = bf16[7,448,512]{2,1,0:T(8,128)(2,1)S(1)} custom-call(bf16[316,4096]{1,0:T(8,128)(2,1)S(1)} %copy-done), custom_call_target="tpu_custom_call" | custom-call | tf_op jit(solution)/shard_map/table/pallas_call | solution.py:263
  28.8 0.0 collective-permute-done.4
  28.9 0.6 %slice.122 = f32[36,128]{1,0:T(8,128)} slice(f32[100,128]{1,0:T(8,128)S(1)} %get-tuple-element.17), slice={[64:100], [0:128]} | slice | bytes 36864 | tf_op jit(solution)/shard_map/slice | solution.py:281
  29.5 0.6 %slice.120 = f32[64,128]{1,0:T(8,128)} slice(f32[100,128]{1,0:T(8,128)S(1)} %get-tuple-element.17), slice={[0:64], [0:128]} | slice | bytes 65536 | tf_op jit(solution)/shard_map/slice | solution.py:281
  30.1 0.6 %slice.123 = f32[36,128]{1,0:T(8,128)} slice(f32[100,128]{1,0:T(8,128)S(1)} %get-tuple-element.18), slice={[64:100], [0:128]} | slice | bytes 36864 | tf_op jit(solution)/shard_map/slice | solution.py:281
  30.7 0.6 %slice.121 = f32[64,128]{1,0:T(8,128)} slice(f32[100,128]{1,0:T(8,128)S(1)} %get-tuple-element.18), slice={[0:64], [0:128]} | slice | bytes 65536 | tf_op jit(solution)/shard_map/slice | solution.py:281
  31.3 0.8 %reshape.103 = f32[4,1,6,192]{3,2,0,1:T(8,128)S(1)} reshape(f32[36,128]{1,0:T(8,128)} %slice.122) | data formatting | bytes 36864 | tf_op jit(solution)/shard_map/reshape | solution.py:281
  32.1 1.4 %reshape.104 = f32[4,1,6,192]{3,2,0,1:T(8,128)} reshape(f32[36,128]{1,0:T(8,128)} %slice.123) | data formatting | bytes 36864 | tf_op jit(solution)/shard_map/reshape | solution.py:281
  33.5 0.0 copy-done.1
  33.5 0.0 copy-done.5
  33.5 0.9 %pad_maximum_fusion = f32[4,6,6,192]{3,2,1,0:T(8,128)S(1)} fusion(f32[4,1,6,192]{3,2,1,0:T(8,128)} %bitcast.43, f32[4,4,6,32]{3,2,1,0:T(8,128)S(1)} %reshape.97, f32[4,4,1,128]{3,2,1,0:T(1,128)S(1)} %bitcast.41, f32[1,4,4,128]{3,2,1,0:T(4,128)S(1)} %bitcast.31, f32[3,4,4,128]{3,2,1,0:T(4,128)S(1)} %copy-done.1, f32[4,4,1,128]{3,2,1,0:T(1,128)S(1)} %bitcast.38, ...), kind=kLoop, calls=%fused_computation | loop fusion | flops 193536 | bytes 221184 | tf_op jit(solution)/shard_map/concatenate | solution.py:299
  34.4 0.1 fusion.4
  34.6 0.0 copy-done.4
  34.6 0.8 %pad_maximum_fusion.2.u_ref = f32[8,4,8,128]{3,2,1,0:T(8,128)S(1)} fusion(f32[2,4,8,128]{3,2,1,0:T(8,128)} %bitcast.53, f32[4,4,2,128]{3,2,1,0:T(2,128)S(1)} %bitcast.35, f32[4,1,4,128]{3,2,1,0:T(4,128)S(1)} %bitcast.51, f32[4,2,4,128]{3,2,1,0:T(4,128)S(1)} %bitcast.25, f32[4,1,4,128]{3,2,1,0:T(4,128)S(1)} %bitcast.48, f32[4,4,2,128]{3,2,1,0:T(2,128)S(1)} %bitcast.33, ...), kind=kLoop, calls=%fused_computation.2 | loop fusion | flops 196608 | bytes 262144 | tf_op jit(solution)/shard_map/concatenate | solution.py:298
  35.5 0.0 copy-done.2
  35.5 0.0 copy-done.3
  35.5 7.6 %final.1 = f32[4,4,128]{2,1,0:T(4,128)} custom-call(f32[3,4,4,128]{3,2,1,0:T(4,128)S(1)} %copy-done.1, f32[8,4,8,128]{3,2,1,0:T(8,128)S(1)} %pad_maximum_fusion.2.u_ref, bf16[7,448,512]{2,1,0:T(8,128)(2,1)S(1)} %table.1.w_ref, f32[64,64]{1,0:T(8,128)S(1)} %copy-done.3, f32[64,128]{1,0:T(8,128)S(1)} %copy-done.2, f32[2,4,36,128]{3,2,1,0:T(8,128)S(1)} %pad_maximum_fusion.1.body_ref), custom_call_target="tpu_custom_call" | custom-call | tf_op jit(solution)/shard_map/final/pallas_call | solution.py:304
  (18 shorter events, 0.2 us)
Async XLA Ops:
  3.8 5.4 %collective-permute-start = (f32[32,128]{1,0:T(8,128)S(1)}, f32[32,128]{1,0:T(8,128)S(1)}, u32[]{:S(2)}, u32[]{:S(2)}) collective-permute-start(f32[32,128]{1,0:T(8,128)S(1)} %get-tuple-element.23), channel_id=1, source_target_pairs={{4,8},{8,4},{5,9},{9,5},{6,10},{10,6},{7,11},{11,7},{20,24},{24,20... | collective-permute-start | bytes 49160 | tf_op jit(solution)/shard_map/ppermute | solution.py:235
  7.0 2.7 %collective-permute-start.1 = (f32[32,128]{1,0:T(8,128)S(1)}, f32[32,128]{1,0:T(8,128)S(1)}, u32[]{:S(2)}, u32[]{:S(2)}) collective-permute-start(f32[32,128]{1,0:T(8,128)S(1)} %get-tuple-element.24), channel_id=1, source_target_pairs={{0,4},{4,0},{8,12},{12,8},{1,5},{5,1},{9,13},{13,9},{2,6},{6,2},{1... | collective-permute-start | bytes 49160 | tf_op jit(solution)/shard_map/ppermute | solution.py:231
  11.4 4.6 %collective-permute-start.2 = (f32[56,128]{1,0:T(8,128)S(1)}, f32[56,128]{1,0:T(8,128)S(1)}, u32[]{:S(2)}, u32[]{:S(2)}) collective-permute-start(f32[56,128]{1,0:T(8,128)S(1)} %get-tuple-element.15), channel_id=1, source_target_pairs={{1,2},{2,1},{5,6},{6,5},{9,10},{10,9},{13,14},{14,13},{17,18},{18,... | collective-permute-start | bytes 86024 | tf_op jit(solution)/shard_map/ppermute | solution.py:235
  14.6 2.8 %collective-permute-start.3 = (f32[56,128]{1,0:T(8,128)S(1)}, f32[56,128]{1,0:T(8,128)S(1)}, u32[]{:S(2)}, u32[]{:S(2)}) collective-permute-start(f32[56,128]{1,0:T(8,128)S(1)} %get-tuple-element.16), channel_id=1, source_target_pairs={{0,1},{1,0},{2,3},{3,2},{4,5},{5,4},{6,7},{7,6},{8,9},{9,8},{10,11... | collective-permute-start | bytes 86024 | tf_op jit(solution)/shard_map/ppermute | solution.py:231
  19.4 14.0 %copy-start.1 = (f32[3,4,4,128]{3,2,1,0:T(4,128)S(1)}, f32[3,4,4,128]{3,2,1,0:T(4,128)}, u32[]{:S(2)}) copy-start(f32[3,4,4,128]{3,2,1,0:T(4,128)} %offs_ref.3) | copy-start | bytes 73732
  19.4 14.0 %copy-start.5 = (f32[4,4,128]{2,1,0:T(4,128)S(1)}, f32[4,4,128]{2,1,0:T(4,128)}, u32[]{:S(2)}) copy-start(f32[4,4,128]{2,1,0:T(4,128)} %q_ref.1) | copy-start | bytes 24580
  19.4 9.4 %collective-permute-start.4 = (f32[100,128]{1,0:T(8,128)S(1)}, f32[100,128]{1,0:T(8,128)S(1)}, u32[]{:S(2)}, u32[]{:S(2)}) collective-permute-start(f32[100,128]{1,0:T(8,128)S(1)} %maximum_select_fusion), channel_id=1, source_target_pairs={{0,16},{16,0},{1,17},{17,1},{2,18},{18,2},{3,19},{19,3},{4,20},{20... | collective-permute-start | bytes 153608 | tf_op jit(solution)/shard_map/ppermute | solution.py:231
  23.0 1.7 %copy-start = (bf16[316,4096]{1,0:T(8,128)(2,1)S(1)}, bf16[316,4096]{1,0:T(8,128)(2,1)}, u32[]{:S(2)}) copy-start(bf16[316,4096]{1,0:T(8,128)(2,1)} %t_ref.1) | copy-start | bytes 7766020
  24.8 9.8 %copy-start.4 = (f32[32,128]{1,0:T(8,128)S(1)}, f32[32,128]{1,0:T(8,128)}, u32[]{:S(2)}) copy-start(f32[32,128]{1,0:T(8,128)} %upward.1) | copy-start | bytes 49156
  24.8 10.7 %copy-start.2 = (f32[64,128]{1,0:T(8,128)S(1)}, f32[64,128]{1,0:T(8,128)}, u32[]{:S(2)}) copy-start(f32[64,128]{1,0:T(8,128)} %constant.41.clone.sphere_ref) | copy-start | bytes 98308
  24.8 10.7 %copy-start.3 = (f32[64,64]{1,0:T(8,128)S(1)}, f32[64,64]{1,0:T(8,128)}, u32[]{:S(2)}) copy-start(f32[64,64]{1,0:T(8,128)} %dinv_ref.1) | copy-start | bytes 49156

commit v2 on v1

v2 whole, which is shorter than its diff:
```python
import functools
import math

import jax
import jax.numpy as jnp
import numpy as np
from jax import lax
from jax.experimental import pallas as pl
from jax.experimental.pallas import tpu as pltpu
from jax.sharding import PartitionSpec as P

BODIES = 32
RADIUS = 0.9
REACH = 3
SPAN = 2 * REACH + 1
F32 = jnp.float32
BF16 = jnp.bfloat16
NT = (((1,), (1,)), ((), ()))


def surface(points):
    number = np.arange(points).astype(np.float32)
    height = np.float32(1.0) - (np.float32(2.0) * number + np.float32(1.0)) / np.float32(points)
    across = np.sqrt(np.float32(1.0) - height * height)
    turned = number * np.float32(math.pi * (3.0 - math.sqrt(5.0)))
    columns = np.zeros((points, 128), np.float32)
    columns[:, 0] = RADIUS * across * np.cos(turned)
    columns[:, 1] = RADIUS * across * np.sin(turned)
    columns[:, 2] = RADIUS * height
    return columns


def numbering():
    table, count = {}, 0
    for ox in range(-REACH, REACH + 1):
        for oy in range(-REACH, REACH + 1):
            for oz in range(-REACH, REACH + 1):
                if max(abs(ox), abs(oy), abs(oz)) >= 2:
                    table[ox, oy, oz] = count
                    count += 1
    return table


def split(value):
    high = value.astype(BF16)
    return high, (value - high.astype(F32)).astype(BF16)


def surface_green(sphere, offs_ref, x, y):
    rows = [offs_ref[c, x, pl.ds(y, 1), :] - 0.5 for c in range(3)]
    square = None
    for c in range(3):
        delta = sphere[:, c : c + 1] - rows[c]
        square = delta * delta if square is None else square + delta * delta
    return lax.rsqrt(square)


def select(even, one, two):
    return jnp.where(even, one, two), jnp.where(even, two, one)


def put(refs, at, even, low, high):
    refs[0][at, :] = jnp.where(even, high, low)
    for ref in refs[1:]:
        ref[at, :] = jnp.where(even, low, high)


def get(refs, even):
    one = refs[0][...]
    return select(even, one, refs[1][...] if len(refs) > 1 else jnp.zeros_like(one))


def upward_kernel(offs_hbm, q_hbm, sphere_hbm, uinv_hbm, u_ref, *rest):
    *packets, offs_ref, q_ref, sphere_ref, uinv_ref, check_ref, wide_ref, sems = rest
    copies = [
        pltpu.make_async_copy(source, target, sems.at[n])
        for n, (source, target) in enumerate(
            ((offs_hbm, offs_ref), (q_hbm, q_ref), (sphere_hbm, sphere_ref), (uinv_hbm, uinv_ref))
        )
    ]
    for copy in copies:
        copy.start()
    _, lx, ly, lanes = offs_ref.shape
    lz = lanes // BODIES
    half = ly // 2
    points = uinv_ref.shape[0]
    even = lax.axis_index("gy") % 2 == 0
    segment = (
        lax.broadcasted_iota(jnp.int32, (8, lanes), 1) // BODIES
        == lax.broadcasted_iota(jnp.int32, (8, lanes), 0)
    ).astype(BF16)
    wide_ref[...] = jnp.zeros_like(wide_ref)
    column = lax.broadcasted_iota(jnp.int32, (2 * points, 2 * points), 1)
    within = column % points
    wanted = column - within + jnp.where(within < points // 2, 2 * within, 2 * within - points + 1)
    shuffle = (lax.broadcasted_iota(jnp.int32, (2 * points, 2 * points), 0) == wanted).astype(BF16)
    for copy in copies[:3]:
        copy.wait()
    sphere = sphere_ref[...]
    for c in range(4):
        for x in range(lx):
            low, high = [
                offs_ref[c, x, pl.ds(y, 1), :] if c < 3 else q_ref[x, pl.ds(y, 1), :] for y in (0, ly - 1)
            ]
            put(packets, pl.ds(lx * lz + c * lx + x, 1), even, low, high)
    for x in range(lx):
        for pair in range(half):
            parts = [
                surface_green(sphere, offs_ref, x, 2 * pair + par) * q_ref[x, pl.ds(2 * pair + par, 1), :]
                for par in range(2)
            ]
            high, low = split(jnp.concatenate(parts, axis=0))
            sums = lax.dot_general(segment, high, NT, preferred_element_type=F32)
            sums = sums + lax.dot_general(segment, low, NT, preferred_element_type=F32)
            check_ref[pl.ds((x * half + pair) * lz, lz), :] = sums[:lz]
    copies[3].wait()
    wide_ref[:points, :points] = uinv_ref[...]
    wide_ref[points:, points:] = uinv_ref[...]
    density = jnp.dot(
        check_ref[...], wide_ref[...], precision=lax.Precision.HIGHEST, preferred_element_type=F32
    ).astype(BF16)
    u_ref[...] = jnp.dot(density, shuffle, preferred_element_type=F32)
    for x in range(lx):
        low = u_ref[pl.ds(x * half * lz, lz), :]
        high = u_ref[pl.ds((x * half + half - 1) * lz, lz), :]
        put(packets, pl.ds(x * lz, lz), even, low, high)


def table_kernel(t_ref, after_ref, w_ref, rows_ref):
    count, width = t_ref.shape
    groups = width // 128
    stride = rows_ref.shape[0] // groups
    points = math.isqrt(width)
    half = points // 2
    order = numbering()
    for a in range(groups):
        rows_ref[pl.ds(a * stride, count), :] = t_ref[:, a * 128 : (a + 1) * 128].astype(F32)
    left = lax.broadcasted_iota(jnp.int32, (groups, 128), 1) < points
    zero = jnp.zeros((groups, 128), F32)
    for ox in range(SPAN):
        for oy in range(SPAN):
            for k in range((SPAN + 1) // 2):
                loaded = []
                for oz in (2 * k, 2 * k + 1):
                    at = order.get((ox - REACH, oy - REACH, oz - REACH))
                    loaded.append(zero if at is None else rows_ref[pl.ds(at, groups, stride=stride), :])
                one, two = loaded
                even = jnp.where(left, one, pltpu.roll(two, points, 1))
                odd = jnp.where(left, pltpu.roll(one, points, 1), two)
                at = slice(k * 128, (k + 1) * 128)
                w_ref[ox, pl.ds(oy * points, half), at] = even.astype(BF16)
                w_ref[ox, pl.ds(oy * points + half, half), at] = odd.astype(BF16)


def zpack_kernel(count, offs_ref, q_ref, u_ref, *rest):
    received, (d_ref, r_ref, *packets) = rest[:count], rest[count:]
    _, lx, ly, lanes = offs_ref.shape
    lz = lanes // BODIES
    half = ly // 2
    wide = ly + 2
    above, below = get(received, lax.axis_index("gy") % 2 == 0)
    even = lax.axis_index("gz") % 2 == 0
    for x in range(lx):
        at = x * (half + 2) * lz
        d_ref[pl.ds(at, lz), :] = below[x * lz : (x + 1) * lz]
        d_ref[pl.ds(at + lz, half * lz), :] = u_ref[pl.ds(x * half * lz, half * lz), :]
        d_ref[pl.ds(at + (half + 1) * lz, lz), :] = above[x * lz : (x + 1) * lz]
        for c in range(4):
            row = lx * lz + c * lx + x
            r_ref[c, pl.ds(x * wide, 1), :] = below[row : row + 1]
            r_ref[c, pl.ds(x * wide + 1, ly), :] = offs_ref[c, x] if c < 3 else q_ref[x]
            r_ref[c, pl.ds(x * wide + ly + 1, 1), :] = above[row : row + 1]
    for g in range(lx * (half + 2)):
        put(packets, pl.ds(g * 2, 2), even, d_ref[pl.ds(g * lz, 2), :], d_ref[pl.ds(g * lz + lz - 2, 2), :])
    spot = lax.broadcasted_iota(jnp.int32, (lx, lanes), 1) // BODIES
    base = lx * (half + 2) * 2
    for c in range(4):
        rows = [r_ref[c, pl.ds(j, lx, stride=wide), :] for j in range(wide)]
        for pack in range(half):
            low = high = None
            for j in range(4):
                row = rows[2 * pack + j]
                first = pltpu.roll(row, j * BODIES, 1) if j else row
                last = pltpu.roll(row, (j + 1) % 4 * BODIES, 1) if (j + 1) % 4 else row
                low = first if low is None else jnp.where(spot == j, first, low)
                high = last if high is None else jnp.where(spot == j, last, high)
            put(packets, pl.ds(base + (c * half + pack) * lx, lx), even, low, high)


def xpack_kernel(count, d_ref, r_ref, *rest):
    received, (e_ref, zl_ref, zh_ref, *packets) = rest[:count], rest[count:]
    groups = e_ref.shape[0]
    lx = zl_ref.shape[1] // 2
    pairs = groups // lx
    half = pairs - 2
    wide = 2 * half + 2
    lz = d_ref.shape[0] // groups
    above, below = get(received, lax.axis_index("gz") % 2 == 0)
    even = lax.axis_index("gx") % 2 == 0
    for g in range(groups):
        e_ref[g, pl.ds(0, 2), :] = below[g * 2 : g * 2 + 2]
        e_ref[g, pl.ds(2, lz), :] = d_ref[pl.ds(g * lz, lz), :]
        e_ref[g, pl.ds(2 + lz, 2), :] = above[g * 2 : g * 2 + 2]
    base = groups * 2
    for c in range(4):
        zl_ref[c] = below[base + c * half * lx : base + (c + 1) * half * lx]
        zh_ref[c] = above[base + c * half * lx : base + (c + 1) * half * lx]
    deep = lz + 4
    for n in range(2 * pairs):
        put(packets, pl.ds(n * deep, deep), even, e_ref[n], e_ref[groups - 2 * pairs + n])
    base = 2 * pairs * deep
    for c in range(4):
        low, high = r_ref[c, pl.ds(0, wide), :], r_ref[c, pl.ds((lx - 1) * wide, wide), :]
        put(packets, pl.ds(base + c * wide, wide), even, low, high)
    base = base + 4 * wide
    for end, ref in enumerate((zl_ref, zh_ref)):
        for c in range(4):
            for pack in range(half):
                low, high = ref[c, pl.ds(pack * lx, 1), :], ref[c, pl.ds(pack * lx + lx - 1, 1), :]
                put(packets, pl.ds(base + (end * 4 + c) * half + pack, 1), even, low, high)


def turn(offs_ref, x):
    _, _, ly, lanes = offs_ref.shape
    lead = lax.broadcasted_iota(jnp.int32, (ly, lanes), 0).astype(F32)
    spots = (lax.broadcasted_iota(jnp.int32, (ly, lanes), 1) // BODIES).astype(F32)
    places = [offs_ref[0, x] + float(x), offs_ref[1, x] + lead, offs_ref[2, x] + spots]
    return jnp.concatenate(places + [places[0]], axis=0).T


def pick(turned, ly, y, z):
    return [turned[z * BODIES : (z + 1) * BODIES, c * ly + y : c * ly + y + 1] for c in range(3)]


def attract(total, target, source, weight, own=False):
    square = None
    for t, s in zip(target, source):
        delta = t - s
        square = delta * delta if square is None else square + delta * delta
    inverse = lax.rsqrt(square)
    if own:
        inverse = jnp.where(square > 0.0, inverse, 0.0)
    term = inverse * weight
    return term if total is None else total + term


def lane_sum(ones, parts):
    high, low = split(jnp.concatenate(parts, axis=0))
    out = lax.dot_general(ones, high, NT, preferred_element_type=F32)
    return (out + lax.dot_general(ones, low, NT, preferred_element_type=F32))[:1]


def spans(value, spot, lz):
    return [jnp.where((spot >= z - 1) & (spot <= z + 1), value, 0.0) for z in range(lz)]


def gather(out_ref, n, y, turned, lz, rows):
    _, ly, lanes = out_ref.shape
    ones = jnp.ones((8, lanes), BF16)
    parts = []
    for z in range(lz):
        target = pick(turned, ly, y, z)
        total = None
        for source, weight, own in rows(z):
            total = attract(total, target, source, weight, own)
        parts.append(jnp.zeros((BODIES, lanes), F32) if total is None else total)
    out_ref[n, pl.ds(y, 1), :] = lane_sum(ones, parts)


def row_source(ref, at, z, own=False):
    return [ref[c, at, :] for c in range(3)], ref[3 + z, at, :], own


def edge_kernel(offs_ref, q_ref, out_ref, win_ref):
    _, lx, ly, lanes = offs_ref.shape
    lz = lanes // BODIES
    spot = lax.broadcasted_iota(jnp.int32, (ly, lanes), 1) // BODIES
    lead = lax.broadcasted_iota(jnp.int32, (ly, lanes), 0)
    for x in range(lx):
        at = pl.ds(x * ly, ly)
        shift = [float(x), lead.astype(F32), spot.astype(F32)]
        for c in range(3):
            win_ref[c, at, :] = offs_ref[c, x] + shift[c]
        for z, value in enumerate(spans(q_ref[x], spot, lz)):
            win_ref[3 + z, at, :] = value
    for n, x in enumerate((0, lx - 1)):
        turned = turn(offs_ref, x)
        for y in range(ly):

            def rows(z):
                for xx in range(max(x - 1, 0), min(x + 2, lx)):
                    for yy in range(max(y - 1, 0), min(y + 2, ly)):
                        yield row_source(win_ref, pl.ds(xx * ly + yy, 1), z, xx == x and yy == y)

            gather(out_ref, n, y, turned, lz, rows)


def strips(r_ref, win_ref, wide, lz):
    _, rows, lanes = r_ref.shape
    place = lax.broadcasted_iota(jnp.int32, (rows, lanes), 0)
    spot = lax.broadcasted_iota(jnp.int32, (rows, lanes), 1) // BODIES
    base = [place // wide, place % wide - 1, spot]
    for c in range(3):
        win_ref[c] = r_ref[c] + base[c].astype(F32)
    for z, value in enumerate(spans(r_ref[3], spot, lz)):
        win_ref[3 + z] = value


def inner_kernel(offs_ref, r_ref, out_ref, win_ref):
    _, lx, ly, lanes = offs_ref.shape
    lz = lanes // BODIES
    wide = ly + 2
    strips(r_ref, win_ref, wide, lz)
    for x in range(1, lx - 1):
        turned = turn(offs_ref, x)
        for y in range(ly):

            def rows(z):
                for xx in range(x - 1, x + 2):
                    for dy in range(3):
                        yield row_source(win_ref, pl.ds(xx * wide + y + dy, 1), z, xx == x and dy == 1)

            gather(out_ref, x - 1, y, turned, lz, rows)


def ends_kernel(offs_ref, r_ref, zl_ref, zh_ref, out_ref, win_ref, end_ref):
    _, lx, ly, lanes = offs_ref.shape
    lz = lanes // BODIES
    half = ly // 2
    wide = ly + 2
    strips(r_ref, win_ref, wide, lz)
    end_windows(zl_ref, -1.0, end_ref, 0, lz, half)
    end_windows(zh_ref, float(lz), end_ref, 5, lz, half)
    for x in range(lx):
        turned = turn(offs_ref, x)
        for y in range(ly):

            def rows(z):
                nearby = range(max(x - 1, 0), min(x + 2, lx))
                if x in (0, lx - 1):
                    for yy in (y, y + 2):
                        if yy in (0, ly + 1):
                            for xx in nearby:
                                yield row_source(win_ref, pl.ds(xx * wide + yy, 1), z)
                for end in range(2):
                    if z == (0 if end == 0 else lz - 1):
                        for xx in nearby:
                            at = pl.ds(y // 2 * lx + xx, 1)
                            source = [end_ref[end * 5 + c, at, :] for c in range(3)]
                            yield source, end_ref[end * 5 + 3 + y % 2, at, :], False

            gather(out_ref, x, y, turned, lz, rows)


def end_windows(end_ref, base, win_ref, at, lz, half):
    rows = end_ref.shape[1]
    lanes = end_ref.shape[2]
    count = rows // half
    place = lax.broadcasted_iota(jnp.int32, (rows, lanes), 0)
    spot = lax.broadcasted_iota(jnp.int32, (rows, lanes), 1) // BODIES
    shift = [(place % count).astype(F32), (spot + 2 * (place // count) - 1).astype(F32), base]
    for c in range(3):
        win_ref[at + c] = end_ref[c] + shift[c]
    for s in range(2):
        win_ref[at + 3 + s] = jnp.where((spot >= s) & (spot < s + 3), end_ref[3], 0.0)


def final_kernel(count, offs_ref, e_ref, near_edge_ref, near_in_ref, near_end_ref, w_ref, dinv_ref, sphere_ref, *rest):
    received, rest = rest[:count], rest[count:]
    out_ref, left_ref, acc_ref, dense_ref, sum_ref, side_ref, edge_ref = rest
    _, lx, ly, lanes = offs_ref.shape
    lz = lanes // BODIES
    points = dinv_ref.shape[0]
    half = ly // 2
    pairs = half + 2
    wide = ly + 2
    deep = lz + 4
    block = half * deep
    width = (SPAN - 1) * points
    above, below = get(received, lax.axis_index("gx") % 2 == 0)

    def plane(x, pair):
        if x < 2:
            return below[(x * pairs + pair) * deep : (x * pairs + pair + 1) * deep]
        if x < lx + 2:
            return e_ref[(x - 2) * pairs + pair]
        return above[((x - lx - 2) * pairs + pair) * deep : ((x - lx - 2) * pairs + pair + 1) * deep]

    for x in range(lx + 4):
        planes = [plane(x, pair) for pair in range(pairs)]
        for j in range(SPAN // 2):
            left_ref[pl.ds(x * block, block), j * 128 : (j + 1) * 128] = jnp.concatenate(
                planes[j : j + half], axis=0
            ).astype(BF16)
    twice = jnp.concatenate([dinv_ref[...]] * 2, axis=0)
    expand = (
        lax.broadcasted_iota(jnp.int32, (lx * half * lz, lx * half * lanes), 1) // BODIES
        == lax.broadcasted_iota(jnp.int32, (lx * half * lz, lx * half * lanes), 0)
    ).astype(BF16)
    lane = lax.broadcasted_iota(jnp.int32, (lz, 128), 1)
    level = lax.broadcasted_iota(jnp.int32, (lz, 128), 0)
    for cy in range(2):
        total = [None] * lx
        for ox in range(-REACH, REACH + 1):
            chosen = [b for b in range(lx) if not (ox == -REACH and b % 2 == 0) and not (ox == REACH and b % 2 == 1)]
            parts = [left_ref[pl.ds((b + ox + 2) * block, block), :] for b in chosen]
            lhs = jnp.concatenate(parts, axis=0)
            rhs = w_ref[ox + REACH, pl.ds((1 - cy) * points, width), :]
            got = jnp.dot(lhs, rhs, preferred_element_type=F32)
            for n, b in enumerate(chosen):
                piece = got[n * block : (n + 1) * block]
                total[b] = piece if total[b] is None else total[b] + piece
        for b in range(lx):
            for p in range(half):
                acc_ref[b * half + p, pl.ds(8, deep), :] = total[b][p * deep : (p + 1) * deep]
        for g in range(lx * half):
            folded = None
            for k in range((SPAN + 1) // 2):
                shown = []
                for oz in (2 * k - REACH, 2 * k + 1 - REACH):
                    if oz > REACH:
                        shown.append(jnp.zeros((lz, 128), F32))
                        continue
                    got = acc_ref[g, pl.ds(8 + oz + 2, lz), k * 128 : (k + 1) * 128]
                    if oz == -REACH:
                        got = jnp.where(level % 2 == 1, got, 0.0)
                    if oz == REACH:
                        got = jnp.where(level % 2 == 0, got, 0.0)
                    shown.append(got)
                both = jnp.where(lane < points, shown[0], shown[1])
                folded = both if folded is None else folded + both
            sum_ref[pl.ds(g * lz, lz), :] = folded
        dense = jnp.dot(sum_ref[...], twice, precision=lax.Precision.HIGHEST, preferred_element_type=F32)
        high, low = split(dense.T)
        spread = jnp.dot(high, expand, preferred_element_type=F32)
        spread = spread + jnp.dot(low, expand, preferred_element_type=F32)
        for g in range(lx * half):
            dense_ref[g, cy] = spread[:, g * lanes : (g + 1) * lanes]

    spot = lax.broadcasted_iota(jnp.int32, (wide, lanes), 1) // BODIES
    lead = lax.broadcasted_iota(jnp.int32, (wide, lanes), 0).astype(F32) - 1.0
    base = 2 * pairs * deep
    ends = base + 4 * wide
    for side, value in enumerate((below, above)):
        shift = [-1.0 if side == 0 else float(lx), lead, spot.astype(F32)]
        for c in range(3):
            side_ref[side, c] = value[base + c * wide : base + (c + 1) * wide] + shift[c]
        for z, part in enumerate(spans(value[base + 3 * wide : base + 4 * wide], spot, lz)):
            side_ref[side, 3 + z] = part
    spot = lax.broadcasted_iota(jnp.int32, (half, lanes), 1) // BODIES
    place = lax.broadcasted_iota(jnp.int32, (half, lanes), 0)
    for side, value in enumerate((below, above)):
        for end in range(2):
            shift = [-1.0 if side == 0 else float(lx), (spot + 2 * place - 1).astype(F32), -1.0 if end == 0 else float(lz)]
            for c in range(3):
                at = ends + (end * 4 + c) * half
                edge_ref[side, end * 5 + c] = value[at : at + half] + shift[c]
            at = ends + (end * 4 + 3) * half
            for s in range(2):
                edge_ref[side, end * 5 + 3 + s] = jnp.where((spot >= s) & (spot < s + 3), value[at : at + half], 0.0)

    sphere = sphere_ref[...]
    for x in range(lx):
        turned = turn(offs_ref, x) if x in (0, lx - 1) else None
        for y in range(ly):

            def rows(z):
                for side in range(2):
                    if x == (0 if side == 0 else lx - 1):
                        for dy in range(3):
                            at = pl.ds(y + dy, 1)
                            yield [side_ref[side, c, at, :] for c in range(3)], side_ref[side, 3 + z, at, :], False
                        for end in range(2):
                            if z == (0 if end == 0 else lz - 1):
                                at = pl.ds(y // 2, 1)
                                source = [edge_ref[side, end * 5 + c, at, :] for c in range(3)]
                                yield source, edge_ref[side, end * 5 + 3 + y % 2, at, :], False

            kernel = surface_green(sphere, offs_ref, x, y)
            far = jnp.sum(kernel * dense_ref[x * half + y // 2, y % 2], axis=0, keepdims=True)
            at = pl.ds(y, 1)
            total = near_end_ref[x, at, :] + far
            if x in (0, lx - 1):
                gather(out_ref, x, y, turned, lz, rows)
                total = total + out_ref[x, at, :] + near_edge_ref[0 if x == 0 else 1, at, :]
            else:
                total = total + near_in_ref[x - 1, at, :]
            out_ref[x, at, :] = total


def partners(axis):
    count = lax.axis_size(axis)
    rounds = [[(i, i + 1) for i in range(start, count - 1, 2)] for start in range(2)]
    return [[pair for i, j in pairs for pair in ((i, j), (j, i))] for pairs in rounds if pairs] or [[]]


def exchange(packets, axis):
    return [lax.ppermute(packet, axis, pairs) for packet, pairs in zip(packets, partners(axis))]


def call(kernel, outs, args, scratch=(), limit=8, name=None, spaces=None):
    spec = pl.BlockSpec(memory_space=pltpu.VMEM)
    return pl.pallas_call(
        kernel,
        out_shape=outs,
        in_specs=[pl.BlockSpec(memory_space=space) for space in spaces] if spaces else [spec] * len(args),
        out_specs=[spec] * len(outs),
        scratch_shapes=list(scratch),
        compiler_params=pltpu.CompilerParams(vmem_limit_bytes=limit << 20),
        name=name,
    )(*args)


def shaped(*shape):
    return jax.ShapeDtypeStruct(shape, F32)


def per_device(offsets, charges, up_inverse, translations, down_inverse):
    points = up_inverse.shape[0]
    _, lx, ly, lanes = offsets.shape
    lz = lanes // BODIES
    half = ly // 2
    pairs = half + 2
    wide = ly + 2
    deep = lz + 4
    rounds = {axis: len(partners(axis)) for axis in ("gx", "gy", "gz")}
    sphere = jnp.asarray(surface(points))
    boxes = lx * half * lz
    packet = shaped(lx * lz + 4 * lx, lanes)
    density, *packets = call(
        upward_kernel,
        [shaped(boxes, 2 * points)] + [packet] * rounds["gy"],
        (offsets, charges, sphere, up_inverse),
        [
            pltpu.VMEM(offsets.shape, F32),
            pltpu.VMEM(charges.shape, F32),
            pltpu.VMEM(sphere.shape, F32),
            pltpu.VMEM(up_inverse.shape, F32),
            pltpu.VMEM((boxes, 2 * points), F32),
            pltpu.VMEM((2 * points, 2 * points), F32),
            pltpu.SemaphoreType.DMA((4,)),
        ],
        4,
        "upward",
        [pltpu.HBM] * 4,
    )
    received = exchange(packets, "gy")
    count, width = translations.shape
    stride = count // 2 * 2 + 1
    (weights,) = call(
        table_kernel,
        [jax.ShapeDtypeStruct((SPAN, SPAN * points, (SPAN + 1) * points), BF16)],
        (translations, density),
        [pltpu.VMEM((width // 128 * stride, 128), F32)],
        16,
        "table",
        [pltpu.VMEM, pl.ANY],
    )
    first = lax.optimization_barrier((offsets, charges, weights))
    (edge,) = call(
        edge_kernel,
        [shaped(2, ly, lanes)],
        first[:2],
        [pltpu.VMEM((3 + lz, lx * ly, lanes), F32)],
        name="near_edge",
    )
    weights = first[2]
    received, edge, weights = lax.optimization_barrier((received, edge, weights))
    packet = shaped(lx * pairs * 2 + 4 * half * lx, lanes)
    dense, body, *packets = call(
        functools.partial(zpack_kernel, len(received)),
        [shaped(lx * pairs * lz, 2 * points), shaped(4, lx * wide, lanes)] + [packet] * rounds["gz"],
        (offsets, charges, density, *received),
        name="zpack",
    )
    packets, body = lax.optimization_barrier((packets, body))
    received = exchange(packets, "gz")
    windows = [pltpu.VMEM((3 + lz, lx * wide, lanes), F32)]
    (inner,) = call(inner_kernel, [shaped(lx - 2, ly, lanes)], (offsets, body), windows, name="near_inner")
    received, inner = lax.optimization_barrier((received, inner))
    packet = shaped(2 * pairs * deep + 4 * wide + 8 * half, lanes)
    end = shaped(4, half * lx, lanes)
    dense, low, high, *packets = call(
        functools.partial(xpack_kernel, len(received)),
        [shaped(lx * pairs, deep, 2 * points), end, end] + [packet] * rounds["gx"],
        (dense, body, *received),
        name="xpack",
    )
    packets, body = lax.optimization_barrier((packets, body))
    received = exchange(packets, "gx")
    (ends,) = call(
        ends_kernel,
        [shaped(lx, ly, lanes)],
        (offsets, body, low, high),
        windows + [pltpu.VMEM((10, half * lx, lanes), F32)],
        name="near_ends",
    )
    received, ends = lax.optimization_barrier((received, ends))
    (out,) = call(
        functools.partial(final_kernel, len(received)),
        [shaped(lx, ly, lanes)],
        (offsets, dense, edge, inner, ends, weights, down_inverse, sphere, *received),
        [
            pltpu.VMEM(((lx + 4) * half * deep, 6 * points), BF16),
            pltpu.VMEM((lx * half, 8 + deep + 8, (SPAN + 1) * points), F32),
            pltpu.VMEM((lx * half, 2, points, lanes), F32),
            pltpu.VMEM((boxes, 2 * points), F32),
            pltpu.VMEM((2, 3 + lz, wide, lanes), F32),
            pltpu.VMEM((2, 10, half, lanes), F32),
        ],
        24,
        "final",
    )
    return out


def solution(mesh):
    in_specs = (P(None, "gx", "gy", "gz"), P("gx", "gy", "gz"), P(), P(), P())
    out_specs = P("gx", "gy", "gz")
    return jax.shard_map(
        per_device, mesh=mesh, in_specs=in_specs, out_specs=out_specs, check_vma=False
    )
```

time: 43.9 us -> 26.3 us (0.60)
  the two profiles are of different devices: /device:TPU:11 before, /device:TPU:19 now
where the time goes in v2:
time: 26.3 us; the launch traced here: 25.9 us
  starting transfers between devices  10.4 us (40%)
  Pallas kernels  10.1 us (38%)
  local copies, waits for them, and re-layouts  4.71 us (18%)
  waiting for transfers between devices  0.59 us (2%)
    ppermute x5, starting transfers between devices, exchange(): lax.ppermute(packet, axis, pairs)  10.4 us
    pallas_call x8, Pallas kernels, call(): pl.pallas_call(kernel, out_shape=outs, in_specs=[pl.BlockSpec(memory_spac...  10.1 us
    unnamed x18, local copies, waits for them, and re-layouts  4.71 us
    ppermute x5, waiting for transfers between devices, exchange(): lax.ppermute(packet, axis, pairs)  0.59 us
  transfers between devices with their start and end apart: 5, of which 1 were waited for; matrix products, arithmetic and copies ran while one was open for 0% of the time, Pallas kernels for 22%

profile of v2, /device:TPU:19, one launch (start us, length us, event | category | flops | bytes accessed | tf_op | source)
XLA Modules:
  0.0 25.9 jit_solution(5700213281389605423)
XLA Ops:
  0.0 0.0 copy-start.1
  0.0 0.7 %copy-done.1 = f32[3,4,4,128]{3,2,1,0:T(4,128)S(1)} copy-done((f32[3,4,4,128]{3,2,1,0:T(4,128)S(1)}, f32[3,4,4,128]{3,2,1,0:T(4,128)}, u32[]{:S(2)}) %copy-start.1) | copy-done | bytes 24600
  0.7 0.0 copy-start.3
  0.7 0.8 %copy-done.3 = f32[64,128]{1,0:T(8,128)S(1)} copy-done((f32[64,128]{1,0:T(8,128)S(1)}, f32[64,128]{1,0:T(8,128)}, u32[]{:S(2)}) %copy-start.3) | copy-done | bytes 32792
  1.5 0.0 copy-start.5
  1.5 0.7 %copy-done.5 = f32[4,4,128]{2,1,0:T(4,128)S(1)} copy-done((f32[4,4,128]{2,1,0:T(4,128)S(1)}, f32[4,4,128]{2,1,0:T(4,128)}, u32[]{:S(2)}) %copy-start.5) | copy-done | bytes 8216
  2.2 0.0 copy-start.8
  2.2 0.8 %copy-done.8 = f32[64,64]{1,0:T(8,128)S(1)} copy-done((f32[64,64]{1,0:T(8,128)S(1)}, f32[64,64]{1,0:T(8,128)}, u32[]{:S(2)}) %copy-start.8) | copy-done | bytes 16408
  3.0 0.0 copy-start.2
  3.0 0.0 copy-start.6
  3.0 0.0 copy-start.4
  3.0 0.0 copy-start.7
  3.0 1.1 %upward.1 = (f32[32,128]{1,0:T(8,128)S(1)}, f32[32,128]{1,0:T(8,128)S(1)}, f32[32,128]{1,0:T(8,128)S(1)}) custom-call(f32[3,4,4,128]{3,2,1,0:T(4,128)S(1)} %copy-done.1, f32[4,4,128]{2,1,0:T(4,128)S(1)} %copy-done.5, f32[64,128]{1,0:T(8,128)S(1)} %copy-done.3, f32[64,64]{1,0:T(8,128)S(1)} %copy-done.8), custom_call_target="tpu_custom_call" | custom-call | tf_op jit(solution)/shard_map/upward/pallas_call | solution.py:503
  4.1 0.3 %collective-permute-start = (f32[32,128]{1,0:T(8,128)S(1)}, f32[32,128]{1,0:T(8,128)S(1)}, u32[]{:S(2)}, u32[]{:S(2)}) collective-permute-start(f32[32,128]{1,0:T(8,128)S(1)} %get-tuple-element.34), channel_id=1, source_target_pairs={{0,4},{4,0},{8,12},{12,8},{1,5},{5,1},{9,13},{13,9},{2,6},{6,2},{1... | collective-permute-start | bytes 49160 | tf_op jit(solution)/shard_map/ppermute | solution.py:498
  4.4 4.1 %collective-permute-start.1 = (f32[32,128]{1,0:T(8,128)S(1)}, f32[32,128]{1,0:T(8,128)S(1)}, u32[]{:S(2)}, u32[]{:S(2)}) collective-permute-start(f32[32,128]{1,0:T(8,128)S(1)} %get-tuple-element.35), channel_id=1, source_target_pairs={{4,8},{8,4},{5,9},{9,5},{6,10},{10,6},{7,11},{11,7},{20,24},{24,20... | collective-permute-start | bytes 49160 | tf_op jit(solution)/shard_map/ppermute | solution.py:498
  8.5 0.0 copy-start
  8.5 1.7 %copy-done = bf16[316,4096]{1,0:T(8,128)(2,1)S(1)} copy-done((bf16[316,4096]{1,0:T(8,128)(2,1)S(1)}, bf16[316,4096]{1,0:T(8,128)(2,1)}, u32[]{:S(2)}) %copy-start) | copy-done | bytes 2588696
  10.2 1.1 %table.1.w_ref = bf16[7,448,512]{2,1,0:T(8,128)(2,1)S(1)} custom-call(bf16[316,4096]{1,0:T(8,128)(2,1)S(1)} %copy-done, f32[32,128]{1,0:T(8,128)S(1)} %get-tuple-element.33.after_ref.u_ref), custom_call_target="tpu_custom_call" | custom-call | tf_op jit(solution)/shard_map/table/pallas_call | solution.py:503
  11.4 0.0 copy-done.2
  11.4 0.0 copy-done.6
  11.4 1.4 %near_edge.1.near_edge_ref = f32[2,4,128]{2,1,0:T(4,128)S(1)} custom-call(f32[3,4,4,128]{3,2,1,0:T(4,128)S(1)} %copy-done.2, f32[4,4,128]{2,1,0:T(4,128)S(1)} %copy-done.6), custom_call_target="tpu_custom_call" | custom-call | tf_op jit(solution)/shard_map/near_edge/pallas_call | solution.py:503
  12.7 0.0 collective-permute-done.rest_0_
  12.7 0.0 collective-permute-done.1.rest_1_
  12.8 0.1 zpack.1
  12.9 1.4 %collective-permute-start.2 = (f32[64,128]{1,0:T(8,128)S(1)}, f32[64,128]{1,0:T(8,128)S(1)}, u32[]{:S(2)}, u32[]{:S(2)}) collective-permute-start(f32[64,128]{1,0:T(8,128)S(1)} %get-tuple-element.46), channel_id=1, source_target_pairs={{0,1},{1,0},{2,3},{3,2},{4,5},{5,4},{6,7},{7,6},{8,9},{9,8},{10,11... | collective-permute-start | bytes 98312 | tf_op jit(solution)/shard_map/ppermute | solution.py:498
  14.3 1.9 %collective-permute-start.3 = (f32[64,128]{1,0:T(8,128)S(1)}, f32[64,128]{1,0:T(8,128)S(1)}, u32[]{:S(2)}, u32[]{:S(2)}) collective-permute-start(f32[64,128]{1,0:T(8,128)S(1)} %get-tuple-element.47), channel_id=1, source_target_pairs={{1,2},{2,1},{5,6},{6,5},{9,10},{10,9},{13,14},{14,13},{17,18},{18,... | collective-permute-start | bytes 98312 | tf_op jit(solution)/shard_map/ppermute | solution.py:498
  16.2 2.2 %near_inner.1.near_in_ref = f32[2,4,128]{2,1,0:T(4,128)S(1)} custom-call(f32[3,4,4,128]{3,2,1,0:T(4,128)S(1)} %copy-done.2, f32[4,24,128]{2,1,0:T(8,128)S(1)} %get-tuple-element.55.r_ref), custom_call_target="tpu_custom_call" | custom-call | tf_op jit(solution)/shard_map/near_inner/pallas_call | solution.py:503
  18.4 0.0 collective-permute-done.2.rest_0_
  18.4 0.6 %collective-permute-done.3.rest_1_ = f32[64,128]{1,0:T(8,128)S(1)} collective-permute-done((f32[64,128]{1,0:T(8,128)S(1)}, f32[64,128]{1,0:T(8,128)S(1)}, u32[]{:S(2)}, u32[]{:S(2)}) %collective-permute-start.3) | collective-permute-done | bytes 32800 | tf_op jit(solution)/shard_map/ppermute | solution.py:498
  19.0 2.7 %collective-permute-start.4 = (f32[104,128]{1,0:T(8,128)S(1)}, f32[104,128]{1,0:T(8,128)S(1)}, u32[]{:S(2)}, u32[]{:S(2)}) collective-permute-start(f32[104,128]{1,0:T(8,128)S(1)} %get-tuple-element.54), channel_id=1, source_target_pairs={{0,16},{16,0},{1,17},{17,1},{2,18},{18,2},{3,19},{19,3},{4,20},{20... | collective-permute-start | bytes 159752 | tf_op jit(solution)/shard_map/ppermute | solution.py:498
  21.7 1.2 %near_ends.1.near_end_ref = f32[4,4,128]{2,1,0:T(4,128)S(1)} custom-call(f32[3,4,4,128]{3,2,1,0:T(4,128)S(1)} %copy-done.2, f32[4,24,128]{2,1,0:T(8,128)S(1)} %get-tuple-element.55.r_ref, f32[4,8,128]{2,1,0:T(8,128)S(1)} %get-tuple-element.56.zl_ref, f32[4,8,128]{2,1,0:T(8,128)S(1)} %get-tuple-element.57.zh_ref), custom_call_target="tpu_custom_call" | custom-call | tf_op jit(solution)/shard_map/near_ends/pallas_call | solution.py:503
  22.9 0.0 collective-permute-done.4.rest_0_
  22.9 0.0 copy-done.4
  22.9 0.0 copy-done.7
  22.9 3.0 %final.1 = f32[4,4,128]{2,1,0:T(4,128)} custom-call(f32[3,4,4,128]{3,2,1,0:T(4,128)S(1)} %copy-done.2, f32[16,8,128]{2,1,0:T(8,128)S(1)} %get-tuple-element.50.e_ref, f32[2,4,128]{2,1,0:T(4,128)S(1)} %near_edge.1.near_edge_ref, f32[2,4,128]{2,1,0:T(4,128)S(1)} %near_inner.1.near_in_ref, f32[4,4,128]{2,1,0:T(4,128)S(1)} %near_ends.1.near_end_ref, ...), custom_call_target="tpu_custom_call" | custom-call | tf_op jit(solution)/shard_map/final/pallas_call | solution.py:503
  (1 shorter events, 0.0 us)
Async XLA Ops:
  0.0 0.7 %copy-start.1 = (f32[3,4,4,128]{3,2,1,0:T(4,128)S(1)}, f32[3,4,4,128]{3,2,1,0:T(4,128)}, u32[]{:S(2)}) copy-start(f32[3,4,4,128]{3,2,1,0:T(4,128)} %offs_ref.8) | copy-start | bytes 73732
  0.7 0.8 %copy-start.3 = (f32[64,128]{1,0:T(8,128)S(1)}, f32[64,128]{1,0:T(8,128)}, u32[]{:S(2)}) copy-start(f32[64,128]{1,0:T(8,128)} %constant.2.clone.sphere_hbm.sphere_ref) | copy-start | bytes 98308
  1.5 0.7 %copy-start.5 = (f32[4,4,128]{2,1,0:T(4,128)S(1)}, f32[4,4,128]{2,1,0:T(4,128)}, u32[]{:S(2)}) copy-start(f32[4,4,128]{2,1,0:T(4,128)} %q_ref.2) | copy-start | bytes 24580
  2.2 0.8 %copy-start.8 = (f32[64,64]{1,0:T(8,128)S(1)}, f32[64,64]{1,0:T(8,128)}, u32[]{:S(2)}) copy-start(f32[64,64]{1,0:T(8,128)} %uinv_hbm.1) | copy-start | bytes 49156
  3.0 8.4 %copy-start.2 = (f32[3,4,4,128]{3,2,1,0:T(4,128)S(1)}, f32[3,4,4,128]{3,2,1,0:T(4,128)}, u32[]{:S(2)}) copy-start(f32[3,4,4,128]{3,2,1,0:T(4,128)} %offs_ref.8) | copy-start | bytes 73732
  3.0 8.4 %copy-start.6 = (f32[4,4,128]{2,1,0:T(4,128)S(1)}, f32[4,4,128]{2,1,0:T(4,128)}, u32[]{:S(2)}) copy-start(f32[4,4,128]{2,1,0:T(4,128)} %q_ref.2) | copy-start | bytes 24580
  3.0 19.9 %copy-start.4 = (f32[64,128]{1,0:T(8,128)S(1)}, f32[64,128]{1,0:T(8,128)}, u32[]{:S(2)}) copy-start(f32[64,128]{1,0:T(8,128)} %constant.2.clone.sphere_hbm.sphere_ref) | copy-start | bytes 98308
  3.0 19.9 %copy-start.7 = (f32[64,64]{1,0:T(8,128)S(1)}, f32[64,64]{1,0:T(8,128)}, u32[]{:S(2)}) copy-start(f32[64,64]{1,0:T(8,128)} %dinv_ref.1) | copy-start | bytes 49156
  4.1 8.6 %collective-permute-start = (f32[32,128]{1,0:T(8,128)S(1)}, f32[32,128]{1,0:T(8,128)S(1)}, u32[]{:S(2)}, u32[]{:S(2)}) collective-permute-start(f32[32,128]{1,0:T(8,128)S(1)} %get-tuple-element.34), channel_id=1, source_target_pairs={{0,4},{4,0},{8,12},{12,8},{1,5},{5,1},{9,13},{13,9},{2,6},{6,2},{1... | collective-permute-start | bytes 49160 | tf_op jit(solution)/shard_map/ppermute | solution.py:498
  4.4 8.3 %collective-permute-start.1 = (f32[32,128]{1,0:T(8,128)S(1)}, f32[32,128]{1,0:T(8,128)S(1)}, u32[]{:S(2)}, u32[]{:S(2)}) collective-permute-start(f32[32,128]{1,0:T(8,128)S(1)} %get-tuple-element.35), channel_id=1, source_target_pairs={{4,8},{8,4},{5,9},{9,5},{6,10},{10,6},{7,11},{11,7},{20,24},{24,20... | collective-permute-start | bytes 49160 | tf_op jit(solution)/shard_map/ppermute | solution.py:498
  8.5 1.7 %copy-start = (bf16[316,4096]{1,0:T(8,128)(2,1)S(1)}, bf16[316,4096]{1,0:T(8,128)(2,1)}, u32[]{:S(2)}) copy-start(bf16[316,4096]{1,0:T(8,128)(2,1)} %t_ref.1) | copy-start | bytes 7766020
  12.9 5.4 %collective-permute-start.2 = (f32[64,128]{1,0:T(8,128)S(1)}, f32[64,128]{1,0:T(8,128)S(1)}, u32[]{:S(2)}, u32[]{:S(2)}) collective-permute-start(f32[64,128]{1,0:T(8,128)S(1)} %get-tuple-element.46), channel_id=1, source_target_pairs={{0,1},{1,0},{2,3},{3,2},{4,5},{5,4},{6,7},{7,6},{8,9},{9,8},{10,11... | collective-permute-start | bytes 98312 | tf_op jit(solution)/shard_map/ppermute | solution.py:498
  14.3 4.6 %collective-permute-start.3 = (f32[64,128]{1,0:T(8,128)S(1)}, f32[64,128]{1,0:T(8,128)S(1)}, u32[]{:S(2)}, u32[]{:S(2)}) collective-permute-start(f32[64,128]{1,0:T(8,128)S(1)} %get-tuple-element.47), channel_id=1, source_target_pairs={{1,2},{2,1},{5,6},{6,5},{9,10},{10,9},{13,14},{14,13},{17,18},{18,... | collective-permute-start | bytes 98312 | tf_op jit(solution)/shard_map/ppermute | solution.py:498
  19.0 3.9 %collective-permute-start.4 = (f32[104,128]{1,0:T(8,128)S(1)}, f32[104,128]{1,0:T(8,128)S(1)}, u32[]{:S(2)}, u32[]{:S(2)}) collective-permute-start(f32[104,128]{1,0:T(8,128)S(1)} %get-tuple-element.54), channel_id=1, source_target_pairs={{0,16},{16,0},{1,17},{17,1},{2,18},{18,2},{3,19},{19,3},{4,20},{20... | collective-permute-start | bytes 159752 | tf_op jit(solution)/shard_map/ppermute | solution.py:498

commit v3 on v2

--- a/solution.py
+++ b/solution.py
@@ -70,12 +70,20 @@
     return select(even, one, refs[1][...] if len(refs) > 1 else jnp.zeros_like(one))
 
 
-def upward_kernel(offs_hbm, q_hbm, sphere_hbm, uinv_hbm, u_ref, *rest):
-    *packets, offs_ref, q_ref, sphere_ref, uinv_ref, check_ref, wide_ref, sems = rest
+def upward_kernel(
+    offs_hbm, q_hbm, sphere_hbm, uinv_hbm, dinv_hbm, offs_ref, q_ref, sphere_ref, dinv_ref, u_ref, *rest
+):
+    *packets, uinv_ref, check_ref, wide_ref, sems = rest
     copies = [
         pltpu.make_async_copy(source, target, sems.at[n])
         for n, (source, target) in enumerate(
-            ((offs_hbm, offs_ref), (q_hbm, q_ref), (sphere_hbm, sphere_ref), (uinv_hbm, uinv_ref))
+            (
+                (offs_hbm, offs_ref),
+                (q_hbm, q_ref),
+                (sphere_hbm, sphere_ref),
+                (uinv_hbm, uinv_ref),
+                (dinv_hbm, dinv_ref),
+            )
         )
     ]
     for copy in copies:
@@ -124,9 +132,10 @@
         low = u_ref[pl.ds(x * half * lz, lz), :]
         high = u_ref[pl.ds((x * half + half - 1) * lz, lz), :]
         put(packets, pl.ds(x * lz, lz), even, low, high)
-
-
-def table_kernel(t_ref, after_ref, w_ref, rows_ref):
+    copies[4].wait()
+
+
+def relay(t_ref, copies, w_ref, rows_ref):
     count, width = t_ref.shape
     groups = width // 128
     stride = rows_ref.shape[0] // groups
@@ -134,6 +143,8 @@
     half = points // 2
     order = numbering()
     for a in range(groups):
+        if a % (groups // len(copies)) == 0:
+            copies[a // (groups // len(copies))].wait()
         rows_ref[pl.ds(a * stride, count), :] = t_ref[:, a * 128 : (a + 1) * 128].astype(F32)
     left = lax.broadcasted_iota(jnp.int32, (groups, 128), 1) < points
     zero = jnp.zeros((groups, 128), F32)
@@ -271,7 +282,17 @@
     return [ref[c, at, :] for c in range(3)], ref[3 + z, at, :], own
 
 
-def edge_kernel(offs_ref, q_ref, out_ref, win_ref):
+def edge_kernel(t_hbm, after_ref, offs_ref, q_ref, out_ref, w_ref, win_ref, t_ref, rows_ref, sems):
+    chunks = sems.shape[0]
+    cut = t_ref.shape[1] // chunks
+    copies = [
+        pltpu.make_async_copy(
+            t_hbm.at[:, pl.ds(n * cut, cut)], t_ref.at[:, pl.ds(n * cut, cut)], sems.at[n]
+        )
+        for n in range(chunks)
+    ]
+    for copy in copies:
+        copy.start()
     _, lx, ly, lanes = offs_ref.shape
     lz = lanes // BODIES
     spot = lax.broadcasted_iota(jnp.int32, (ly, lanes), 1) // BODIES
@@ -293,6 +314,7 @@
                         yield row_source(win_ref, pl.ds(xx * ly + yy, 1), z, xx == x and yy == y)
 
             gather(out_ref, n, y, turned, lz, rows)
+    relay(t_ref, copies, w_ref, rows_ref)
 
 
 def strips(r_ref, win_ref, wide, lz):
@@ -527,44 +549,46 @@
     sphere = jnp.asarray(surface(points))
     boxes = lx * half * lz
     packet = shaped(lx * lz + 4 * lx, lanes)
-    density, *packets = call(
+    inputs = [
+        pltpu.with_memory_space_constraint(value, pltpu.HBM)
+        for value in (offsets, charges, sphere, up_inverse, down_inverse)
+    ]
+    offsets, charges, sphere, down_inverse, density, *packets = call(
         upward_kernel,
-        [shaped(boxes, 2 * points)] + [packet] * rounds["gy"],
-        (offsets, charges, sphere, up_inverse),
+        [shaped(*value.shape) for value in (offsets, charges, sphere, down_inverse)]
+        + [shaped(boxes, 2 * points)]
+        + [packet] * rounds["gy"],
+        inputs,
         [
-            pltpu.VMEM(offsets.shape, F32),
-            pltpu.VMEM(charges.shape, F32),
-            pltpu.VMEM(sphere.shape, F32),
             pltpu.VMEM(up_inverse.shape, F32),
             pltpu.VMEM((boxes, 2 * points), F32),
             pltpu.VMEM((2 * points, 2 * points), F32),
-            pltpu.SemaphoreType.DMA((4,)),
+            pltpu.SemaphoreType.DMA((5,)),
         ],
         4,
         "upward",
-        [pltpu.HBM] * 4,
+        [pltpu.HBM] * 5,
     )
     received = exchange(packets, "gy")
     count, width = translations.shape
     stride = count // 2 * 2 + 1
-    (weights,) = call(
-        table_kernel,
-        [jax.ShapeDtypeStruct((SPAN, SPAN * points, (SPAN + 1) * points), BF16)],
-        (translations, density),
-        [pltpu.VMEM((width // 128 * stride, 128), F32)],
-        16,
-        "table",
-        [pltpu.VMEM, pl.ANY],
+    edge, weights = call(
+        edge_kernel,
+        [
+            shaped(2, ly, lanes),
+            jax.ShapeDtypeStruct((SPAN, SPAN * points, (SPAN + 1) * points), BF16),
+        ],
+        (pltpu.with_memory_space_constraint(translations, pltpu.HBM), density, offsets, charges),
+        [
+            pltpu.VMEM((3 + lz, lx * ly, lanes), F32),
+            pltpu.VMEM(translations.shape, BF16),
+            pltpu.VMEM((width // 128 * stride, 128), F32),
+            pltpu.SemaphoreType.DMA((4,)),
+        ],
+        24,
+        "near_edge",
+        [pltpu.HBM, pl.ANY, pltpu.VMEM, pltpu.VMEM],
     )
-    first = lax.optimization_barrier((offsets, charges, weights))
-    (edge,) = call(
-        edge_kernel,
-        [shaped(2, ly, lanes)],
-        first[:2],
-        [pltpu.VMEM((3 + lz, lx * ly, lanes), F32)],
-        name="near_edge",
-    )
-    weights = first[2]
     received, edge, weights = lax.optimization_barrier((received, edge, weights))
     packet = shaped(lx * pairs * 2 + 4 * half * lx, lanes)
     dense, body, *packets = call(

time: 26.3 us -> 22.7 us (0.86)
  the two profiles are of different devices: /device:TPU:19 before, /device:TPU:21 now
where the time goes in v3:
time: 22.7 us; the launch traced here: 22.5 us
  Pallas kernels  11 us (48%)
  starting transfers between devices  10.2 us (45%)
  waiting for transfers between devices  1.2 us (5%)
    pallas_call x7, Pallas kernels, call(): pl.pallas_call(kernel, out_shape=outs, in_specs=[pl.BlockSpec(memory_spac...  11 us
    ppermute x5, starting transfers between devices, exchange(): lax.ppermute(packet, axis, pairs)  10.2 us
    ppermute x5, waiting for transfers between devices, exchange(): lax.ppermute(packet, axis, pairs)  1.2 us
  transfers between devices with their start and end apart: 5, of which 2 were waited for; matrix products, arithmetic and copies ran while one was open for 0% of the time, Pallas kernels for 26%

profile of v3, /device:TPU:21, one launch (start us, length us, event | category | flops | bytes accessed | tf_op | source)
XLA Modules:
  0.0 22.5 jit_solution(4502327473125697271)
XLA Ops:
  0.0 1.8 %upward.1 = (f32[3,4,4,128]{3,2,1,0:T(4,128)S(1)}, f32[4,4,128]{2,1,0:T(4,128)S(1)}, f32[64,128]{1,0:T(8,128)S(1)}, f32[64,64]{1,0:T(8,128)S(1)}, f32[32,128]{1,...) custom-call(f32[3,4,4,128]{3,2,1,0:T(4,128)} %offs_hbm.1, f32[4,4,128]{2,1,0:T(4,128)} %q_hbm.1, ...), custom_call_target="tpu_custom_call" | custom-call | tf_op jit(solution)/shard_map/upward/pallas_call | solution.py:525
  1.8 1.3 %collective-permute-start = (f32[32,128]{1,0:T(8,128)S(1)}, f32[32,128]{1,0:T(8,128)S(1)}, u32[]{:S(2)}, u32[]{:S(2)}) collective-permute-start(f32[32,128]{1,0:T(8,128)S(1)} %get-tuple-element.39), channel_id=1, source_target_pairs={{0,4},{4,0},{8,12},{12,8},{1,5},{5,1},{9,13},{13,9},{2,6},{6,2},{1... | collective-permute-start | bytes 49160 | tf_op jit(solution)/shard_map/ppermute | solution.py:520
  3.1 2.1 %collective-permute-start.1 = (f32[32,128]{1,0:T(8,128)S(1)}, f32[32,128]{1,0:T(8,128)S(1)}, u32[]{:S(2)}, u32[]{:S(2)}) collective-permute-start(f32[32,128]{1,0:T(8,128)S(1)} %get-tuple-element.40), channel_id=1, source_target_pairs={{4,8},{8,4},{5,9},{9,5},{6,10},{10,6},{7,11},{11,7},{20,24},{24,20... | collective-permute-start | bytes 49160 | tf_op jit(solution)/shard_map/ppermute | solution.py:520
  5.2 2.6 %near_edge.1 = (f32[2,4,128]{2,1,0:T(4,128)S(1)}, bf16[7,448,512]{2,1,0:T(8,128)(2,1)S(1)}) custom-call(bf16[316,4096]{1,0:T(8,128)(2,1)} %t_hbm.1, f32[32,128]{1,0:T(8,128)S(1)} %get-tuple-element.38.after_ref.u_ref, f32[3,4,4,128]{3,2,1,0:T(4,128)S(1)} %get-tuple-element.36.offs_ref, f32[4,4,128]{2,1,0:T(4,128)S(1)} %get-tuple-element.37.q_ref), custom_call_target="tpu_custom_call" | custom-call | tf_op jit(solution)/shard_map/near_edge/pallas_call | solution.py:525
  7.8 0.0 collective-permute-done.rest_0_
  7.8 0.6 %collective-permute-done.1.rest_1_ = f32[32,128]{1,0:T(8,128)S(1)} collective-permute-done((f32[32,128]{1,0:T(8,128)S(1)}, f32[32,128]{1,0:T(8,128)S(1)}, u32[]{:S(2)}, u32[]{:S(2)}) %collective-permute-start.1) | collective-permute-done | bytes 16416 | tf_op jit(solution)/shard_map/ppermute | solution.py:520
  8.4 0.1 zpack.1
  8.6 1.4 %collective-permute-start.2 = (f32[64,128]{1,0:T(8,128)S(1)}, f32[64,128]{1,0:T(8,128)S(1)}, u32[]{:S(2)}, u32[]{:S(2)}) collective-permute-start(f32[64,128]{1,0:T(8,128)S(1)} %get-tuple-element.50), channel_id=1, source_target_pairs={{0,1},{1,0},{2,3},{3,2},{4,5},{5,4},{6,7},{7,6},{8,9},{9,8},{10,11... | collective-permute-start | bytes 98312 | tf_op jit(solution)/shard_map/ppermute | solution.py:520
  9.9 1.9 %collective-permute-start.3 = (f32[64,128]{1,0:T(8,128)S(1)}, f32[64,128]{1,0:T(8,128)S(1)}, u32[]{:S(2)}, u32[]{:S(2)}) collective-permute-start(f32[64,128]{1,0:T(8,128)S(1)} %get-tuple-element.51), channel_id=1, source_target_pairs={{1,2},{2,1},{5,6},{6,5},{9,10},{10,9},{13,14},{14,13},{17,18},{18,... | collective-permute-start | bytes 98312 | tf_op jit(solution)/shard_map/ppermute | solution.py:520
  11.9 2.2 %near_inner.1.near_in_ref = f32[2,4,128]{2,1,0:T(4,128)S(1)} custom-call(f32[3,4,4,128]{3,2,1,0:T(4,128)S(1)} %get-tuple-element.36.offs_ref, f32[4,24,128]{2,1,0:T(8,128)S(1)} %get-tuple-element.59.r_ref), custom_call_target="tpu_custom_call" | custom-call | tf_op jit(solution)/shard_map/near_inner/pallas_call | solution.py:525
  14.0 0.0 collective-permute-done.2.rest_0_
  14.0 0.6 %collective-permute-done.3.rest_1_ = f32[64,128]{1,0:T(8,128)S(1)} collective-permute-done((f32[64,128]{1,0:T(8,128)S(1)}, f32[64,128]{1,0:T(8,128)S(1)}, u32[]{:S(2)}, u32[]{:S(2)}) %collective-permute-start.3) | collective-permute-done | bytes 32800 | tf_op jit(solution)/shard_map/ppermute | solution.py:520
  14.6 3.6 %collective-permute-start.4 = (f32[104,128]{1,0:T(8,128)S(1)}, f32[104,128]{1,0:T(8,128)S(1)}, u32[]{:S(2)}, u32[]{:S(2)}) collective-permute-start(f32[104,128]{1,0:T(8,128)S(1)} %get-tuple-element.58), channel_id=1, source_target_pairs={{0,16},{16,0},{1,17},{17,1},{2,18},{18,2},{3,19},{19,3},{4,20},{20... | collective-permute-start | bytes 159752 | tf_op jit(solution)/shard_map/ppermute | solution.py:520
  18.2 1.2 %near_ends.1.near_end_ref = f32[4,4,128]{2,1,0:T(4,128)S(1)} custom-call(f32[3,4,4,128]{3,2,1,0:T(4,128)S(1)} %get-tuple-element.36.offs_ref, f32[4,24,128]{2,1,0:T(8,128)S(1)} %get-tuple-element.59.r_ref, f32[4,8,128]{2,1,0:T(8,128)S(1)} %get-tuple-element.60.zl_ref, f32[4,8,128]{2,1,0:T(8,128)S(1)} %get-tuple-element.61.zh_ref), custom_call_target="tpu_custom_call" | custom-call | tf_op jit(solution)/shard_map/near_ends/pallas_call | solution.py:525
  19.4 0.0 collective-permute-done.4.rest_0_
  19.4 3.1 %final.1 = f32[4,4,128]{2,1,0:T(4,128)} custom-call(f32[3,4,4,128]{3,2,1,0:T(4,128)S(1)} %get-tuple-element.36.offs_ref, f32[16,8,128]{2,1,0:T(8,128)S(1)} %get-tuple-element.54.e_ref, f32[2,4,128]{2,1,0:T(4,128)S(1)} %get-tuple-element.55.near_edge_ref, f32[2,4,128]{2,1,0:T(4,128)S(1)} %near_inner.1.near_in_ref, f32[4,4,128]{2,1,0:T(4,128)S(1)} %near_ends.1.near_end_ref, ...), custom_call_target="tpu_custom_call" | custom-call | tf_op jit(solution)/shard_map/final/pallas_call | solution.py:525
  (1 shorter events, 0.0 us)
Async XLA Ops:
  1.8 6.0 %collective-permute-start = (f32[32,128]{1,0:T(8,128)S(1)}, f32[32,128]{1,0:T(8,128)S(1)}, u32[]{:S(2)}, u32[]{:S(2)}) collective-permute-start(f32[32,128]{1,0:T(8,128)S(1)} %get-tuple-element.39), channel_id=1, source_target_pairs={{0,4},{4,0},{8,12},{12,8},{1,5},{5,1},{9,13},{13,9},{2,6},{6,2},{1... | collective-permute-start | bytes 49160 | tf_op jit(solution)/shard_map/ppermute | solution.py:520
  3.1 5.4 %collective-permute-start.1 = (f32[32,128]{1,0:T(8,128)S(1)}, f32[32,128]{1,0:T(8,128)S(1)}, u32[]{:S(2)}, u32[]{:S(2)}) collective-permute-start(f32[32,128]{1,0:T(8,128)S(1)} %get-tuple-element.40), channel_id=1, source_target_pairs={{4,8},{8,4},{5,9},{9,5},{6,10},{10,6},{7,11},{11,7},{20,24},{24,20... | collective-permute-start | bytes 49160 | tf_op jit(solution)/shard_map/ppermute | solution.py:520
  8.6 5.4 %collective-permute-start.2 = (f32[64,128]{1,0:T(8,128)S(1)}, f32[64,128]{1,0:T(8,128)S(1)}, u32[]{:S(2)}, u32[]{:S(2)}) collective-permute-start(f32[64,128]{1,0:T(8,128)S(1)} %get-tuple-element.50), channel_id=1, source_target_pairs={{0,1},{1,0},{2,3},{3,2},{4,5},{5,4},{6,7},{7,6},{8,9},{9,8},{10,11... | collective-permute-start | bytes 98312 | tf_op jit(solution)/shard_map/ppermute | solution.py:520
  9.9 4.6 %collective-permute-start.3 = (f32[64,128]{1,0:T(8,128)S(1)}, f32[64,128]{1,0:T(8,128)S(1)}, u32[]{:S(2)}, u32[]{:S(2)}) collective-permute-start(f32[64,128]{1,0:T(8,128)S(1)} %get-tuple-element.51), channel_id=1, source_target_pairs={{1,2},{2,1},{5,6},{6,5},{9,10},{10,9},{13,14},{14,13},{17,18},{18,... | collective-permute-start | bytes 98312 | tf_op jit(solution)/shard_map/ppermute | solution.py:520
  14.6 4.8 %collective-permute-start.4 = (f32[104,128]{1,0:T(8,128)S(1)}, f32[104,128]{1,0:T(8,128)S(1)}, u32[]{:S(2)}, u32[]{:S(2)}) collective-permute-start(f32[104,128]{1,0:T(8,128)S(1)} %get-tuple-element.58), channel_id=1, source_target_pairs={{0,16},{16,0},{1,17},{17,1},{2,18},{18,2},{3,19},{19,3},{4,20},{20... | collective-permute-start | bytes 159752 | tf_op jit(solution)/shard_map/ppermute | solution.py:520

commit v4 on v3

--- a/solution.py
+++ b/solution.py
@@ -65,15 +65,17 @@
         ref[at, :] = jnp.where(even, low, high)
 
 
-def get(refs, even):
+def get(refs, axis):
+    index = lax.axis_index(axis)
     one = refs[0][...]
-    return select(even, one, refs[1][...] if len(refs) > 1 else jnp.zeros_like(one))
+    above, below = select(index % 2 == 0, one, refs[1][...] if len(refs) > 1 else one)
+    return jnp.where(index == lax.axis_size(axis) - 1, 0.0, above), jnp.where(index == 0, 0.0, below)
 
 
 def upward_kernel(
-    offs_hbm, q_hbm, sphere_hbm, uinv_hbm, dinv_hbm, offs_ref, q_ref, sphere_ref, dinv_ref, u_ref, *rest
+    offs_hbm, q_hbm, sphere_hbm, uinv_hbm, dinv_hbm, offs_ref, q_ref, dinv_ref, g_ref, u_ref, *rest
 ):
-    *packets, uinv_ref, check_ref, wide_ref, sems = rest
+    *packets, sphere_ref, uinv_ref, check_ref, wide_ref, sems = rest
     copies = [
         pltpu.make_async_copy(source, target, sems.at[n])
         for n, (source, target) in enumerate(
@@ -113,10 +115,11 @@
             put(packets, pl.ds(lx * lz + c * lx + x, 1), even, low, high)
     for x in range(lx):
         for pair in range(half):
-            parts = [
-                surface_green(sphere, offs_ref, x, 2 * pair + par) * q_ref[x, pl.ds(2 * pair + par, 1), :]
-                for par in range(2)
-            ]
+            parts = []
+            for y in (2 * pair, 2 * pair + 1):
+                kernel = surface_green(sphere, offs_ref, x, y)
+                g_ref[x * ly + y] = kernel
+                parts.append(kernel * q_ref[x, pl.ds(y, 1), :])
             high, low = split(jnp.concatenate(parts, axis=0))
             sums = lax.dot_general(segment, high, NT, preferred_element_type=F32)
             sums = sums + lax.dot_general(segment, low, NT, preferred_element_type=F32)
@@ -169,7 +172,7 @@
     lz = lanes // BODIES
     half = ly // 2
     wide = ly + 2
-    above, below = get(received, lax.axis_index("gy") % 2 == 0)
+    above, below = get(received, "gy")
     even = lax.axis_index("gz") % 2 == 0
     for x in range(lx):
         at = x * (half + 2) * lz
@@ -206,7 +209,7 @@
     half = pairs - 2
     wide = 2 * half + 2
     lz = d_ref.shape[0] // groups
-    above, below = get(received, lax.axis_index("gz") % 2 == 0)
+    above, below = get(received, "gz")
     even = lax.axis_index("gx") % 2 == 0
     for g in range(groups):
         e_ref[g, pl.ds(0, 2), :] = below[g * 2 : g * 2 + 2]
@@ -387,7 +390,7 @@
         win_ref[at + 3 + s] = jnp.where((spot >= s) & (spot < s + 3), end_ref[3], 0.0)
 
 
-def final_kernel(count, offs_ref, e_ref, near_edge_ref, near_in_ref, near_end_ref, w_ref, dinv_ref, sphere_ref, *rest):
+def final_kernel(count, offs_ref, e_ref, near_edge_ref, near_in_ref, near_end_ref, w_ref, dinv_ref, g_ref, *rest):
     received, rest = rest[:count], rest[count:]
     out_ref, left_ref, acc_ref, dense_ref, sum_ref, side_ref, edge_ref = rest
     _, lx, ly, lanes = offs_ref.shape
@@ -399,7 +402,7 @@
     deep = lz + 4
     block = half * deep
     width = (SPAN - 1) * points
-    above, below = get(received, lax.axis_index("gx") % 2 == 0)
+    above, below = get(received, "gx")
 
     def plane(x, pair):
         if x < 2:
@@ -414,6 +417,52 @@
             left_ref[pl.ds(x * block, block), j * 128 : (j + 1) * 128] = jnp.concatenate(
                 planes[j : j + half], axis=0
             ).astype(BF16)
+    spot = lax.broadcasted_iota(jnp.int32, (wide, lanes), 1) // BODIES
+    lead = lax.broadcasted_iota(jnp.int32, (wide, lanes), 0).astype(F32) - 1.0
+    base = 2 * pairs * deep
+    ends = base + 4 * wide
+    for side, value in enumerate((below, above)):
+        shift = [-1.0 if side == 0 else float(lx), lead, spot.astype(F32)]
+        for c in range(3):
+            side_ref[side, c] = value[base + c * wide : base + (c + 1) * wide] + shift[c]
+        for z, part in enumerate(spans(value[base + 3 * wide : base + 4 * wide], spot, lz)):
+            side_ref[side, 3 + z] = part
+    spot = lax.broadcasted_iota(jnp.int32, (half, lanes), 1) // BODIES
+    place = lax.broadcasted_iota(jnp.int32, (half, lanes), 0)
+    for side, value in enumerate((below, above)):
+        for end in range(2):
+            shift = [-1.0 if side == 0 else float(lx), (spot + 2 * place - 1).astype(F32), -1.0 if end == 0 else float(lz)]
+            for c in range(3):
+                at = ends + (end * 4 + c) * half
+                edge_ref[side, end * 5 + c] = value[at : at + half] + shift[c]
+            at = ends + (end * 4 + 3) * half
+            for s in range(2):
+                edge_ref[side, end * 5 + 3 + s] = jnp.where((spot >= s) & (spot < s + 3), value[at : at + half], 0.0)
+
+
+    def side_unit(x, y, turned):
+        side = 0 if x == 0 else 1
+
+        def rows(z):
+            for dy in range(3):
+                at = pl.ds(y + dy, 1)
+                yield [side_ref[side, c, at, :] for c in range(3)], side_ref[side, 3 + z, at, :], False
+            for end in range(2):
+                if z == (0 if end == 0 else lz - 1):
+                    at = pl.ds(y // 2, 1)
+                    source = [edge_ref[side, end * 5 + c, at, :] for c in range(3)]
+                    yield source, edge_ref[side, end * 5 + 3 + y % 2, at, :], False
+
+        gather(out_ref, x, y, turned, lz, rows)
+
+    def units():
+        for x in (0, lx - 1):
+            turned = turn(offs_ref, x)
+            for y in range(ly):
+                side_unit(x, y, turned)
+                yield
+
+    waiting = units()
     twice = jnp.concatenate([dinv_ref[...]] * 2, axis=0)
     expand = (
         lax.broadcasted_iota(jnp.int32, (lx * half * lz, lx * half * lanes), 1) // BODIES
@@ -432,6 +481,7 @@
             for n, b in enumerate(chosen):
                 piece = got[n * block : (n + 1) * block]
                 total[b] = piece if total[b] is None else total[b] + piece
+            next(waiting, None)
         for b in range(lx):
             for p in range(half):
                 acc_ref[b * half + p, pl.ds(8, deep), :] = total[b][p * deep : (p + 1) * deep]
@@ -459,65 +509,42 @@
         for g in range(lx * half):
             dense_ref[g, cy] = spread[:, g * lanes : (g + 1) * lanes]
 
-    spot = lax.broadcasted_iota(jnp.int32, (wide, lanes), 1) // BODIES
-    lead = lax.broadcasted_iota(jnp.int32, (wide, lanes), 0).astype(F32) - 1.0
-    base = 2 * pairs * deep
-    ends = base + 4 * wide
-    for side, value in enumerate((below, above)):
-        shift = [-1.0 if side == 0 else float(lx), lead, spot.astype(F32)]
-        for c in range(3):
-            side_ref[side, c] = value[base + c * wide : base + (c + 1) * wide] + shift[c]
-        for z, part in enumerate(spans(value[base + 3 * wide : base + 4 * wide], spot, lz)):
-            side_ref[side, 3 + z] = part
-    spot = lax.broadcasted_iota(jnp.int32, (half, lanes), 1) // BODIES
-    place = lax.broadcasted_iota(jnp.int32, (half, lanes), 0)
-    for side, value in enumerate((below, above)):
-        for end in range(2):
-            shift = [-1.0 if side == 0 else float(lx), (spot + 2 * place - 1).astype(F32), -1.0 if end == 0 else float(lz)]
-            for c in range(3):
-                at = ends + (end * 4 + c) * half
-                edge_ref[side, end * 5 + c] = value[at : at + half] + shift[c]
-            at = ends + (end * 4 + 3) * half
-            for s in range(2):
-                edge_ref[side, end * 5 + 3 + s] = jnp.where((spot >= s) & (spot < s + 3), value[at : at + half], 0.0)
-
-    sphere = sphere_ref[...]
+    for _ in waiting:
+        pass
     for x in range(lx):
-        turned = turn(offs_ref, x) if x in (0, lx - 1) else None
         for y in range(ly):
-
-            def rows(z):
-                for side in range(2):
-                    if x == (0 if side == 0 else lx - 1):
-                        for dy in range(3):
-                            at = pl.ds(y + dy, 1)
-                            yield [side_ref[side, c, at, :] for c in range(3)], side_ref[side, 3 + z, at, :], False
-                        for end in range(2):
-                            if z == (0 if end == 0 else lz - 1):
-                                at = pl.ds(y // 2, 1)
-                                source = [edge_ref[side, end * 5 + c, at, :] for c in range(3)]
-                                yield source, edge_ref[side, end * 5 + 3 + y % 2, at, :], False
-
-            kernel = surface_green(sphere, offs_ref, x, y)
-            far = jnp.sum(kernel * dense_ref[x * half + y // 2, y % 2], axis=0, keepdims=True)
+            far = jnp.sum(g_ref[x * ly + y] * dense_ref[x * half + y // 2, y % 2], axis=0, keepdims=True)
             at = pl.ds(y, 1)
             total = near_end_ref[x, at, :] + far
             if x in (0, lx - 1):
-                gather(out_ref, x, y, turned, lz, rows)
                 total = total + out_ref[x, at, :] + near_edge_ref[0 if x == 0 else 1, at, :]
             else:
                 total = total + near_in_ref[x - 1, at, :]
             out_ref[x, at, :] = total
 
 
-def partners(axis):
+def rounds_of(axis):
+    return [[(i, i + 1) for i in range(start, lax.axis_size(axis) - 1, 2)] for start in range(2)]
+
+
+def rounds_in(axis):
+    return max(1, sum(1 for pairs in rounds_of(axis) if pairs))
+
+
+def exchange(packets, axis):
     count = lax.axis_size(axis)
-    rounds = [[(i, i + 1) for i in range(start, count - 1, 2)] for start in range(2)]
-    return [[pair for i, j in pairs for pair in ((i, j), (j, i))] for pairs in rounds if pairs] or [[]]
-
-
-def exchange(packets, axis):
-    return [lax.ppermute(packet, axis, pairs) for packet, pairs in zip(packets, partners(axis))]
+    planes = lax.axis_size("gx")
+    results = []
+    for packet, pairs in zip(packets, rounds_of(axis)):
+        swaps = [swap for i, j in pairs for swap in ((i, j), (j, i))]
+        idle = sorted(set(range(count)) - {i for i, _ in swaps})
+        if not idle or axis == "gx" or planes % 2:
+            results.append(lax.ppermute(packet, axis, swaps))
+            continue
+        swaps = [(plane * count + i, plane * count + j) for plane in range(planes) for i, j in swaps]
+        swaps += [(plane * count + i, (plane ^ 1) * count + i) for plane in range(planes) for i in idle]
+        results.append(lax.ppermute(packet, ("gx", axis), swaps))
+    return results
 
 
 def call(kernel, outs, args, scratch=(), limit=8, name=None, spaces=None):
@@ -545,7 +572,7 @@
     pairs = half + 2
     wide = ly + 2
     deep = lz + 4
-    rounds = {axis: len(partners(axis)) for axis in ("gx", "gy", "gz")}
+    rounds = {axis: rounds_in(axis) for axis in ("gx", "gy", "gz")}
     sphere = jnp.asarray(surface(points))
     boxes = lx * half * lz
     packet = shaped(lx * lz + 4 * lx, lanes)
@@ -553,13 +580,14 @@
         pltpu.with_memory_space_constraint(value, pltpu.HBM)
         for value in (offsets, charges, sphere, up_inverse, down_inverse)
     ]
-    offsets, charges, sphere, down_inverse, density, *packets = call(
+    offsets, charges, down_inverse, surfaces, density, *packets = call(
         upward_kernel,
-        [shaped(*value.shape) for value in (offsets, charges, sphere, down_inverse)]
-        + [shaped(boxes, 2 * points)]
+        [shaped(*value.shape) for value in (offsets, charges, down_inverse)]
+        + [shaped(lx * ly, points, lanes), shaped(boxes, 2 * points)]
         + [packet] * rounds["gy"],
         inputs,
         [
+            pltpu.VMEM(sphere.shape, F32),
             pltpu.VMEM(up_inverse.shape, F32),
             pltpu.VMEM((boxes, 2 * points), F32),
             pltpu.VMEM((2 * points, 2 * points), F32),
@@ -623,7 +651,7 @@
     (out,) = call(
         functools.partial(final_kernel, len(received)),
         [shaped(lx, ly, lanes)],
-        (offsets, dense, edge, inner, ends, weights, down_inverse, sphere, *received),
+        (offsets, dense, edge, inner, ends, weights, down_inverse, surfaces, *received),
         [
             pltpu.VMEM(((lx + 4) * half * deep, 6 * points), BF16),
             pltpu.VMEM((lx * half, 8 + deep + 8, (SPAN + 1) * points), F32),

time: 22.7 us -> 19.2 us (0.85)
  starting transfers between devices: 10.2 us -> 6.44 us
  Pallas kernels: 11 us -> 11.3 us
    ppermute x5, starting transfers between devices: 10.2 us -> 6.44 us  [the longest x3 6.24 us: exchange(): results.append(lax.ppermute(packet, axis, swaps))]
    pallas_call x7, Pallas kernels: 11 us -> 11.3 us  [call(): pl.pallas_call(kernel, out_shape=outs, in_specs=[pl.BlockSpec(memory_spac...]
  transfers between devices with their start and end apart: 5 -> 5, of which waited for: 2 -> 2; matrix products, arithmetic and copies ran while one was open for 0% -> 0% of each run, Pallas kernels for 26% -> 31%
where the time goes in v4:
time: 19.2 us; the launch traced here: 19 us
  Pallas kernels  11.3 us (59%)
  starting transfers between devices  6.44 us (34%)
  waiting for transfers between devices  1.25 us (7%)
    pallas_call x7, Pallas kernels, call(): pl.pallas_call(kernel, out_shape=outs, in_specs=[pl.BlockSpec(memory_spac...  11.3 us
    ppermute x3, starting transfers between devices, exchange(): results.append(lax.ppermute(packet, axis, swaps))  6.24 us
    ppermute x2, waiting for transfers between devices, exchange(): results.append(lax.ppermute(packet, ('gx', axis), swaps))  1.25 us
  transfers between devices with their start and end apart: 5, of which 2 were waited for; matrix products, arithmetic and copies ran while one was open for 0% of the time, Pallas kernels for 31%

profile of v4, /device:TPU:21, one launch (start us, length us, event | category | flops | bytes accessed | tf_op | source)
XLA Modules:
  0.0 19.0 jit_solution(5771714348847804762)
XLA Ops:
  0.0 1.8 %upward.1 = (f32[3,4,4,128]{3,2,1,0:T(4,128)S(1)}, f32[4,4,128]{2,1,0:T(4,128)S(1)}, f32[64,64]{1,0:T(8,128)S(1)}, f32[16,64,128]{2,1,0:T(8,128)S(1)}, f32[32,12...) custom-call(f32[3,4,4,128]{3,2,1,0:T(4,128)} %offs_hbm.1, f32[4,4,128]{2,1,0:T(4,128)} %q_hbm.1, ...), custom_call_target="tpu_custom_call" | custom-call | tf_op jit(solution)/shard_map/upward/pallas_call | solution.py:552
  1.8 1.3 %collective-permute-start = (f32[32,128]{1,0:T(8,128)S(1)}, f32[32,128]{1,0:T(8,128)S(1)}, u32[]{:S(2)}, u32[]{:S(2)}) collective-permute-start(f32[32,128]{1,0:T(8,128)S(1)} %get-tuple-element.39), channel_id=1, source_target_pairs={{0,4},{4,0},{8,12},{12,8},{1,5},{5,1},{9,13},{13,9},{2,6},{6,2},{1... | collective-permute-start | bytes 49160 | tf_op jit(solution)/shard_map/ppermute | solution.py:542
  3.1 0.2 %collective-permute-start.1 = (f32[32,128]{1,0:T(8,128)S(1)}, f32[32,128]{1,0:T(8,128)S(1)}, u32[]{:S(2)}, u32[]{:S(2)}) collective-permute-start(f32[32,128]{1,0:T(8,128)S(1)} %get-tuple-element.40), channel_id=1, source_target_pairs={{4,8},{8,4},{20,24},{24,20},{0,16},{12,28},{16,0},{28,12},{5,9},{9... | collective-permute-start | bytes 49160 | tf_op jit(solution)/shard_map/ppermute | solution.py:546
  3.3 2.6 %near_edge.1 = (f32[2,4,128]{2,1,0:T(4,128)S(1)}, bf16[7,448,512]{2,1,0:T(8,128)(2,1)S(1)}) custom-call(bf16[316,4096]{1,0:T(8,128)(2,1)} %t_hbm.1, f32[32,128]{1,0:T(8,128)S(1)} %get-tuple-element.38.after_ref.u_ref, f32[3,4,4,128]{3,2,1,0:T(4,128)S(1)} %get-tuple-element.36.offs_ref, f32[4,4,128]{2,1,0:T(4,128)S(1)} %get-tuple-element.37.q_ref), custom_call_target="tpu_custom_call" | custom-call | tf_op jit(solution)/shard_map/near_edge/pallas_call | solution.py:552
  5.9 0.0 collective-permute-done.rest_0_
  5.9 0.7 %collective-permute-done.1.rest_1_ = f32[32,128]{1,0:T(8,128)S(1)} collective-permute-done((f32[32,128]{1,0:T(8,128)S(1)}, f32[32,128]{1,0:T(8,128)S(1)}, u32[]{:S(2)}, u32[]{:S(2)}) %collective-permute-start.1) | collective-permute-done | bytes 16416 | tf_op jit(solution)/shard_map/ppermute | solution.py:546
  6.6 0.1 zpack.1
  6.7 1.4 %collective-permute-start.2 = (f32[64,128]{1,0:T(8,128)S(1)}, f32[64,128]{1,0:T(8,128)S(1)}, u32[]{:S(2)}, u32[]{:S(2)}) collective-permute-start(f32[64,128]{1,0:T(8,128)S(1)} %get-tuple-element.50), channel_id=1, source_target_pairs={{0,1},{1,0},{2,3},{3,2},{4,5},{5,4},{6,7},{7,6},{8,9},{9,8},{10,11... | collective-permute-start | bytes 98312 | tf_op jit(solution)/shard_map/ppermute | solution.py:542
  8.1 0.0 collective-permute-start.3
  8.1 2.2 %near_inner.1.near_in_ref = f32[2,4,128]{2,1,0:T(4,128)S(1)} custom-call(f32[3,4,4,128]{3,2,1,0:T(4,128)S(1)} %get-tuple-element.36.offs_ref, f32[4,24,128]{2,1,0:T(8,128)S(1)} %get-tuple-element.59.r_ref), custom_call_target="tpu_custom_call" | custom-call | tf_op jit(solution)/shard_map/near_inner/pallas_call | solution.py:552
  10.2 0.0 collective-permute-done.2.rest_0_
  10.2 0.6 %collective-permute-done.3.rest_1_ = f32[64,128]{1,0:T(8,128)S(1)} collective-permute-done((f32[64,128]{1,0:T(8,128)S(1)}, f32[64,128]{1,0:T(8,128)S(1)}, u32[]{:S(2)}, u32[]{:S(2)}) %collective-permute-start.3) | collective-permute-done | bytes 32800 | tf_op jit(solution)/shard_map/ppermute | solution.py:546
  10.9 3.6 %collective-permute-start.4 = (f32[104,128]{1,0:T(8,128)S(1)}, f32[104,128]{1,0:T(8,128)S(1)}, u32[]{:S(2)}, u32[]{:S(2)}) collective-permute-start(f32[104,128]{1,0:T(8,128)S(1)} %get-tuple-element.58), channel_id=1, source_target_pairs={{0,16},{16,0},{1,17},{17,1},{2,18},{18,2},{3,19},{19,3},{4,20},{20... | collective-permute-start | bytes 159752 | tf_op jit(solution)/shard_map/ppermute | solution.py:542
  14.5 1.2 %near_ends.1.near_end_ref = f32[4,4,128]{2,1,0:T(4,128)S(1)} custom-call(f32[3,4,4,128]{3,2,1,0:T(4,128)S(1)} %get-tuple-element.36.offs_ref, f32[4,24,128]{2,1,0:T(8,128)S(1)} %get-tuple-element.59.r_ref, f32[4,8,128]{2,1,0:T(8,128)S(1)} %get-tuple-element.60.zl_ref, f32[4,8,128]{2,1,0:T(8,128)S(1)} %get-tuple-element.61.zh_ref), custom_call_target="tpu_custom_call" | custom-call | tf_op jit(solution)/shard_map/near_ends/pallas_call | solution.py:552
  15.6 0.0 collective-permute-done.4.rest_0_
  15.6 3.4 %final.1 = f32[4,4,128]{2,1,0:T(4,128)} custom-call(f32[3,4,4,128]{3,2,1,0:T(4,128)S(1)} %get-tuple-element.36.offs_ref, f32[16,8,128]{2,1,0:T(8,128)S(1)} %get-tuple-element.54.e_ref, f32[2,4,128]{2,1,0:T(4,128)S(1)} %get-tuple-element.55.near_edge_ref, f32[2,4,128]{2,1,0:T(4,128)S(1)} %near_inner.1.near_in_ref, f32[4,4,128]{2,1,0:T(4,128)S(1)} %near_ends.1.near_end_ref, ...), custom_call_target="tpu_custom_call" | custom-call | tf_op jit(solution)/shard_map/final/pallas_call | solution.py:552
  (1 shorter events, 0.0 us)
Async XLA Ops:
  1.8 4.1 %collective-permute-start = (f32[32,128]{1,0:T(8,128)S(1)}, f32[32,128]{1,0:T(8,128)S(1)}, u32[]{:S(2)}, u32[]{:S(2)}) collective-permute-start(f32[32,128]{1,0:T(8,128)S(1)} %get-tuple-element.39), channel_id=1, source_target_pairs={{0,4},{4,0},{8,12},{12,8},{1,5},{5,1},{9,13},{13,9},{2,6},{6,2},{1... | collective-permute-start | bytes 49160 | tf_op jit(solution)/shard_map/ppermute | solution.py:542
  3.1 3.5 %collective-permute-start.1 = (f32[32,128]{1,0:T(8,128)S(1)}, f32[32,128]{1,0:T(8,128)S(1)}, u32[]{:S(2)}, u32[]{:S(2)}) collective-permute-start(f32[32,128]{1,0:T(8,128)S(1)} %get-tuple-element.40), channel_id=1, source_target_pairs={{4,8},{8,4},{20,24},{24,20},{0,16},{12,28},{16,0},{28,12},{5,9},{9... | collective-permute-start | bytes 49160 | tf_op jit(solution)/shard_map/ppermute | solution.py:546
  6.7 3.5 %collective-permute-start.2 = (f32[64,128]{1,0:T(8,128)S(1)}, f32[64,128]{1,0:T(8,128)S(1)}, u32[]{:S(2)}, u32[]{:S(2)}) collective-permute-start(f32[64,128]{1,0:T(8,128)S(1)} %get-tuple-element.50), channel_id=1, source_target_pairs={{0,1},{1,0},{2,3},{3,2},{4,5},{5,4},{6,7},{7,6},{8,9},{9,8},{10,11... | collective-permute-start | bytes 98312 | tf_op jit(solution)/shard_map/ppermute | solution.py:542
  8.1 2.8 %collective-permute-start.3 = (f32[64,128]{1,0:T(8,128)S(1)}, f32[64,128]{1,0:T(8,128)S(1)}, u32[]{:S(2)}, u32[]{:S(2)}) collective-permute-start(f32[64,128]{1,0:T(8,128)S(1)} %get-tuple-element.51), channel_id=1, source_target_pairs={{1,2},{2,1},{17,18},{18,17},{0,16},{3,19},{16,0},{19,3},{5,6},{6,5... | collective-permute-start | bytes 98312 | tf_op jit(solution)/shard_map/ppermute | solution.py:546
  10.9 4.8 %collective-permute-start.4 = (f32[104,128]{1,0:T(8,128)S(1)}, f32[104,128]{1,0:T(8,128)S(1)}, u32[]{:S(2)}, u32[]{:S(2)}) collective-permute-start(f32[104,128]{1,0:T(8,128)S(1)} %get-tuple-element.58), channel_id=1, source_target_pairs={{0,16},{16,0},{1,17},{17,1},{2,18},{18,2},{3,19},{19,3},{4,20},{20... | collective-permute-start | bytes 159752 | tf_op jit(solution)/shard_map/ppermute | solution.py:542

commit v5 on v4

--- a/solution.py
+++ b/solution.py
@@ -401,7 +401,6 @@
     wide = ly + 2
     deep = lz + 4
     block = half * deep
-    width = (SPAN - 1) * points
     above, below = get(received, "gx")
 
     def plane(x, pair):
@@ -411,12 +410,20 @@
             return e_ref[(x - 2) * pairs + pair]
         return above[((x - lx - 2) * pairs + pair) * deep : ((x - lx - 2) * pairs + pair + 1) * deep]
 
+    side = lax.broadcasted_iota(jnp.int32, (deep, 128), 1) < points
     for x in range(lx + 4):
         planes = [plane(x, pair) for pair in range(pairs)]
-        for j in range(SPAN // 2):
-            left_ref[pl.ds(x * block, block), j * 128 : (j + 1) * 128] = jnp.concatenate(
-                planes[j : j + half], axis=0
-            ).astype(BF16)
+        turned = [pltpu.roll(value, points, 1) for value in planes]
+        at = pl.ds(x * block, block)
+        for j in range(SPAN // 2 + 1):
+            early, late = [], []
+            for p in range(half):
+                before = turned[p + j - 1] if j else 0.0
+                after = turned[p + j] if j < SPAN // 2 else 0.0
+                early.append(jnp.where(side, before, after))
+                late.append(planes[p + j] if j < SPAN // 2 else jnp.zeros((deep, 128), F32))
+            left_ref[0, at, j * 128 : (j + 1) * 128] = jnp.concatenate(early, axis=0).astype(BF16)
+            left_ref[1, at, j * 128 : (j + 1) * 128] = jnp.concatenate(late, axis=0).astype(BF16)
     spot = lax.broadcasted_iota(jnp.int32, (wide, lanes), 1) // BODIES
     lead = lax.broadcasted_iota(jnp.int32, (wide, lanes), 0).astype(F32) - 1.0
     base = 2 * pairs * deep
@@ -470,21 +477,20 @@
     ).astype(BF16)
     lane = lax.broadcasted_iota(jnp.int32, (lz, 128), 1)
     level = lax.broadcasted_iota(jnp.int32, (lz, 128), 0)
+    total = {}
+    for ox in range(-REACH, REACH + 1):
+        chosen = [b for b in range(lx) if not (ox == -REACH and b % 2 == 0) and not (ox == REACH and b % 2 == 1)]
+        wanted = [(cy, b) for cy in range(2) for b in chosen]
+        parts = [left_ref[cy, pl.ds((b + ox + 2) * block, block), : SPAN * points] for cy, b in wanted]
+        got = jnp.dot(jnp.concatenate(parts, axis=0), w_ref[ox + REACH], preferred_element_type=F32)
+        for n, key in enumerate(wanted):
+            piece = got[n * block : (n + 1) * block]
+            total[key] = total[key] + piece if key in total else piece
+        next(waiting, None)
     for cy in range(2):
-        total = [None] * lx
-        for ox in range(-REACH, REACH + 1):
-            chosen = [b for b in range(lx) if not (ox == -REACH and b % 2 == 0) and not (ox == REACH and b % 2 == 1)]
-            parts = [left_ref[pl.ds((b + ox + 2) * block, block), :] for b in chosen]
-            lhs = jnp.concatenate(parts, axis=0)
-            rhs = w_ref[ox + REACH, pl.ds((1 - cy) * points, width), :]
-            got = jnp.dot(lhs, rhs, preferred_element_type=F32)
-            for n, b in enumerate(chosen):
-                piece = got[n * block : (n + 1) * block]
-                total[b] = piece if total[b] is None else total[b] + piece
-            next(waiting, None)
         for b in range(lx):
             for p in range(half):
-                acc_ref[b * half + p, pl.ds(8, deep), :] = total[b][p * deep : (p + 1) * deep]
+                acc_ref[b * half + p, pl.ds(8, deep), :] = total[cy, b][p * deep : (p + 1) * deep]
         for g in range(lx * half):
             folded = None
             for k in range((SPAN + 1) // 2):
@@ -653,7 +659,7 @@
         [shaped(lx, ly, lanes)],
         (offsets, dense, edge, inner, ends, weights, down_inverse, surfaces, *received),
         [
-            pltpu.VMEM(((lx + 4) * half * deep, 6 * points), BF16),
+            pltpu.VMEM((2, (lx + 4) * half * deep, (SPAN + 1) * points), BF16),
             pltpu.VMEM((lx * half, 8 + deep + 8, (SPAN + 1) * points), F32),
             pltpu.VMEM((lx * half, 2, points, lanes), F32),
             pltpu.VMEM((boxes, 2 * points), F32),

time: 19.2 us -> 18.6 us (0.969)
  Pallas kernels: 11.3 us -> 10.7 us
    pallas_call x7, Pallas kernels: 11.3 us -> 10.7 us  [call(): pl.pallas_call(kernel, out_shape=outs, in_specs=[pl.BlockSpec(memory_spac...]
  transfers between devices with their start and end apart: 5 -> 5, of which waited for: 2 -> 2; matrix products, arithmetic and copies ran while one was open for 0% -> 0% of each run, Pallas kernels for 31% -> 32%
where the time goes in v5:
time: 18.6 us; the launch traced here: 18.4 us
  Pallas kernels  10.7 us (58%)
  starting transfers between devices  6.44 us (35%)
  waiting for transfers between devices  1.25 us (7%)
    pallas_call x7, Pallas kernels, call(): pl.pallas_call(kernel, out_shape=outs, in_specs=[pl.BlockSpec(memory_spac...  10.7 us
    ppermute x3, starting transfers between devices, exchange(): results.append(lax.ppermute(packet, axis, swaps))  6.24 us
    ppermute x2, waiting for transfers between devices, exchange(): results.append(lax.ppermute(packet, ('gx', axis), swaps))  1.25 us
  transfers between devices with their start and end apart: 5, of which 2 were waited for; matrix products, arithmetic and copies ran while one was open for 0% of the time, Pallas kernels for 32%

profile of v5, /device:TPU:21, one launch (start us, length us, event | category | flops | bytes accessed | tf_op | source)
XLA Modules:
  0.0 18.4 jit_solution(15996677924220206155)
XLA Ops:
  0.0 1.8 %upward.1 = (f32[3,4,4,128]{3,2,1,0:T(4,128)S(1)}, f32[4,4,128]{2,1,0:T(4,128)S(1)}, f32[64,64]{1,0:T(8,128)S(1)}, f32[16,64,128]{2,1,0:T(8,128)S(1)}, f32[32,12...) custom-call(f32[3,4,4,128]{3,2,1,0:T(4,128)} %offs_hbm.1, f32[4,4,128]{2,1,0:T(4,128)} %q_hbm.1, ...), custom_call_target="tpu_custom_call" | custom-call | tf_op jit(solution)/shard_map/upward/pallas_call | solution.py:558
  1.8 1.3 %collective-permute-start = (f32[32,128]{1,0:T(8,128)S(1)}, f32[32,128]{1,0:T(8,128)S(1)}, u32[]{:S(2)}, u32[]{:S(2)}) collective-permute-start(f32[32,128]{1,0:T(8,128)S(1)} %get-tuple-element.39), channel_id=1, source_target_pairs={{0,4},{4,0},{8,12},{12,8},{1,5},{5,1},{9,13},{13,9},{2,6},{6,2},{1... | collective-permute-start | bytes 49160 | tf_op jit(solution)/shard_map/ppermute | solution.py:548
  3.1 0.2 %collective-permute-start.1 = (f32[32,128]{1,0:T(8,128)S(1)}, f32[32,128]{1,0:T(8,128)S(1)}, u32[]{:S(2)}, u32[]{:S(2)}) collective-permute-start(f32[32,128]{1,0:T(8,128)S(1)} %get-tuple-element.40), channel_id=1, source_target_pairs={{4,8},{8,4},{20,24},{24,20},{0,16},{12,28},{16,0},{28,12},{5,9},{9... | collective-permute-start | bytes 49160 | tf_op jit(solution)/shard_map/ppermute | solution.py:552
  3.3 2.6 %near_edge.1 = (f32[2,4,128]{2,1,0:T(4,128)S(1)}, bf16[7,448,512]{2,1,0:T(8,128)(2,1)S(1)}) custom-call(bf16[316,4096]{1,0:T(8,128)(2,1)} %t_hbm.1, f32[32,128]{1,0:T(8,128)S(1)} %get-tuple-element.38.after_ref.u_ref, f32[3,4,4,128]{3,2,1,0:T(4,128)S(1)} %get-tuple-element.36.offs_ref, f32[4,4,128]{2,1,0:T(4,128)S(1)} %get-tuple-element.37.q_ref), custom_call_target="tpu_custom_call" | custom-call | tf_op jit(solution)/shard_map/near_edge/pallas_call | solution.py:558
  5.9 0.0 collective-permute-done.rest_0_
  5.9 0.7 %collective-permute-done.1.rest_1_ = f32[32,128]{1,0:T(8,128)S(1)} collective-permute-done((f32[32,128]{1,0:T(8,128)S(1)}, f32[32,128]{1,0:T(8,128)S(1)}, u32[]{:S(2)}, u32[]{:S(2)}) %collective-permute-start.1) | collective-permute-done | bytes 16416 | tf_op jit(solution)/shard_map/ppermute | solution.py:552
  6.6 0.1 zpack.1
  6.7 1.4 %collective-permute-start.2 = (f32[64,128]{1,0:T(8,128)S(1)}, f32[64,128]{1,0:T(8,128)S(1)}, u32[]{:S(2)}, u32[]{:S(2)}) collective-permute-start(f32[64,128]{1,0:T(8,128)S(1)} %get-tuple-element.50), channel_id=1, source_target_pairs={{0,1},{1,0},{2,3},{3,2},{4,5},{5,4},{6,7},{7,6},{8,9},{9,8},{10,11... | collective-permute-start | bytes 98312 | tf_op jit(solution)/shard_map/ppermute | solution.py:548
  8.1 0.0 collective-permute-start.3
  8.1 2.2 %near_inner.1.near_in_ref = f32[2,4,128]{2,1,0:T(4,128)S(1)} custom-call(f32[3,4,4,128]{3,2,1,0:T(4,128)S(1)} %get-tuple-element.36.offs_ref, f32[4,24,128]{2,1,0:T(8,128)S(1)} %get-tuple-element.59.r_ref), custom_call_target="tpu_custom_call" | custom-call | tf_op jit(solution)/shard_map/near_inner/pallas_call | solution.py:558
  10.2 0.0 collective-permute-done.2.rest_0_
  10.2 0.6 %collective-permute-done.3.rest_1_ = f32[64,128]{1,0:T(8,128)S(1)} collective-permute-done((f32[64,128]{1,0:T(8,128)S(1)}, f32[64,128]{1,0:T(8,128)S(1)}, u32[]{:S(2)}, u32[]{:S(2)}) %collective-permute-start.3) | collective-permute-done | bytes 32800 | tf_op jit(solution)/shard_map/ppermute | solution.py:552
  10.9 3.6 %collective-permute-start.4 = (f32[104,128]{1,0:T(8,128)S(1)}, f32[104,128]{1,0:T(8,128)S(1)}, u32[]{:S(2)}, u32[]{:S(2)}) collective-permute-start(f32[104,128]{1,0:T(8,128)S(1)} %get-tuple-element.58), channel_id=1, source_target_pairs={{0,16},{16,0},{1,17},{17,1},{2,18},{18,2},{3,19},{19,3},{4,20},{20... | collective-permute-start | bytes 159752 | tf_op jit(solution)/shard_map/ppermute | solution.py:548
  14.5 1.2 %near_ends.1.near_end_ref = f32[4,4,128]{2,1,0:T(4,128)S(1)} custom-call(f32[3,4,4,128]{3,2,1,0:T(4,128)S(1)} %get-tuple-element.36.offs_ref, f32[4,24,128]{2,1,0:T(8,128)S(1)} %get-tuple-element.59.r_ref, f32[4,8,128]{2,1,0:T(8,128)S(1)} %get-tuple-element.60.zl_ref, f32[4,8,128]{2,1,0:T(8,128)S(1)} %get-tuple-element.61.zh_ref), custom_call_target="tpu_custom_call" | custom-call | tf_op jit(solution)/shard_map/near_ends/pallas_call | solution.py:558
  15.6 0.0 collective-permute-done.4.rest_0_
  15.6 2.8 %final.1 = f32[4,4,128]{2,1,0:T(4,128)} custom-call(f32[3,4,4,128]{3,2,1,0:T(4,128)S(1)} %get-tuple-element.36.offs_ref, f32[16,8,128]{2,1,0:T(8,128)S(1)} %get-tuple-element.54.e_ref, f32[2,4,128]{2,1,0:T(4,128)S(1)} %get-tuple-element.55.near_edge_ref, f32[2,4,128]{2,1,0:T(4,128)S(1)} %near_inner.1.near_in_ref, f32[4,4,128]{2,1,0:T(4,128)S(1)} %near_ends.1.near_end_ref, ...), custom_call_target="tpu_custom_call" | custom-call | tf_op jit(solution)/shard_map/final/pallas_call | solution.py:558
  (1 shorter events, 0.0 us)
Async XLA Ops:
  1.8 4.1 %collective-permute-start = (f32[32,128]{1,0:T(8,128)S(1)}, f32[32,128]{1,0:T(8,128)S(1)}, u32[]{:S(2)}, u32[]{:S(2)}) collective-permute-start(f32[32,128]{1,0:T(8,128)S(1)} %get-tuple-element.39), channel_id=1, source_target_pairs={{0,4},{4,0},{8,12},{12,8},{1,5},{5,1},{9,13},{13,9},{2,6},{6,2},{1... | collective-permute-start | bytes 49160 | tf_op jit(solution)/shard_map/ppermute | solution.py:548
  3.1 3.5 %collective-permute-start.1 = (f32[32,128]{1,0:T(8,128)S(1)}, f32[32,128]{1,0:T(8,128)S(1)}, u32[]{:S(2)}, u32[]{:S(2)}) collective-permute-start(f32[32,128]{1,0:T(8,128)S(1)} %get-tuple-element.40), channel_id=1, source_target_pairs={{4,8},{8,4},{20,24},{24,20},{0,16},{12,28},{16,0},{28,12},{5,9},{9... | collective-permute-start | bytes 49160 | tf_op jit(solution)/shard_map/ppermute | solution.py:552
  6.7 3.5 %collective-permute-start.2 = (f32[64,128]{1,0:T(8,128)S(1)}, f32[64,128]{1,0:T(8,128)S(1)}, u32[]{:S(2)}, u32[]{:S(2)}) collective-permute-start(f32[64,128]{1,0:T(8,128)S(1)} %get-tuple-element.50), channel_id=1, source_target_pairs={{0,1},{1,0},{2,3},{3,2},{4,5},{5,4},{6,7},{7,6},{8,9},{9,8},{10,11... | collective-permute-start | bytes 98312 | tf_op jit(solution)/shard_map/ppermute | solution.py:548
  8.1 2.8 %collective-permute-start.3 = (f32[64,128]{1,0:T(8,128)S(1)}, f32[64,128]{1,0:T(8,128)S(1)}, u32[]{:S(2)}, u32[]{:S(2)}) collective-permute-start(f32[64,128]{1,0:T(8,128)S(1)} %get-tuple-element.51), channel_id=1, source_target_pairs={{1,2},{2,1},{17,18},{18,17},{0,16},{3,19},{16,0},{19,3},{5,6},{6,5... | collective-permute-start | bytes 98312 | tf_op jit(solution)/shard_map/ppermute | solution.py:552
  10.9 4.8 %collective-permute-start.4 = (f32[104,128]{1,0:T(8,128)S(1)}, f32[104,128]{1,0:T(8,128)S(1)}, u32[]{:S(2)}, u32[]{:S(2)}) collective-permute-start(f32[104,128]{1,0:T(8,128)S(1)} %get-tuple-element.58), channel_id=1, source_target_pairs={{0,16},{16,0},{1,17},{17,1},{2,18},{18,2},{3,19},{19,3},{4,20},{20... | collective-permute-start | bytes 159752 | tf_op jit(solution)/shard_map/ppermute | solution.py:548

commit v6 on v5

--- a/solution.py
+++ b/solution.py
@@ -75,7 +75,7 @@
 def upward_kernel(
     offs_hbm, q_hbm, sphere_hbm, uinv_hbm, dinv_hbm, offs_ref, q_ref, dinv_ref, g_ref, u_ref, *rest
 ):
-    *packets, sphere_ref, uinv_ref, check_ref, wide_ref, sems = rest
+    *packets, sphere_ref, uinv_ref, wide_ref, sems = rest
     copies = [
         pltpu.make_async_copy(source, target, sems.at[n])
         for n, (source, target) in enumerate(
@@ -95,10 +95,8 @@
     half = ly // 2
     points = uinv_ref.shape[0]
     even = lax.axis_index("gy") % 2 == 0
-    segment = (
-        lax.broadcasted_iota(jnp.int32, (8, lanes), 1) // BODIES
-        == lax.broadcasted_iota(jnp.int32, (8, lanes), 0)
-    ).astype(BF16)
+    offset = lax.broadcasted_iota(jnp.int32, (lanes, 2 * points), 1)
+    offset = offset - lax.broadcasted_iota(jnp.int32, (lanes, 2 * points), 0) // BODIES
     wide_ref[...] = jnp.zeros_like(wide_ref)
     column = lax.broadcasted_iota(jnp.int32, (2 * points, 2 * points), 1)
     within = column % points
@@ -106,6 +104,7 @@
     shuffle = (lax.broadcasted_iota(jnp.int32, (2 * points, 2 * points), 0) == wanted).astype(BF16)
     for copy in copies[:3]:
         copy.wait()
+    check = None
     sphere = sphere_ref[...]
     for c in range(4):
         for x in range(lx):
@@ -120,17 +119,24 @@
                 kernel = surface_green(sphere, offs_ref, x, y)
                 g_ref[x * ly + y] = kernel
                 parts.append(kernel * q_ref[x, pl.ds(y, 1), :])
-            high, low = split(jnp.concatenate(parts, axis=0))
-            sums = lax.dot_general(segment, high, NT, preferred_element_type=F32)
-            sums = sums + lax.dot_general(segment, low, NT, preferred_element_type=F32)
-            check_ref[pl.ds((x * half + pair) * lz, lz), :] = sums[:lz]
+            part = (offset == (x * half + pair) * lz).astype(BF16)
+            part = jnp.dot(
+                jnp.concatenate(split(jnp.concatenate(parts, axis=0)), axis=1),
+                jnp.concatenate([part, part], axis=0),
+                preferred_element_type=F32,
+            )
+            check = part if check is None else check + part
     copies[3].wait()
     wide_ref[:points, :points] = uinv_ref[...]
     wide_ref[points:, points:] = uinv_ref[...]
+    inverse = [jnp.dot(part, shuffle, preferred_element_type=F32).astype(BF16) for part in split(wide_ref[...])]
+    high, low = split(check.T[: u_ref.shape[0]])
     density = jnp.dot(
-        check_ref[...], wide_ref[...], precision=lax.Precision.HIGHEST, preferred_element_type=F32
-    ).astype(BF16)
-    u_ref[...] = jnp.dot(density, shuffle, preferred_element_type=F32)
+        jnp.concatenate([high, high, low], axis=1),
+        jnp.concatenate(inverse + inverse[:1], axis=0),
+        preferred_element_type=F32,
+    )
+    u_ref[...] = density.astype(BF16).astype(F32)
     for x in range(lx):
         low = u_ref[pl.ds(x * half * lz, lz), :]
         high = u_ref[pl.ds((x * half + half - 1) * lz, lz), :]
@@ -392,7 +398,7 @@
 
 def final_kernel(count, offs_ref, e_ref, near_edge_ref, near_in_ref, near_end_ref, w_ref, dinv_ref, g_ref, *rest):
     received, rest = rest[:count], rest[count:]
-    out_ref, left_ref, acc_ref, dense_ref, sum_ref, side_ref, edge_ref = rest
+    out_ref, left_ref, acc_ref, sum_ref, side_ref, edge_ref = rest
     _, lx, ly, lanes = offs_ref.shape
     lz = lanes // BODIES
     points = dinv_ref.shape[0]
@@ -470,14 +476,16 @@
                 yield
 
     waiting = units()
-    twice = jnp.concatenate([dinv_ref[...]] * 2, axis=0)
+    high, low = split(jnp.concatenate([dinv_ref[...].T] * 2, axis=1))
+    turned_inverse = jnp.concatenate([high, low, high], axis=1)
+    boxes = lx * half * lz
+    shape = (2 * boxes, lx * half * lanes)
     expand = (
-        lax.broadcasted_iota(jnp.int32, (lx * half * lz, lx * half * lanes), 1) // BODIES
-        == lax.broadcasted_iota(jnp.int32, (lx * half * lz, lx * half * lanes), 0)
+        lax.broadcasted_iota(jnp.int32, shape, 1) // BODIES == lax.broadcasted_iota(jnp.int32, shape, 0) % boxes
     ).astype(BF16)
     lane = lax.broadcasted_iota(jnp.int32, (lz, 128), 1)
     level = lax.broadcasted_iota(jnp.int32, (lz, 128), 0)
-    total = {}
+    totals = {}
     for ox in range(-REACH, REACH + 1):
         chosen = [b for b in range(lx) if not (ox == -REACH and b % 2 == 0) and not (ox == REACH and b % 2 == 1)]
         wanted = [(cy, b) for cy in range(2) for b in chosen]
@@ -485,12 +493,12 @@
         got = jnp.dot(jnp.concatenate(parts, axis=0), w_ref[ox + REACH], preferred_element_type=F32)
         for n, key in enumerate(wanted):
             piece = got[n * block : (n + 1) * block]
-            total[key] = total[key] + piece if key in total else piece
+            totals[key] = totals[key] + piece if key in totals else piece
         next(waiting, None)
     for cy in range(2):
         for b in range(lx):
             for p in range(half):
-                acc_ref[b * half + p, pl.ds(8, deep), :] = total[cy, b][p * deep : (p + 1) * deep]
+                acc_ref[cy, b * half + p, pl.ds(8, deep), :] = totals[cy, b][p * deep : (p + 1) * deep]
         for g in range(lx * half):
             folded = None
             for k in range((SPAN + 1) // 2):
@@ -499,7 +507,7 @@
                     if oz > REACH:
                         shown.append(jnp.zeros((lz, 128), F32))
                         continue
-                    got = acc_ref[g, pl.ds(8 + oz + 2, lz), k * 128 : (k + 1) * 128]
+                    got = acc_ref[cy, g, pl.ds(8 + oz + 2, lz), k * 128 : (k + 1) * 128]
                     if oz == -REACH:
                         got = jnp.where(level % 2 == 1, got, 0.0)
                     if oz == REACH:
@@ -507,19 +515,23 @@
                     shown.append(got)
                 both = jnp.where(lane < points, shown[0], shown[1])
                 folded = both if folded is None else folded + both
-            sum_ref[pl.ds(g * lz, lz), :] = folded
-        dense = jnp.dot(sum_ref[...], twice, precision=lax.Precision.HIGHEST, preferred_element_type=F32)
-        high, low = split(dense.T)
-        spread = jnp.dot(high, expand, preferred_element_type=F32)
-        spread = spread + jnp.dot(low, expand, preferred_element_type=F32)
-        for g in range(lx * half):
-            dense_ref[g, cy] = spread[:, g * lanes : (g + 1) * lanes]
-
+            sum_ref[pl.ds((cy * lx * half + g) * lz, lz), :] = folded
     for _ in waiting:
         pass
+    high, low = split(sum_ref[...])
+    dense = lax.dot_general(
+        turned_inverse, jnp.concatenate([high, high, low], axis=1), NT, preferred_element_type=F32
+    )
+    parts = split(dense)
+    parts = [
+        jnp.concatenate([part[:, cy * boxes : (cy + 1) * boxes] for part in parts], axis=1) for cy in range(2)
+    ]
+    dense = jnp.dot(jnp.concatenate(parts, axis=0), expand, preferred_element_type=F32)
     for x in range(lx):
         for y in range(ly):
-            far = jnp.sum(g_ref[x * ly + y] * dense_ref[x * half + y // 2, y % 2], axis=0, keepdims=True)
+            g = x * half + y // 2
+            part = dense[y % 2 * points : (y % 2 + 1) * points, g * lanes : (g + 1) * lanes]
+            far = jnp.sum(g_ref[x * ly + y] * part, axis=0, keepdims=True)
             at = pl.ds(y, 1)
             total = near_end_ref[x, at, :] + far
             if x in (0, lx - 1):
@@ -595,7 +607,6 @@
         [
             pltpu.VMEM(sphere.shape, F32),
             pltpu.VMEM(up_inverse.shape, F32),
-            pltpu.VMEM((boxes, 2 * points), F32),
             pltpu.VMEM((2 * points, 2 * points), F32),
             pltpu.SemaphoreType.DMA((5,)),
         ],
@@ -660,9 +671,8 @@
         (offsets, dense, edge, inner, ends, weights, down_inverse, surfaces, *received),
         [
             pltpu.VMEM((2, (lx + 4) * half * deep, (SPAN + 1) * points), BF16),
-            pltpu.VMEM((lx * half, 8 + deep + 8, (SPAN + 1) * points), F32),
-            pltpu.VMEM((lx * half, 2, points, lanes), F32),
-            pltpu.VMEM((boxes, 2 * points), F32),
+            pltpu.VMEM((2, lx * half, 8 + deep + 8, (SPAN + 1) * points), F32),
+            pltpu.VMEM((2 * boxes, 2 * points), F32),
             pltpu.VMEM((2, 3 + lz, wide, lanes), F32),
             pltpu.VMEM((2, 10, half, lanes), F32),
         ],

time: 18.6 us -> 18.1 us (0.973)
  Pallas kernels: 10.7 us -> 10.1 us
    pallas_call x7, Pallas kernels: 10.7 us -> 10.1 us  [call(): pl.pallas_call(kernel, out_shape=outs, in_specs=[pl.BlockSpec(memory_spac...]
  transfers between devices with their start and end apart: 5 -> 5, of which waited for: 2 -> 2; matrix products, arithmetic and copies ran while one was open for 0% -> 0% of each run, Pallas kernels for 32% -> 33%
where the time goes in v6:
time: 18.1 us; the launch traced here: 17.9 us
  Pallas kernels  10.1 us (56%)
  starting transfers between devices  6.44 us (36%)
  waiting for transfers between devices  1.25 us (7%)
    pallas_call x7, Pallas kernels, call(): pl.pallas_call(kernel, out_shape=outs, in_specs=[pl.BlockSpec(memory_spac...  10.1 us
    ppermute x3, starting transfers between devices, exchange(): results.append(lax.ppermute(packet, axis, swaps))  6.24 us
    ppermute x2, waiting for transfers between devices, exchange(): results.append(lax.ppermute(packet, ('gx', axis), swaps))  1.25 us
  transfers between devices with their start and end apart: 5, of which 2 were waited for; matrix products, arithmetic and copies ran while one was open for 0% of the time, Pallas kernels for 33%

profile of v6, /device:TPU:21, one launch (start us, length us, event | category | flops | bytes accessed | tf_op | source)
XLA Modules:
  0.0 17.9 jit_solution(9428771431480886355)
XLA Ops:
  0.0 1.7 %upward.1 = (f32[3,4,4,128]{3,2,1,0:T(4,128)S(1)}, f32[4,4,128]{2,1,0:T(4,128)S(1)}, f32[64,64]{1,0:T(8,128)S(1)}, f32[16,64,128]{2,1,0:T(8,128)S(1)}, f32[32,12...) custom-call(f32[3,4,4,128]{3,2,1,0:T(4,128)} %offs_hbm.1, f32[4,4,128]{2,1,0:T(4,128)} %q_hbm.1, ...), custom_call_target="tpu_custom_call" | custom-call | tf_op jit(solution)/shard_map/upward/pallas_call | solution.py:570
  1.7 1.3 %collective-permute-start = (f32[32,128]{1,0:T(8,128)S(1)}, f32[32,128]{1,0:T(8,128)S(1)}, u32[]{:S(2)}, u32[]{:S(2)}) collective-permute-start(f32[32,128]{1,0:T(8,128)S(1)} %get-tuple-element.39), channel_id=1, source_target_pairs={{0,4},{4,0},{8,12},{12,8},{1,5},{5,1},{9,13},{13,9},{2,6},{6,2},{1... | collective-permute-start | bytes 49160 | tf_op jit(solution)/shard_map/ppermute | solution.py:560
  2.9 0.2 %collective-permute-start.1 = (f32[32,128]{1,0:T(8,128)S(1)}, f32[32,128]{1,0:T(8,128)S(1)}, u32[]{:S(2)}, u32[]{:S(2)}) collective-permute-start(f32[32,128]{1,0:T(8,128)S(1)} %get-tuple-element.40), channel_id=1, source_target_pairs={{4,8},{8,4},{20,24},{24,20},{0,16},{12,28},{16,0},{28,12},{5,9},{9... | collective-permute-start | bytes 49160 | tf_op jit(solution)/shard_map/ppermute | solution.py:564
  3.1 2.6 %near_edge.1 = (f32[2,4,128]{2,1,0:T(4,128)S(1)}, bf16[7,448,512]{2,1,0:T(8,128)(2,1)S(1)}) custom-call(bf16[316,4096]{1,0:T(8,128)(2,1)} %t_hbm.1, f32[32,128]{1,0:T(8,128)S(1)} %get-tuple-element.38.after_ref.u_ref, f32[3,4,4,128]{3,2,1,0:T(4,128)S(1)} %get-tuple-element.36.offs_ref, f32[4,4,128]{2,1,0:T(4,128)S(1)} %get-tuple-element.37.q_ref), custom_call_target="tpu_custom_call" | custom-call | tf_op jit(solution)/shard_map/near_edge/pallas_call | solution.py:570
  5.8 0.0 collective-permute-done.rest_0_
  5.8 0.7 %collective-permute-done.1.rest_1_ = f32[32,128]{1,0:T(8,128)S(1)} collective-permute-done((f32[32,128]{1,0:T(8,128)S(1)}, f32[32,128]{1,0:T(8,128)S(1)}, u32[]{:S(2)}, u32[]{:S(2)}) %collective-permute-start.1) | collective-permute-done | bytes 16416 | tf_op jit(solution)/shard_map/ppermute | solution.py:564
  6.4 0.1 zpack.1
  6.6 1.4 %collective-permute-start.2 = (f32[64,128]{1,0:T(8,128)S(1)}, f32[64,128]{1,0:T(8,128)S(1)}, u32[]{:S(2)}, u32[]{:S(2)}) collective-permute-start(f32[64,128]{1,0:T(8,128)S(1)} %get-tuple-element.50), channel_id=1, source_target_pairs={{0,1},{1,0},{2,3},{3,2},{4,5},{5,4},{6,7},{7,6},{8,9},{9,8},{10,11... | collective-permute-start | bytes 98312 | tf_op jit(solution)/shard_map/ppermute | solution.py:560
  7.9 0.0 collective-permute-start.3
  7.9 2.2 %near_inner.1.near_in_ref = f32[2,4,128]{2,1,0:T(4,128)S(1)} custom-call(f32[3,4,4,128]{3,2,1,0:T(4,128)S(1)} %get-tuple-element.36.offs_ref, f32[4,24,128]{2,1,0:T(8,128)S(1)} %get-tuple-element.59.r_ref), custom_call_target="tpu_custom_call" | custom-call | tf_op jit(solution)/shard_map/near_inner/pallas_call | solution.py:570
  10.1 0.0 collective-permute-done.2.rest_0_
  10.1 0.6 %collective-permute-done.3.rest_1_ = f32[64,128]{1,0:T(8,128)S(1)} collective-permute-done((f32[64,128]{1,0:T(8,128)S(1)}, f32[64,128]{1,0:T(8,128)S(1)}, u32[]{:S(2)}, u32[]{:S(2)}) %collective-permute-start.3) | collective-permute-done | bytes 32800 | tf_op jit(solution)/shard_map/ppermute | solution.py:564
  10.7 3.6 %collective-permute-start.4 = (f32[104,128]{1,0:T(8,128)S(1)}, f32[104,128]{1,0:T(8,128)S(1)}, u32[]{:S(2)}, u32[]{:S(2)}) collective-permute-start(f32[104,128]{1,0:T(8,128)S(1)} %get-tuple-element.58), channel_id=1, source_target_pairs={{0,16},{16,0},{1,17},{17,1},{2,18},{18,2},{3,19},{19,3},{4,20},{20... | collective-permute-start | bytes 159752 | tf_op jit(solution)/shard_map/ppermute | solution.py:560
  14.3 1.2 %near_ends.1.near_end_ref = f32[4,4,128]{2,1,0:T(4,128)S(1)} custom-call(f32[3,4,4,128]{3,2,1,0:T(4,128)S(1)} %get-tuple-element.36.offs_ref, f32[4,24,128]{2,1,0:T(8,128)S(1)} %get-tuple-element.59.r_ref, f32[4,8,128]{2,1,0:T(8,128)S(1)} %get-tuple-element.60.zl_ref, f32[4,8,128]{2,1,0:T(8,128)S(1)} %get-tuple-element.61.zh_ref), custom_call_target="tpu_custom_call" | custom-call | tf_op jit(solution)/shard_map/near_ends/pallas_call | solution.py:570
  15.5 0.0 collective-permute-done.4.rest_0_
  15.5 2.4 %final.1 = f32[4,4,128]{2,1,0:T(4,128)} custom-call(f32[3,4,4,128]{3,2,1,0:T(4,128)S(1)} %get-tuple-element.36.offs_ref, f32[16,8,128]{2,1,0:T(8,128)S(1)} %get-tuple-element.54.e_ref, f32[2,4,128]{2,1,0:T(4,128)S(1)} %get-tuple-element.55.near_edge_ref, f32[2,4,128]{2,1,0:T(4,128)S(1)} %near_inner.1.near_in_ref, f32[4,4,128]{2,1,0:T(4,128)S(1)} %near_ends.1.near_end_ref, ...), custom_call_target="tpu_custom_call" | custom-call | tf_op jit(solution)/shard_map/final/pallas_call | solution.py:570
  (1 shorter events, 0.0 us)
Async XLA Ops:
  1.7 4.1 %collective-permute-start = (f32[32,128]{1,0:T(8,128)S(1)}, f32[32,128]{1,0:T(8,128)S(1)}, u32[]{:S(2)}, u32[]{:S(2)}) collective-permute-start(f32[32,128]{1,0:T(8,128)S(1)} %get-tuple-element.39), channel_id=1, source_target_pairs={{0,4},{4,0},{8,12},{12,8},{1,5},{5,1},{9,13},{13,9},{2,6},{6,2},{1... | collective-permute-start | bytes 49160 | tf_op jit(solution)/shard_map/ppermute | solution.py:560
  2.9 3.5 %collective-permute-start.1 = (f32[32,128]{1,0:T(8,128)S(1)}, f32[32,128]{1,0:T(8,128)S(1)}, u32[]{:S(2)}, u32[]{:S(2)}) collective-permute-start(f32[32,128]{1,0:T(8,128)S(1)} %get-tuple-element.40), channel_id=1, source_target_pairs={{4,8},{8,4},{20,24},{24,20},{0,16},{12,28},{16,0},{28,12},{5,9},{9... | collective-permute-start | bytes 49160 | tf_op jit(solution)/shard_map/ppermute | solution.py:564
  6.6 3.5 %collective-permute-start.2 = (f32[64,128]{1,0:T(8,128)S(1)}, f32[64,128]{1,0:T(8,128)S(1)}, u32[]{:S(2)}, u32[]{:S(2)}) collective-permute-start(f32[64,128]{1,0:T(8,128)S(1)} %get-tuple-element.50), channel_id=1, source_target_pairs={{0,1},{1,0},{2,3},{3,2},{4,5},{5,4},{6,7},{7,6},{8,9},{9,8},{10,11... | collective-permute-start | bytes 98312 | tf_op jit(solution)/shard_map/ppermute | solution.py:560
  7.9 2.8 %collective-permute-start.3 = (f32[64,128]{1,0:T(8,128)S(1)}, f32[64,128]{1,0:T(8,128)S(1)}, u32[]{:S(2)}, u32[]{:S(2)}) collective-permute-start(f32[64,128]{1,0:T(8,128)S(1)} %get-tuple-element.51), channel_id=1, source_target_pairs={{1,2},{2,1},{17,18},{18,17},{0,16},{3,19},{16,0},{19,3},{5,6},{6,5... | collective-permute-start | bytes 98312 | tf_op jit(solution)/shard_map/ppermute | solution.py:564
  10.7 4.8 %collective-permute-start.4 = (f32[104,128]{1,0:T(8,128)S(1)}, f32[104,128]{1,0:T(8,128)S(1)}, u32[]{:S(2)}, u32[]{:S(2)}) collective-permute-start(f32[104,128]{1,0:T(8,128)S(1)} %get-tuple-element.58), channel_id=1, source_target_pairs={{0,16},{16,0},{1,17},{17,1},{2,18},{18,2},{3,19},{19,3},{4,20},{20... | collective-permute-start | bytes 159752 | tf_op jit(solution)/shard_map/ppermute | solution.py:560

commit v7 on v6

--- a/solution.py
+++ b/solution.py
@@ -274,7 +274,7 @@
     return [jnp.where((spot >= z - 1) & (spot <= z + 1), value, 0.0) for z in range(lz)]
 
 
-def gather(out_ref, n, y, turned, lz, rows):
+def gather(out_ref, n, y, turned, lz, rows, start=0.0):
     _, ly, lanes = out_ref.shape
     ones = jnp.ones((8, lanes), BF16)
     parts = []
@@ -284,11 +284,31 @@
         for source, weight, own in rows(z):
             total = attract(total, target, source, weight, own)
         parts.append(jnp.zeros((BODIES, lanes), F32) if total is None else total)
-    out_ref[n, pl.ds(y, 1), :] = lane_sum(ones, parts)
+    out_ref[n, pl.ds(y, 1), :] = start + lane_sum(ones, parts)
 
 
 def row_source(ref, at, z, own=False):
     return [ref[c, at, :] for c in range(3)], ref[3 + z, at, :], own
+
+
+def lay_pairs(ref, at, rows):
+    lanes = ref.shape[2]
+    side = lax.broadcasted_iota(jnp.int32, (rows, lanes), 1) < lanes // 2
+    values = [ref[c] for c in range(3)] + [ref[at - 1]]
+    after = [pltpu.roll(jnp.concatenate([value[1:], value[:1]], axis=0), lanes // 2, 1) for value in values]
+    for end in range(2):
+        keep = side if end == 0 else ~side
+        for c in range(4):
+            ref[at + end * 5 + c] = jnp.where(keep, values[c], after[c])
+        ref[at + end * 5 + 4] = jnp.where(keep, values[3], 0.0)
+
+
+def pair_sources(ref, base, z, lz, at, own):
+    end = 0 if z == 0 else 1
+    for n in range(0, len(at), 2):
+        row = pl.ds(at[n], 1)
+        source = [ref[base + end * 5 + c, row, :] for c in range(3)]
+        yield source, ref[base + end * 5 + (3 if n + 1 < len(at) else 4), row, :], own in (at[n], at[n] + 1)
 
 
 def edge_kernel(t_hbm, after_ref, offs_ref, q_ref, out_ref, w_ref, win_ref, t_ref, rows_ref, sems):
@@ -335,31 +355,41 @@
         win_ref[c] = r_ref[c] + base[c].astype(F32)
     for z, value in enumerate(spans(r_ref[3], spot, lz)):
         win_ref[3 + z] = value
-
-
-def inner_kernel(offs_ref, r_ref, out_ref, win_ref):
+    win_ref[3 + lz] = r_ref[3]
+    lay_pairs(win_ref, 4 + lz, rows)
+
+
+def inner_kernel(offs_ref, r_ref, near_ref, out_ref, win_ref):
     _, lx, ly, lanes = offs_ref.shape
     lz = lanes // BODIES
     wide = ly + 2
     strips(r_ref, win_ref, wide, lz)
-    for x in range(1, lx - 1):
+    for x in range(lx):
+        outer = x in (0, lx - 1)
         turned = turn(offs_ref, x)
         for y in range(ly):
+            halo = [yy for yy in (y, y + 2) if yy in (0, ly + 1)]
 
             def rows(z):
-                for xx in range(x - 1, x + 2):
-                    for dy in range(3):
-                        yield row_source(win_ref, pl.ds(xx * wide + y + dy, 1), z, xx == x and dy == 1)
-
-            gather(out_ref, x - 1, y, turned, lz, rows)
-
-
-def ends_kernel(offs_ref, r_ref, zl_ref, zh_ref, out_ref, win_ref, end_ref):
+                for xx in range(max(x - 1, 0), min(x + 2, lx)):
+                    at = [xx * wide + yy for yy in (halo if outer else range(y, y + 3))]
+                    if z in (0, lz - 1):
+                        yield from pair_sources(win_ref, 4 + lz, z, lz, at, x * wide + y + 1)
+                    else:
+                        for row in at:
+                            yield row_source(win_ref, pl.ds(row, 1), z, row == x * wide + y + 1)
+
+            start = near_ref[0 if x == 0 else 1, pl.ds(y, 1), :] if outer else 0.0
+            if outer and not halo:
+                out_ref[x, pl.ds(y, 1), :] = start
+            else:
+                gather(out_ref, x, y, turned, lz, rows, start)
+
+
+def ends_kernel(offs_ref, zl_ref, zh_ref, near_ref, out_ref, end_ref):
     _, lx, ly, lanes = offs_ref.shape
     lz = lanes // BODIES
     half = ly // 2
-    wide = ly + 2
-    strips(r_ref, win_ref, wide, lz)
     end_windows(zl_ref, -1.0, end_ref, 0, lz, half)
     end_windows(zh_ref, float(lz), end_ref, 5, lz, half)
     for x in range(lx):
@@ -368,11 +398,6 @@
 
             def rows(z):
                 nearby = range(max(x - 1, 0), min(x + 2, lx))
-                if x in (0, lx - 1):
-                    for yy in (y, y + 2):
-                        if yy in (0, ly + 1):
-                            for xx in nearby:
-                                yield row_source(win_ref, pl.ds(xx * wide + yy, 1), z)
                 for end in range(2):
                     if z == (0 if end == 0 else lz - 1):
                         for xx in nearby:
@@ -380,7 +405,7 @@
                             source = [end_ref[end * 5 + c, at, :] for c in range(3)]
                             yield source, end_ref[end * 5 + 3 + y % 2, at, :], False
 
-            gather(out_ref, x, y, turned, lz, rows)
+            gather(out_ref, x, y, turned, lz, rows, near_ref[x, pl.ds(y, 1), :])
 
 
 def end_windows(end_ref, base, win_ref, at, lz, half):
@@ -396,7 +421,7 @@
         win_ref[at + 3 + s] = jnp.where((spot >= s) & (spot < s + 3), end_ref[3], 0.0)
 
 
-def final_kernel(count, offs_ref, e_ref, near_edge_ref, near_in_ref, near_end_ref, w_ref, dinv_ref, g_ref, *rest):
+def final_kernel(count, offs_ref, e_ref, near_ref, w_ref, dinv_ref, g_ref, *rest):
     received, rest = rest[:count], rest[count:]
     out_ref, left_ref, acc_ref, sum_ref, side_ref, edge_ref = rest
     _, lx, ly, lanes = offs_ref.shape
@@ -466,7 +491,7 @@
                     source = [edge_ref[side, end * 5 + c, at, :] for c in range(3)]
                     yield source, edge_ref[side, end * 5 + 3 + y % 2, at, :], False
 
-        gather(out_ref, x, y, turned, lz, rows)
+        gather(out_ref, x, y, turned, lz, rows, near_ref[x, pl.ds(y, 1), :])
 
     def units():
         for x in (0, lx - 1):
@@ -533,12 +558,8 @@
             part = dense[y % 2 * points : (y % 2 + 1) * points, g * lanes : (g + 1) * lanes]
             far = jnp.sum(g_ref[x * ly + y] * part, axis=0, keepdims=True)
             at = pl.ds(y, 1)
-            total = near_end_ref[x, at, :] + far
-            if x in (0, lx - 1):
-                total = total + out_ref[x, at, :] + near_edge_ref[0 if x == 0 else 1, at, :]
-            else:
-                total = total + near_in_ref[x - 1, at, :]
-            out_ref[x, at, :] = total
+            start = out_ref[x, at, :] if x in (0, lx - 1) else near_ref[x, at, :]
+            out_ref[x, at, :] = start + far
 
 
 def rounds_of(axis):
@@ -644,8 +665,8 @@
     )
     packets, body = lax.optimization_barrier((packets, body))
     received = exchange(packets, "gz")
-    windows = [pltpu.VMEM((3 + lz, lx * wide, lanes), F32)]
-    (inner,) = call(inner_kernel, [shaped(lx - 2, ly, lanes)], (offsets, body), windows, name="near_inner")
+    windows = [pltpu.VMEM((14 + lz, lx * wide, lanes), F32)]
+    (inner,) = call(inner_kernel, [shaped(lx, ly, lanes)], (offsets, body, edge), windows, name="near_inner")
     received, inner = lax.optimization_barrier((received, inner))
     packet = shaped(2 * pairs * deep + 4 * wide + 8 * half, lanes)
     end = shaped(4, half * lx, lanes)
@@ -660,15 +681,15 @@
     (ends,) = call(
         ends_kernel,
         [shaped(lx, ly, lanes)],
-        (offsets, body, low, high),
-        windows + [pltpu.VMEM((10, half * lx, lanes), F32)],
+        (offsets, low, high, inner),
+        [pltpu.VMEM((10, half * lx, lanes), F32)],
         name="near_ends",
     )
     received, ends = lax.optimization_barrier((received, ends))
     (out,) = call(
         functools.partial(final_kernel, len(received)),
         [shaped(lx, ly, lanes)],
-        (offsets, dense, edge, inner, ends, weights, down_inverse, surfaces, *received),
+        (offsets, dense, ends, weights, down_inverse, surfaces, *received),
         [
             pltpu.VMEM((2, (lx + 4) * half * deep, (SPAN + 1) * points), BF16),
             pltpu.VMEM((2, lx * half, 8 + deep + 8, (SPAN + 1) * points), F32),

time: 18.1 us -> 18 us (level)
  no operation moved by 1% of the time
where the time goes in v7:
time: 18 us; the launch traced here: 17.8 us
  Pallas kernels  10 us (56%)
  starting transfers between devices  6.44 us (36%)
  waiting for transfers between devices  1.28 us (7%)
    pallas_call x7, Pallas kernels, call(): pl.pallas_call(kernel, out_shape=outs, in_specs=[pl.BlockSpec(memory_spac...  10 us
    ppermute x3, starting transfers between devices, exchange(): results.append(lax.ppermute(packet, axis, swaps))  6.24 us
    ppermute x2, waiting for transfers between devices, exchange(): results.append(lax.ppermute(packet, ('gx', axis), swaps))  1.26 us
  transfers between devices with their start and end apart: 5, of which 2 were waited for; matrix products, arithmetic and copies ran while one was open for 0% of the time, Pallas kernels for 33%

profile of v7, /device:TPU:21, one launch (start us, length us, event | category | flops | bytes accessed | tf_op | source)
XLA Modules:
  0.0 17.8 jit_solution(1097053088660094317)
XLA Ops:
  0.0 1.7 %upward.1 = (f32[3,4,4,128]{3,2,1,0:T(4,128)S(1)}, f32[4,4,128]{2,1,0:T(4,128)S(1)}, f32[64,64]{1,0:T(8,128)S(1)}, f32[16,64,128]{2,1,0:T(8,128)S(1)}, f32[32,12...) custom-call(f32[3,4,4,128]{3,2,1,0:T(4,128)} %offs_hbm.1, f32[4,4,128]{2,1,0:T(4,128)} %q_hbm.1, ...), custom_call_target="tpu_custom_call" | custom-call | tf_op jit(solution)/shard_map/upward/pallas_call | solution.py:591
  1.7 1.3 %collective-permute-start = (f32[32,128]{1,0:T(8,128)S(1)}, f32[32,128]{1,0:T(8,128)S(1)}, u32[]{:S(2)}, u32[]{:S(2)}) collective-permute-start(f32[32,128]{1,0:T(8,128)S(1)} %get-tuple-element.38), channel_id=1, source_target_pairs={{0,4},{4,0},{8,12},{12,8},{1,5},{5,1},{9,13},{13,9},{2,6},{6,2},{1... | collective-permute-start | bytes 49160 | tf_op jit(solution)/shard_map/ppermute | solution.py:581
  2.9 0.2 %collective-permute-start.1 = (f32[32,128]{1,0:T(8,128)S(1)}, f32[32,128]{1,0:T(8,128)S(1)}, u32[]{:S(2)}, u32[]{:S(2)}) collective-permute-start(f32[32,128]{1,0:T(8,128)S(1)} %get-tuple-element.39), channel_id=1, source_target_pairs={{4,8},{8,4},{20,24},{24,20},{0,16},{12,28},{16,0},{28,12},{5,9},{9... | collective-permute-start | bytes 49160 | tf_op jit(solution)/shard_map/ppermute | solution.py:585
  3.1 2.6 %near_edge.1 = (f32[2,4,128]{2,1,0:T(4,128)S(1)}, bf16[7,448,512]{2,1,0:T(8,128)(2,1)S(1)}) custom-call(bf16[316,4096]{1,0:T(8,128)(2,1)} %t_hbm.1, f32[32,128]{1,0:T(8,128)S(1)} %get-tuple-element.37.after_ref.u_ref, f32[3,4,4,128]{3,2,1,0:T(4,128)S(1)} %get-tuple-element.35.offs_ref, f32[4,4,128]{2,1,0:T(4,128)S(1)} %get-tuple-element.36.q_ref), custom_call_target="tpu_custom_call" | custom-call | tf_op jit(solution)/shard_map/near_edge/pallas_call | solution.py:591
  5.8 0.0 collective-permute-done.rest_0_
  5.8 0.7 %collective-permute-done.1.rest_1_ = f32[32,128]{1,0:T(8,128)S(1)} collective-permute-done((f32[32,128]{1,0:T(8,128)S(1)}, f32[32,128]{1,0:T(8,128)S(1)}, u32[]{:S(2)}, u32[]{:S(2)}) %collective-permute-start.1) | collective-permute-done | bytes 16416 | tf_op jit(solution)/shard_map/ppermute | solution.py:585
  6.4 0.1 zpack.1
  6.6 1.4 %collective-permute-start.2 = (f32[64,128]{1,0:T(8,128)S(1)}, f32[64,128]{1,0:T(8,128)S(1)}, u32[]{:S(2)}, u32[]{:S(2)}) collective-permute-start(f32[64,128]{1,0:T(8,128)S(1)} %get-tuple-element.49), channel_id=1, source_target_pairs={{0,1},{1,0},{2,3},{3,2},{4,5},{5,4},{6,7},{7,6},{8,9},{9,8},{10,11... | collective-permute-start | bytes 98312 | tf_op jit(solution)/shard_map/ppermute | solution.py:581
  7.9 0.0 collective-permute-start.3
  7.9 2.1 %near_inner.1.near_ref = f32[4,4,128]{2,1,0:T(4,128)S(1)} custom-call(f32[3,4,4,128]{3,2,1,0:T(4,128)S(1)} %get-tuple-element.35.offs_ref, f32[4,24,128]{2,1,0:T(8,128)S(1)} %get-tuple-element.48.r_ref, f32[2,4,128]{2,1,0:T(4,128)S(1)} %get-tuple-element.51.near_ref), custom_call_target="tpu_custom_call" | custom-call | tf_op jit(solution)/shard_map/near_inner/pallas_call | solution.py:591
  10.1 0.0 collective-permute-done.2.rest_0_
  10.1 0.6 %collective-permute-done.3.rest_1_ = f32[64,128]{1,0:T(8,128)S(1)} collective-permute-done((f32[64,128]{1,0:T(8,128)S(1)}, f32[64,128]{1,0:T(8,128)S(1)}, u32[]{:S(2)}, u32[]{:S(2)}) %collective-permute-start.3) | collective-permute-done | bytes 32800 | tf_op jit(solution)/shard_map/ppermute | solution.py:585
  10.7 3.6 %collective-permute-start.4 = (f32[104,128]{1,0:T(8,128)S(1)}, f32[104,128]{1,0:T(8,128)S(1)}, u32[]{:S(2)}, u32[]{:S(2)}) collective-permute-start(f32[104,128]{1,0:T(8,128)S(1)} %get-tuple-element.56), channel_id=1, source_target_pairs={{0,16},{16,0},{1,17},{17,1},{2,18},{18,2},{3,19},{19,3},{4,20},{20... | collective-permute-start | bytes 159752 | tf_op jit(solution)/shard_map/ppermute | solution.py:581
  14.3 1.1 %near_ends.1.near_ref = f32[4,4,128]{2,1,0:T(4,128)S(1)} custom-call(f32[3,4,4,128]{3,2,1,0:T(4,128)S(1)} %get-tuple-element.35.offs_ref, f32[4,8,128]{2,1,0:T(8,128)S(1)} %get-tuple-element.57.zl_ref, f32[4,8,128]{2,1,0:T(8,128)S(1)} %get-tuple-element.58.zh_ref, f32[4,4,128]{2,1,0:T(4,128)S(1)} %near_inner.1.near_ref), custom_call_target="tpu_custom_call" | custom-call | tf_op jit(solution)/shard_map/near_ends/pallas_call | solution.py:591
  15.4 0.0 collective-permute-done.4.rest_0_
  15.4 2.4 %final.1 = f32[4,4,128]{2,1,0:T(4,128)} custom-call(f32[3,4,4,128]{3,2,1,0:T(4,128)S(1)} %get-tuple-element.35.offs_ref, f32[16,8,128]{2,1,0:T(8,128)S(1)} %get-tuple-element.54.e_ref, f32[4,4,128]{2,1,0:T(4,128)S(1)} %near_ends.1.near_ref, bf16[7,448,512]{2,1,0:T(8,128)(2,1)S(1)} %get-tuple-element.61.w_ref, f32[64,64]{1,0:T(8,128)S(1)} %get-tuple-element.62.dinv_ref, ...), custom_call_target="tpu_custom_call" | custom-call | tf_op jit(solution)/shard_map/final/pallas_call | solution.py:591
  (1 shorter events, 0.0 us)
Async XLA Ops:
  1.7 4.1 %collective-permute-start = (f32[32,128]{1,0:T(8,128)S(1)}, f32[32,128]{1,0:T(8,128)S(1)}, u32[]{:S(2)}, u32[]{:S(2)}) collective-permute-start(f32[32,128]{1,0:T(8,128)S(1)} %get-tuple-element.38), channel_id=1, source_target_pairs={{0,4},{4,0},{8,12},{12,8},{1,5},{5,1},{9,13},{13,9},{2,6},{6,2},{1... | collective-permute-start | bytes 49160 | tf_op jit(solution)/shard_map/ppermute | solution.py:581
  2.9 3.5 %collective-permute-start.1 = (f32[32,128]{1,0:T(8,128)S(1)}, f32[32,128]{1,0:T(8,128)S(1)}, u32[]{:S(2)}, u32[]{:S(2)}) collective-permute-start(f32[32,128]{1,0:T(8,128)S(1)} %get-tuple-element.39), channel_id=1, source_target_pairs={{4,8},{8,4},{20,24},{24,20},{0,16},{12,28},{16,0},{28,12},{5,9},{9... | collective-permute-start | bytes 49160 | tf_op jit(solution)/shard_map/ppermute | solution.py:585
  6.6 3.5 %collective-permute-start.2 = (f32[64,128]{1,0:T(8,128)S(1)}, f32[64,128]{1,0:T(8,128)S(1)}, u32[]{:S(2)}, u32[]{:S(2)}) collective-permute-start(f32[64,128]{1,0:T(8,128)S(1)} %get-tuple-element.49), channel_id=1, source_target_pairs={{0,1},{1,0},{2,3},{3,2},{4,5},{5,4},{6,7},{7,6},{8,9},{9,8},{10,11... | collective-permute-start | bytes 98312 | tf_op jit(solution)/shard_map/ppermute | solution.py:581
  7.9 2.8 %collective-permute-start.3 = (f32[64,128]{1,0:T(8,128)S(1)}, f32[64,128]{1,0:T(8,128)S(1)}, u32[]{:S(2)}, u32[]{:S(2)}) collective-permute-start(f32[64,128]{1,0:T(8,128)S(1)} %get-tuple-element.50), channel_id=1, source_target_pairs={{1,2},{2,1},{17,18},{18,17},{0,16},{3,19},{16,0},{19,3},{5,6},{6,5... | collective-permute-start | bytes 98312 | tf_op jit(solution)/shard_map/ppermute | solution.py:585
  10.7 4.7 %collective-permute-start.4 = (f32[104,128]{1,0:T(8,128)S(1)}, f32[104,128]{1,0:T(8,128)S(1)}, u32[]{:S(2)}, u32[]{:S(2)}) collective-permute-start(f32[104,128]{1,0:T(8,128)S(1)} %get-tuple-element.56), channel_id=1, source_target_pairs={{0,16},{16,0},{1,17},{17,1},{2,18},{18,2},{3,19},{19,3},{4,20},{20... | collective-permute-start | bytes 159752 | tf_op jit(solution)/shard_map/ppermute | solution.py:581

commit v8 on v7

--- a/solution.py
+++ b/solution.py
@@ -465,6 +465,8 @@
             side_ref[side, c] = value[base + c * wide : base + (c + 1) * wide] + shift[c]
         for z, part in enumerate(spans(value[base + 3 * wide : base + 4 * wide], spot, lz)):
             side_ref[side, 3 + z] = part
+        side_ref[side, 3 + lz] = value[base + 3 * wide : base + 4 * wide]
+        lay_pairs(side_ref.at[side], 4 + lz, wide)
     spot = lax.broadcasted_iota(jnp.int32, (half, lanes), 1) // BODIES
     place = lax.broadcasted_iota(jnp.int32, (half, lanes), 0)
     for side, value in enumerate((below, above)):
@@ -482,9 +484,12 @@
         side = 0 if x == 0 else 1
 
         def rows(z):
-            for dy in range(3):
-                at = pl.ds(y + dy, 1)
-                yield [side_ref[side, c, at, :] for c in range(3)], side_ref[side, 3 + z, at, :], False
+            if z in (0, lz - 1):
+                yield from pair_sources(side_ref.at[side], 4 + lz, z, lz, [y, y + 1, y + 2], None)
+            else:
+                for dy in range(3):
+                    at = pl.ds(y + dy, 1)
+                    yield [side_ref[side, c, at, :] for c in range(3)], side_ref[side, 3 + z, at, :], False
             for end in range(2):
                 if z == (0 if end == 0 else lz - 1):
                     at = pl.ds(y // 2, 1)
@@ -694,7 +699,7 @@
             pltpu.VMEM((2, (lx + 4) * half * deep, (SPAN + 1) * points), BF16),
             pltpu.VMEM((2, lx * half, 8 + deep + 8, (SPAN + 1) * points), F32),
             pltpu.VMEM((2 * boxes, 2 * points), F32),
-            pltpu.VMEM((2, 3 + lz, wide, lanes), F32),
+            pltpu.VMEM((2, 14 + lz, wide, lanes), F32),
             pltpu.VMEM((2, 10, half, lanes), F32),
         ],
         24,

time: 18 us -> 17.9 us (level)
  no operation moved by 1% of the time
where the time goes in v8:
time: 17.9 us; the launch traced here: 17.7 us
  Pallas kernels  9.91 us (55%)
  starting transfers between devices  6.44 us (36%)
  waiting for transfers between devices  1.28 us (7%)
    pallas_call x7, Pallas kernels, call(): pl.pallas_call(kernel, out_shape=outs, in_specs=[pl.BlockSpec(memory_spac...  9.91 us
    ppermute x3, starting transfers between devices, exchange(): results.append(lax.ppermute(packet, axis, swaps))  6.24 us
    ppermute x2, waiting for transfers between devices, exchange(): results.append(lax.ppermute(packet, ('gx', axis), swaps))  1.26 us
  transfers between devices with their start and end apart: 5, of which 2 were waited for; matrix products, arithmetic and copies ran while one was open for 0% of the time, Pallas kernels for 33%

profile of v8, /device:TPU:21, one launch (start us, length us, event | category | flops | bytes accessed | tf_op | source)
XLA Modules:
  0.0 17.7 jit_solution(3889066820700517553)
XLA Ops:
  0.0 1.7 %upward.1 = (f32[3,4,4,128]{3,2,1,0:T(4,128)S(1)}, f32[4,4,128]{2,1,0:T(4,128)S(1)}, f32[64,64]{1,0:T(8,128)S(1)}, f32[16,64,128]{2,1,0:T(8,128)S(1)}, f32[32,12...) custom-call(f32[3,4,4,128]{3,2,1,0:T(4,128)} %offs_hbm.1, f32[4,4,128]{2,1,0:T(4,128)} %q_hbm.1, ...), custom_call_target="tpu_custom_call" | custom-call | tf_op jit(solution)/shard_map/upward/pallas_call | solution.py:596
  1.7 1.3 %collective-permute-start = (f32[32,128]{1,0:T(8,128)S(1)}, f32[32,128]{1,0:T(8,128)S(1)}, u32[]{:S(2)}, u32[]{:S(2)}) collective-permute-start(f32[32,128]{1,0:T(8,128)S(1)} %get-tuple-element.38), channel_id=1, source_target_pairs={{0,4},{4,0},{8,12},{12,8},{1,5},{5,1},{9,13},{13,9},{2,6},{6,2},{1... | collective-permute-start | bytes 49160 | tf_op jit(solution)/shard_map/ppermute | solution.py:586
  2.9 0.2 %collective-permute-start.1 = (f32[32,128]{1,0:T(8,128)S(1)}, f32[32,128]{1,0:T(8,128)S(1)}, u32[]{:S(2)}, u32[]{:S(2)}) collective-permute-start(f32[32,128]{1,0:T(8,128)S(1)} %get-tuple-element.39), channel_id=1, source_target_pairs={{4,8},{8,4},{20,24},{24,20},{0,16},{12,28},{16,0},{28,12},{5,9},{9... | collective-permute-start | bytes 49160 | tf_op jit(solution)/shard_map/ppermute | solution.py:590
  3.1 2.6 %near_edge.1 = (f32[2,4,128]{2,1,0:T(4,128)S(1)}, bf16[7,448,512]{2,1,0:T(8,128)(2,1)S(1)}) custom-call(bf16[316,4096]{1,0:T(8,128)(2,1)} %t_hbm.1, f32[32,128]{1,0:T(8,128)S(1)} %get-tuple-element.37.after_ref.u_ref, f32[3,4,4,128]{3,2,1,0:T(4,128)S(1)} %get-tuple-element.35.offs_ref, f32[4,4,128]{2,1,0:T(4,128)S(1)} %get-tuple-element.36.q_ref), custom_call_target="tpu_custom_call" | custom-call | tf_op jit(solution)/shard_map/near_edge/pallas_call | solution.py:596
  5.8 0.0 collective-permute-done.rest_0_
  5.8 0.7 %collective-permute-done.1.rest_1_ = f32[32,128]{1,0:T(8,128)S(1)} collective-permute-done((f32[32,128]{1,0:T(8,128)S(1)}, f32[32,128]{1,0:T(8,128)S(1)}, u32[]{:S(2)}, u32[]{:S(2)}) %collective-permute-start.1) | collective-permute-done | bytes 16416 | tf_op jit(solution)/shard_map/ppermute | solution.py:590
  6.4 0.1 zpack.1
  6.6 1.4 %collective-permute-start.2 = (f32[64,128]{1,0:T(8,128)S(1)}, f32[64,128]{1,0:T(8,128)S(1)}, u32[]{:S(2)}, u32[]{:S(2)}) collective-permute-start(f32[64,128]{1,0:T(8,128)S(1)} %get-tuple-element.49), channel_id=1, source_target_pairs={{0,1},{1,0},{2,3},{3,2},{4,5},{5,4},{6,7},{7,6},{8,9},{9,8},{10,11... | collective-permute-start | bytes 98312 | tf_op jit(solution)/shard_map/ppermute | solution.py:586
  7.9 0.0 collective-permute-start.3
  7.9 2.1 %near_inner.1.near_ref = f32[4,4,128]{2,1,0:T(4,128)S(1)} custom-call(f32[3,4,4,128]{3,2,1,0:T(4,128)S(1)} %get-tuple-element.35.offs_ref, f32[4,24,128]{2,1,0:T(8,128)S(1)} %get-tuple-element.48.r_ref, f32[2,4,128]{2,1,0:T(4,128)S(1)} %get-tuple-element.51.near_ref), custom_call_target="tpu_custom_call" | custom-call | tf_op jit(solution)/shard_map/near_inner/pallas_call | solution.py:596
  10.1 0.0 collective-permute-done.2.rest_0_
  10.1 0.6 %collective-permute-done.3.rest_1_ = f32[64,128]{1,0:T(8,128)S(1)} collective-permute-done((f32[64,128]{1,0:T(8,128)S(1)}, f32[64,128]{1,0:T(8,128)S(1)}, u32[]{:S(2)}, u32[]{:S(2)}) %collective-permute-start.3) | collective-permute-done | bytes 32800 | tf_op jit(solution)/shard_map/ppermute | solution.py:590
  10.7 3.6 %collective-permute-start.4 = (f32[104,128]{1,0:T(8,128)S(1)}, f32[104,128]{1,0:T(8,128)S(1)}, u32[]{:S(2)}, u32[]{:S(2)}) collective-permute-start(f32[104,128]{1,0:T(8,128)S(1)} %get-tuple-element.56), channel_id=1, source_target_pairs={{0,16},{16,0},{1,17},{17,1},{2,18},{18,2},{3,19},{19,3},{4,20},{20... | collective-permute-start | bytes 159752 | tf_op jit(solution)/shard_map/ppermute | solution.py:586
  14.3 1.1 %near_ends.1.near_ref = f32[4,4,128]{2,1,0:T(4,128)S(1)} custom-call(f32[3,4,4,128]{3,2,1,0:T(4,128)S(1)} %get-tuple-element.35.offs_ref, f32[4,8,128]{2,1,0:T(8,128)S(1)} %get-tuple-element.57.zl_ref, f32[4,8,128]{2,1,0:T(8,128)S(1)} %get-tuple-element.58.zh_ref, f32[4,4,128]{2,1,0:T(4,128)S(1)} %near_inner.1.near_ref), custom_call_target="tpu_custom_call" | custom-call | tf_op jit(solution)/shard_map/near_ends/pallas_call | solution.py:596
  15.4 0.0 collective-permute-done.4.rest_0_
  15.4 2.3 %final.1 = f32[4,4,128]{2,1,0:T(4,128)} custom-call(f32[3,4,4,128]{3,2,1,0:T(4,128)S(1)} %get-tuple-element.35.offs_ref, f32[16,8,128]{2,1,0:T(8,128)S(1)} %get-tuple-element.54.e_ref, f32[4,4,128]{2,1,0:T(4,128)S(1)} %near_ends.1.near_ref, bf16[7,448,512]{2,1,0:T(8,128)(2,1)S(1)} %get-tuple-element.61.w_ref, f32[64,64]{1,0:T(8,128)S(1)} %get-tuple-element.62.dinv_ref, ...), custom_call_target="tpu_custom_call" | custom-call | tf_op jit(solution)/shard_map/final/pallas_call | solution.py:596
  (1 shorter events, 0.0 us)
Async XLA Ops:
  1.7 4.1 %collective-permute-start = (f32[32,128]{1,0:T(8,128)S(1)}, f32[32,128]{1,0:T(8,128)S(1)}, u32[]{:S(2)}, u32[]{:S(2)}) collective-permute-start(f32[32,128]{1,0:T(8,128)S(1)} %get-tuple-element.38), channel_id=1, source_target_pairs={{0,4},{4,0},{8,12},{12,8},{1,5},{5,1},{9,13},{13,9},{2,6},{6,2},{1... | collective-permute-start | bytes 49160 | tf_op jit(solution)/shard_map/ppermute | solution.py:586
  2.9 3.5 %collective-permute-start.1 = (f32[32,128]{1,0:T(8,128)S(1)}, f32[32,128]{1,0:T(8,128)S(1)}, u32[]{:S(2)}, u32[]{:S(2)}) collective-permute-start(f32[32,128]{1,0:T(8,128)S(1)} %get-tuple-element.39), channel_id=1, source_target_pairs={{4,8},{8,4},{20,24},{24,20},{0,16},{12,28},{16,0},{28,12},{5,9},{9... | collective-permute-start | bytes 49160 | tf_op jit(solution)/shard_map/ppermute | solution.py:590
  6.6 3.5 %collective-permute-start.2 = (f32[64,128]{1,0:T(8,128)S(1)}, f32[64,128]{1,0:T(8,128)S(1)}, u32[]{:S(2)}, u32[]{:S(2)}) collective-permute-start(f32[64,128]{1,0:T(8,128)S(1)} %get-tuple-element.49), channel_id=1, source_target_pairs={{0,1},{1,0},{2,3},{3,2},{4,5},{5,4},{6,7},{7,6},{8,9},{9,8},{10,11... | collective-permute-start | bytes 98312 | tf_op jit(solution)/shard_map/ppermute | solution.py:586
  7.9 2.8 %collective-permute-start.3 = (f32[64,128]{1,0:T(8,128)S(1)}, f32[64,128]{1,0:T(8,128)S(1)}, u32[]{:S(2)}, u32[]{:S(2)}) collective-permute-start(f32[64,128]{1,0:T(8,128)S(1)} %get-tuple-element.50), channel_id=1, source_target_pairs={{1,2},{2,1},{17,18},{18,17},{0,16},{3,19},{16,0},{19,3},{5,6},{6,5... | collective-permute-start | bytes 98312 | tf_op jit(solution)/shard_map/ppermute | solution.py:590
  10.7 4.7 %collective-permute-start.4 = (f32[104,128]{1,0:T(8,128)S(1)}, f32[104,128]{1,0:T(8,128)S(1)}, u32[]{:S(2)}, u32[]{:S(2)}) collective-permute-start(f32[104,128]{1,0:T(8,128)S(1)} %get-tuple-element.56), channel_id=1, source_target_pairs={{0,16},{16,0},{1,17},{17,1},{2,18},{18,2},{3,19},{19,3},{4,20},{20... | collective-permute-start | bytes 159752 | tf_op jit(solution)/shard_map/ppermute | solution.py:586

commit v9 on v8

--- a/solution.py
+++ b/solution.py
@@ -654,7 +654,7 @@
             pltpu.VMEM((3 + lz, lx * ly, lanes), F32),
             pltpu.VMEM(translations.shape, BF16),
             pltpu.VMEM((width // 128 * stride, 128), F32),
-            pltpu.SemaphoreType.DMA((4,)),
+            pltpu.SemaphoreType.DMA((8,)),
         ],
         24,
         "near_edge",

time: 17.9 us -> 17.9 us (level)
  waiting for transfers between devices: 1.28 us -> 0.75 us
  Pallas kernels: 9.91 us -> 10.4 us
    pallas_call x7, Pallas kernels: 9.91 us -> 10.4 us  [call(): pl.pallas_call(kernel, out_shape=outs, in_specs=[pl.BlockSpec(memory_spac...]
    ppermute x2, waiting for transfers between devices: 1.26 us -> 0.74 us  [exchange(): results.append(lax.ppermute(packet, ('gx', axis), swaps))]
  transfers between devices with their start and end apart: 5 -> 5, of which waited for: 2 -> 2; matrix products, arithmetic and copies ran while one was open for 0% -> 0% of each run, Pallas kernels for 33% -> 36%
where the time goes in v9:
time: 17.9 us; the launch traced here: 17.7 us
  Pallas kernels  10.4 us (58%)
  starting transfers between devices  6.44 us (36%)
  waiting for transfers between devices  0.75 us (4%)
    pallas_call x7, Pallas kernels, call(): pl.pallas_call(kernel, out_shape=outs, in_specs=[pl.BlockSpec(memory_spac...  10.4 us
    ppermute x3, starting transfers between devices, exchange(): results.append(lax.ppermute(packet, axis, swaps))  6.24 us
    ppermute x2, waiting for transfers between devices, exchange(): results.append(lax.ppermute(packet, ('gx', axis), swaps))  0.74 us
  transfers between devices with their start and end apart: 5, of which 2 were waited for; matrix products, arithmetic and copies ran while one was open for 0% of the time, Pallas kernels for 36%

profile of v9, /device:TPU:21, one launch (start us, length us, event | category | flops | bytes accessed | tf_op | source)
XLA Modules:
  0.0 17.7 jit_solution(580950445164114743)
XLA Ops:
  0.0 1.7 %upward.1 = (f32[3,4,4,128]{3,2,1,0:T(4,128)S(1)}, f32[4,4,128]{2,1,0:T(4,128)S(1)}, f32[64,64]{1,0:T(8,128)S(1)}, f32[16,64,128]{2,1,0:T(8,128)S(1)}, f32[32,12...) custom-call(f32[3,4,4,128]{3,2,1,0:T(4,128)} %offs_hbm.1, f32[4,4,128]{2,1,0:T(4,128)} %q_hbm.1, ...), custom_call_target="tpu_custom_call" | custom-call | tf_op jit(solution)/shard_map/upward/pallas_call | solution.py:596
  1.7 1.3 %collective-permute-start = (f32[32,128]{1,0:T(8,128)S(1)}, f32[32,128]{1,0:T(8,128)S(1)}, u32[]{:S(2)}, u32[]{:S(2)}) collective-permute-start(f32[32,128]{1,0:T(8,128)S(1)} %get-tuple-element.38), channel_id=1, source_target_pairs={{0,4},{4,0},{8,12},{12,8},{1,5},{5,1},{9,13},{13,9},{2,6},{6,2},{1... | collective-permute-start | bytes 49160 | tf_op jit(solution)/shard_map/ppermute | solution.py:586
  2.9 0.2 %collective-permute-start.1 = (f32[32,128]{1,0:T(8,128)S(1)}, f32[32,128]{1,0:T(8,128)S(1)}, u32[]{:S(2)}, u32[]{:S(2)}) collective-permute-start(f32[32,128]{1,0:T(8,128)S(1)} %get-tuple-element.39), channel_id=1, source_target_pairs={{4,8},{8,4},{20,24},{24,20},{0,16},{12,28},{16,0},{28,12},{5,9},{9... | collective-permute-start | bytes 49160 | tf_op jit(solution)/shard_map/ppermute | solution.py:590
  3.1 3.1 %near_edge.1 = (f32[2,4,128]{2,1,0:T(4,128)S(1)}, bf16[7,448,512]{2,1,0:T(8,128)(2,1)S(1)}) custom-call(bf16[316,4096]{1,0:T(8,128)(2,1)} %t_hbm.1, f32[32,128]{1,0:T(8,128)S(1)} %get-tuple-element.37.after_ref.u_ref, f32[3,4,4,128]{3,2,1,0:T(4,128)S(1)} %get-tuple-element.35.offs_ref, f32[4,4,128]{2,1,0:T(4,128)S(1)} %get-tuple-element.36.q_ref), custom_call_target="tpu_custom_call" | custom-call | tf_op jit(solution)/shard_map/near_edge/pallas_call | solution.py:596
  6.3 0.0 collective-permute-done.rest_0_
  6.3 0.1 collective-permute-done.1.rest_1_
  6.4 0.1 zpack.1
  6.6 1.4 %collective-permute-start.2 = (f32[64,128]{1,0:T(8,128)S(1)}, f32[64,128]{1,0:T(8,128)S(1)}, u32[]{:S(2)}, u32[]{:S(2)}) collective-permute-start(f32[64,128]{1,0:T(8,128)S(1)} %get-tuple-element.49), channel_id=1, source_target_pairs={{0,1},{1,0},{2,3},{3,2},{4,5},{5,4},{6,7},{7,6},{8,9},{9,8},{10,11... | collective-permute-start | bytes 98312 | tf_op jit(solution)/shard_map/ppermute | solution.py:586
  7.9 0.0 collective-permute-start.3
  7.9 2.1 %near_inner.1.near_ref = f32[4,4,128]{2,1,0:T(4,128)S(1)} custom-call(f32[3,4,4,128]{3,2,1,0:T(4,128)S(1)} %get-tuple-element.35.offs_ref, f32[4,24,128]{2,1,0:T(8,128)S(1)} %get-tuple-element.48.r_ref, f32[2,4,128]{2,1,0:T(4,128)S(1)} %get-tuple-element.51.near_ref), custom_call_target="tpu_custom_call" | custom-call | tf_op jit(solution)/shard_map/near_inner/pallas_call | solution.py:596
  10.1 0.0 collective-permute-done.2.rest_0_
  10.1 0.6 %collective-permute-done.3.rest_1_ = f32[64,128]{1,0:T(8,128)S(1)} collective-permute-done((f32[64,128]{1,0:T(8,128)S(1)}, f32[64,128]{1,0:T(8,128)S(1)}, u32[]{:S(2)}, u32[]{:S(2)}) %collective-permute-start.3) | collective-permute-done | bytes 32800 | tf_op jit(solution)/shard_map/ppermute | solution.py:590
  10.7 3.6 %collective-permute-start.4 = (f32[104,128]{1,0:T(8,128)S(1)}, f32[104,128]{1,0:T(8,128)S(1)}, u32[]{:S(2)}, u32[]{:S(2)}) collective-permute-start(f32[104,128]{1,0:T(8,128)S(1)} %get-tuple-element.56), channel_id=1, source_target_pairs={{0,16},{16,0},{1,17},{17,1},{2,18},{18,2},{3,19},{19,3},{4,20},{20... | collective-permute-start | bytes 159752 | tf_op jit(solution)/shard_map/ppermute | solution.py:586
  14.3 1.1 %near_ends.1.near_ref = f32[4,4,128]{2,1,0:T(4,128)S(1)} custom-call(f32[3,4,4,128]{3,2,1,0:T(4,128)S(1)} %get-tuple-element.35.offs_ref, f32[4,8,128]{2,1,0:T(8,128)S(1)} %get-tuple-element.57.zl_ref, f32[4,8,128]{2,1,0:T(8,128)S(1)} %get-tuple-element.58.zh_ref, f32[4,4,128]{2,1,0:T(4,128)S(1)} %near_inner.1.near_ref), custom_call_target="tpu_custom_call" | custom-call | tf_op jit(solution)/shard_map/near_ends/pallas_call | solution.py:596
  15.4 0.0 collective-permute-done.4.rest_0_
  15.4 2.3 %final.1 = f32[4,4,128]{2,1,0:T(4,128)} custom-call(f32[3,4,4,128]{3,2,1,0:T(4,128)S(1)} %get-tuple-element.35.offs_ref, f32[16,8,128]{2,1,0:T(8,128)S(1)} %get-tuple-element.54.e_ref, f32[4,4,128]{2,1,0:T(4,128)S(1)} %near_ends.1.near_ref, bf16[7,448,512]{2,1,0:T(8,128)(2,1)S(1)} %get-tuple-element.61.w_ref, f32[64,64]{1,0:T(8,128)S(1)} %get-tuple-element.62.dinv_ref, ...), custom_call_target="tpu_custom_call" | custom-call | tf_op jit(solution)/shard_map/final/pallas_call | solution.py:596
  (1 shorter events, 0.0 us)
Async XLA Ops:
  1.7 4.6 %collective-permute-start = (f32[32,128]{1,0:T(8,128)S(1)}, f32[32,128]{1,0:T(8,128)S(1)}, u32[]{:S(2)}, u32[]{:S(2)}) collective-permute-start(f32[32,128]{1,0:T(8,128)S(1)} %get-tuple-element.38), channel_id=1, source_target_pairs={{0,4},{4,0},{8,12},{12,8},{1,5},{5,1},{9,13},{13,9},{2,6},{6,2},{1... | collective-permute-start | bytes 49160 | tf_op jit(solution)/shard_map/ppermute | solution.py:586
  2.9 3.5 %collective-permute-start.1 = (f32[32,128]{1,0:T(8,128)S(1)}, f32[32,128]{1,0:T(8,128)S(1)}, u32[]{:S(2)}, u32[]{:S(2)}) collective-permute-start(f32[32,128]{1,0:T(8,128)S(1)} %get-tuple-element.39), channel_id=1, source_target_pairs={{4,8},{8,4},{20,24},{24,20},{0,16},{12,28},{16,0},{28,12},{5,9},{9... | collective-permute-start | bytes 49160 | tf_op jit(solution)/shard_map/ppermute | solution.py:590
  6.6 3.5 %collective-permute-start.2 = (f32[64,128]{1,0:T(8,128)S(1)}, f32[64,128]{1,0:T(8,128)S(1)}, u32[]{:S(2)}, u32[]{:S(2)}) collective-permute-start(f32[64,128]{1,0:T(8,128)S(1)} %get-tuple-element.49), channel_id=1, source_target_pairs={{0,1},{1,0},{2,3},{3,2},{4,5},{5,4},{6,7},{7,6},{8,9},{9,8},{10,11... | collective-permute-start | bytes 98312 | tf_op jit(solution)/shard_map/ppermute | solution.py:586
  7.9 2.8 %collective-permute-start.3 = (f32[64,128]{1,0:T(8,128)S(1)}, f32[64,128]{1,0:T(8,128)S(1)}, u32[]{:S(2)}, u32[]{:S(2)}) collective-permute-start(f32[64,128]{1,0:T(8,128)S(1)} %get-tuple-element.50), channel_id=1, source_target_pairs={{1,2},{2,1},{17,18},{18,17},{0,16},{3,19},{16,0},{19,3},{5,6},{6,5... | collective-permute-start | bytes 98312 | tf_op jit(solution)/shard_map/ppermute | solution.py:590
  10.7 4.7 %collective-permute-start.4 = (f32[104,128]{1,0:T(8,128)S(1)}, f32[104,128]{1,0:T(8,128)S(1)}, u32[]{:S(2)}, u32[]{:S(2)}) collective-permute-start(f32[104,128]{1,0:T(8,128)S(1)} %get-tuple-element.56), channel_id=1, source_target_pairs={{0,16},{16,0},{1,17},{17,1},{2,18},{18,2},{3,19},{19,3},{4,20},{20... | collective-permute-start | bytes 159752 | tf_op jit(solution)/shard_map/ppermute | solution.py:586
